TPU v7x, 32 devices: a whole 2x2x4 slice. The times are simulated.
32 devices in a mesh: rep: 2 (over x), lat: 16 (over z, y, core).
Axes of the slice: x: 2, y: 2, z: 4, core: 2. Of those that a mesh axis runs over, the one named last changes fastest.
Arguments:
- ocean_state: bfloat16 [128, 64, 2160], P(None, ('rep', 'lat')), parts along dimension 1, may hold values from -6 to 6
- cotangent: bfloat16 [128, 64, 2160], P(None, ('rep', 'lat')), parts along dimension 1, may hold values from -6 to 6
- land_mask: int32 [32, 2160], P('lat'), may hold values 0 or 1
- fold_partner: int32 [2160], replicated, may hold values from 0 to 2159, each once
- conv_first: bfloat16 [9, 128, 128], replicated, may hold values from -0.1875 to 0.1875
- conv_second: bfloat16 [9, 128, 128], replicated, may hold values from -0.1875 to 0.1875
Outputs:
- updated: bfloat16 [128, 64, 2160], P(None, ('rep', 'lat')), parts along dimension 1
- grad_state: bfloat16 [128, 64, 2160], P(None, ('rep', 'lat')), parts along dimension 1
- grad_first: float32 [2304, 128], P(('rep', 'lat')), parts along dimension 0
- grad_second: float32 [2304, 128], P(('rep', 'lat')), parts along dimension 0
There are 2 independent parts, one for each index of `rep`. A program takes and returns all parts, laid end to end along the dimension named above; an argument that names none is the same for every part. Nothing has to cross between parts.
Inputs may be any that keep to these rules, and one draw needn't show every extreme that they name: `fold_partner`: each column appears exactly once.
All inputs are finite; a program needn't handle non-finite values. No bound on the sum of `land_mask` on one device may be relied on, other than what follows from the above.
Results may differ from a plain program's by a relative error of at most 0.0032.
Values may be sent and summed in bfloat16 or wider, within the bound.
No kernel may reach another device: no remote copies, remote signals or barrier semaphores. Data moves between devices by JAX's collectives and lax.ppermute only.
A program may use at most 64 MiB of HBM per device.

v0:
```python
import functools

import jax
import jax.numpy as jnp
import numpy as np
from jax import lax
from jax.experimental import pallas as pl
from jax.experimental.pallas import tpu as pltpu
from jax.sharding import PartitionSpec as P

C = 128
F32 = jnp.float32
BF16 = jnp.bfloat16
SMEM = pl.BlockSpec(memory_space=pltpu.SMEM)
HBM = pl.BlockSpec(memory_space=pltpu.HBM)
MiB = 1 << 20
OUT, INN = 0, 1
FAR = 2
ROW = 3 * C
CONTRACT_LAST = (((1,), (1,)), ((), ()))
CONTRACT_ROWS = (((0,), (0,)), ((), ()))
FORWARD = ((OUT, OUT, 1), (OUT, INN, 2), (INN, OUT, 0), (INN, INN, 1), (INN, FAR, 2))
ADJOINT = ((OUT, OUT, 1), (INN, OUT, 2), (OUT, INN, 0), (INN, INN, 1), (INN, FAR, 0))
SCALE = np.float32(np.sqrt(2 / np.pi))
CUBE = np.float32(0.044715)
HALF = np.float32(0.5)
LINKS = {}


def chunk_of(n):
    for size in (432, 400, 384, 320, 256, 240, 144, 128, 80, 64, 48, 32, 16):
        if n % size == 0:
            return size
    return n


def put_taps(dst, at, row, adjoint):
    n = row.shape[0]
    wide = row.astype(F32)
    before = pltpu.roll(wide, 1, 0).astype(BF16)
    after = pltpu.roll(wide, n - 1, 0).astype(BF16)
    taps = (after, row, before) if adjoint else (before, row, after)
    for b, tap in enumerate(taps):
        dst[:, at + C * b : at + C * b + C] = tap


def row_tap(a, parity):
    return a + parity * (2 - 2 * a)


def build_forward(dst, w, parity):
    dst[...] = jnp.zeros_like(dst)
    for ro, ri, a in FORWARD:
        for b in range(3):
            at = ROW * ri + C * b
            dst[ro * C : ro * C + C, at : at + C] = w[3 * row_tap(a, parity) + b]


def build_adjoint(dst, w, parity):
    dst[...] = jnp.zeros_like(dst)
    for ro, ri, a in ADJOINT:
        for b in range(3):
            at = ROW * ri + C * b
            dst[at : at + C, ro * C : ro * C + C] = w[3 * row_tap(a, parity) + b]


def gelu_and_slope(x):
    square = x * x
    t = jnp.tanh(SCALE * (x + CUBE * (x * square)))
    cdf = HALF * (1.0 + t)
    slope = cdf + (HALF * x) * (1.0 - t * t) * (SCALE * (1.0 + np.float32(3) * CUBE * square))
    return x * cdf, slope


def over_chunks(n, step):
    m = chunk_of(n)

    def body(k, carry):
        step(pl.ds(pl.multiple_of(k * m, m), m))
        return carry

    lax.fori_loop(0, n // m, body, 0)


def near_forward(parity, rows, w, taps, fw, y):
    build_forward(fw, w, parity)
    for k in range(3):
        put_taps(taps, ROW * k, rows[k], False)
    y[...] = lax.dot_general(taps[...], fw[...], CONTRACT_LAST, preferred_element_type=F32)


def near_adjoint(parity, rows, w, taps, ad, d):
    build_adjoint(ad, w, parity)
    for k in range(3):
        put_taps(taps, ROW * k, rows[k], True)
    d[...] = jnp.dot(taps[...], ad[...], preferred_element_type=F32)


class Fetched:
    def __init__(self, src, dst, sem):
        self.ref, self.copy, self.done = dst, pltpu.make_async_copy(src, dst, sem), False
        self.copy.start()

    def now(self):
        if not self.done:
            self.copy.wait()
            self.done = True
        return self.ref


def start_kernel(flags, state, cotangent, mask, outs, wide, lines, cot, sems):
    parity = flags[0]
    outer, inner, mask_o, mask_i = outs
    n = outer.shape[1]
    lines = Fetched(mask, lines, sems.at[0])
    cots = [Fetched(cotangent.at[r], cot.at[k], sems.at[1 + k]) for k, r in ((0, parity), (1, 1 - parity))]
    states = [Fetched(state.at[r], p.at[0], sems.at[3 + k]) for k, r, p in ((0, parity, outer), (1, 1 - parity, inner))]
    wide[...] = jnp.zeros_like(wide)
    wide[0:2, 0:n] = lines.now()[...].astype(F32)
    for slot, pair, masks in ((0, outer, mask_o), (1, inner, mask_i)):
        cot = cots[slot].now()
        row = parity if slot == 0 else 1 - parity
        is_first = jnp.full((1, C), row, jnp.int32) == 0
        for at in range(0, n, C):
            size = min(C, n - at)
            line = jnp.where(is_first, wide[0:1, at : at + C], wide[1:2, at : at + C])
            tile = jnp.broadcast_to(line, (C, C)).T[:size]
            masks[at : at + size, :] = tile.astype(BF16)
            pair[1, at : at + size, :] = (cot[at : at + size, :].astype(F32) * tile).astype(BF16)
        states[slot].now()
        outs.send(slot)
        outs.send(2 + slot)


def first_kernel(
    flags, partner, outer, inner, halo, mask_i, w1, w2, outs, pre_o, dact_o, fold, spread,
    taps, utaps, fw, ad, y, d, src, dst, wide, wide_dst, row, sems
):
    parity = flags[0]
    n = src.shape[0]
    (inner2,) = outs
    outer, inner, w1, w2 = outer.now(), inner.now(), w1.now(), w2.now()
    halo = halo.now()
    near_forward(parity, (outer[0], inner[0], halo[0]), w1, taps, fw, y)
    pre = Fetched(y.at[:, pl.ds(0, C)], pre_o, sems.at[0])
    near_adjoint(parity, (outer[1], inner[1], halo[1]), w2, utaps, ad, d)
    dact = Fetched(d.at[:, pl.ds(0, C)], dact_o, sems.at[1])
    mask_i = mask_i.now()

    def finish(rows):
        keep = mask_i[rows, :].astype(F32)
        value, slope = gelu_and_slope(y[rows, C:])
        inner2[0, rows, :] = (keep * value).astype(BF16)
        inner2[1, rows, :] = (slope * (keep * d[rows, C:])).astype(BF16)

    over_chunks(n, finish)
    outs.send(0)

    @pl.when(flags[1] != 0)
    def _():
        src[...] = outer[0].astype(F32)
        u = outer[1].astype(F32)
        wide[:, 0:C] = pltpu.roll(u, n - 1, 0)
        wide[:, C : 2 * C] = u
        wide[:, 2 * C :] = pltpu.roll(u, 1, 0)

        def step(i, carry):
            for k in range(8):
                j = i * 8 + k
                at = partner[j]
                dst[pl.ds(j, 1), :] = src[pl.ds(at, 1), :]
                wide_dst[pl.ds(at, 1), :] = wide[pl.ds(j, 1), :]
            return carry

        lax.fori_loop(0, n // 8, step, 0)
        row[...] = dst[...].astype(BF16)
        pltpu.sync_copy(row, fold)
        for b in range(3):
            utaps[:, C * b : C * b + C] = wide_dst[:, C * b : C * b + C].astype(BF16)
        pltpu.sync_copy(utaps.at[:, pl.ds(0, ROW)], spread)

    pre.now()
    dact.now()


def top_copies(top, fold, row, spread, utaps, sems):
    copies = (pltpu.make_async_copy(fold, row, sems.at[0]), pltpu.make_async_copy(spread, utaps, sems.at[1]))

    @pl.when(top != 0)
    def _():
        for copy in copies:
            copy.start()

    return copies


def forward_taps(taps, halo, row, copy, top):
    @pl.when(top == 0)
    def _():
        put_taps(taps, 0, halo[...], False)

    @pl.when(top != 0)
    def _():
        copy.wait()
        put_taps(taps, 0, row[...], False)


def adjoint_taps(utaps, halo, copy, top):
    @pl.when(top == 0)
    def _():
        put_taps(utaps, 0, halo[...], True)

    @pl.when(top != 0)
    def _():
        copy.wait()


def far_kernel(
    flags, halo_s, w1, pre_o, mask_o, halo_g, w2, dact_o, fold, spread, outs, taps, utaps, y, d, row, sems
):
    parity, top = flags[0], flags[1]
    act, dpre = outs[0].at[0], outs[0].at[1]
    copies = top_copies(top, fold, row, spread, utaps, sems)
    halo_s, w1 = halo_s.now(), w1.now()
    forward_taps(taps, halo_s, row, copies[0], top)
    kernel = jnp.concatenate([w1[3 * row_tap(0, parity) + b] for b in range(3)], axis=1)
    y[...] = lax.dot_general(taps[...], kernel, CONTRACT_LAST, preferred_element_type=F32)
    halo_g, w2 = halo_g.now(), w2.now()
    adjoint_taps(utaps, halo_g, copies[1], top)
    a = row_tap(2 - 2 * top, parity)
    kernel = jnp.concatenate([w2[3 * a + b] for b in range(3)], axis=0)
    d[...] = jnp.dot(utaps[...], kernel, preferred_element_type=F32)
    pre_o, dact_o, mask_o = pre_o.now(), dact_o.now(), mask_o.now()

    def step(rows):
        keep = mask_o[rows, :].astype(F32)
        value, slope = gelu_and_slope(pre_o[rows, :] + y[rows, :])
        act[rows, :] = (keep * value).astype(BF16)
        dpre[rows, :] = (slope * (keep * (dact_o[rows, :] + d[rows, :]))).astype(BF16)

    over_chunks(y.shape[0], step)


def weights_kernel(
    flags, outer, inner, halo_in, halo_s, halo_g, outer2, inner2, fold, spread, spread2, outs,
    blank1, blank2, blank3, blank4, blank5, blank6, blank7, g1, g2, taps, utaps, htaps, hutaps, row, sems
):
    parity, top = flags[0], flags[1]
    keep, give = outs
    copies = top_copies(top, fold, row, spread, hutaps, sems)
    for k, pair in enumerate((outer, inner, halo_in)):
        pair = pair.now()
        put_taps(taps, ROW * k, pair[0], False)
        put_taps(utaps, ROW * k, pair[1], True)
    forward_taps(htaps, halo_s.now(), row, copies[0], top)
    adjoint_taps(hutaps, halo_g.now(), copies[1], top)
    outer2, inner2 = outer2.now(), inner2.now()
    act = jnp.concatenate([outer2[0], inner2[0]], axis=1)
    dpre = jnp.concatenate([outer2[1], inner2[1]], axis=1)
    p = lax.dot_general(dpre, taps[...], CONTRACT_ROWS, preferred_element_type=F32)
    q = lax.dot_general(outer2[1], htaps[...], CONTRACT_ROWS, preferred_element_type=F32)
    first, last = row_tap(0, parity), row_tap(2, parity)

    def block(x, r, k, b):
        return x[r * C : r * C + C, ROW * k + C * b : ROW * k + C * b + C]

    for b in range(3):
        g1[3 * first + b] = block(p, INN, OUT, b) + block(q, 0, 0, b)
        g1[3 + b] = block(p, OUT, OUT, b) + block(p, INN, INN, b)
        g1[3 * last + b] = block(p, OUT, INN, b) + block(p, INN, FAR, b)
    p = lax.dot_general(act, utaps[...], CONTRACT_ROWS, preferred_element_type=F32)
    q = lax.dot_general(outer2[0], hutaps[...], CONTRACT_ROWS, preferred_element_type=F32)
    is_top = jnp.full((C, C), top, jnp.int32) != 0
    for b in range(3):
        edge = block(q, 0, 0, b)
        g2[3 * first + b] = (block(p, OUT, INN, b) + block(p, INN, FAR, b) + jnp.where(is_top, edge, 0.0)).T
        g2[3 + b] = (block(p, OUT, OUT, b) + block(p, INN, INN, b)).T
        g2[3 * last + b] = (block(p, INN, OUT, b) + jnp.where(is_top, 0.0, edge)).T
    pairs, _, per, _ = keep.shape
    for here in range(2):

        @pl.when(parity == here)
        def _():
            for which, g in enumerate((g1, g2)):
                for owner in range(2 * pairs):
                    dst = keep if owner % 2 == here else give
                    at = owner * per
                    while at < (owner + 1) * per:
                        t = at // C
                        stop = min((owner + 1) * per, (t + 1) * C)
                        rows = slice(at - owner * per, stop - owner * per)
                        dst[owner // 2, which, rows, :] = g[t, at - t * C : stop - t * C, :]
                        at = stop


def second_forward_kernel(flags, outer2, inner2, halo, w2, outer, inner, mask_i, outs, taps, fw, y):
    upd_i, upd_o = outs
    outer2, inner2, halo, w2 = outer2.now(), inner2.now(), halo.now(), w2.now()
    near_forward(flags[0], (outer2[...], inner2[...], halo[...]), w2, taps, fw, y)
    outer, inner, mask_i = outer.now(), inner.now(), mask_i.now()

    def finish(rows):
        upd_o[rows, :] = outer[rows, :].astype(F32) + y[rows, :C]
        keep = mask_i[rows, :].astype(F32)
        upd_i[rows, :] = (keep * (inner[rows, :].astype(F32) + y[rows, C:])).astype(BF16)

    over_chunks(y.shape[0], finish)


def second_adjoint_kernel(flags, outer2, inner2, halo, w1, outer, inner, outs, taps, ad, d):
    grad_i, grad_o = outs
    outer2, inner2, halo, w1 = outer2.now(), inner2.now(), halo.now(), w1.now()
    near_adjoint(flags[0], (outer2[...], inner2[...], halo[...]), w1, taps, ad, d)
    outer, inner = outer.now(), inner.now()

    def finish(rows):
        grad_o[rows, :] = outer[rows, :].astype(F32) + d[rows, :C]
        grad_i[rows, :] = (inner[rows, :].astype(F32) + d[rows, C:]).astype(BF16)

    over_chunks(d.shape[0], finish)


def fold_act_kernel(flags, partner, outer2, fold, row, src, dst):
    @pl.when(flags[1] != 0)
    def _():
        pltpu.sync_copy(outer2.at[0], row)
        src[...] = row[...].astype(F32)

        def step(i, carry):
            for k in range(16):
                j = i * 16 + k
                dst[pl.ds(j, 1), :] = src[pl.ds(partner[j], 1), :]
            return carry

        lax.fori_loop(0, src.shape[0] // 16, step, 0)
        row[...] = dst[...].astype(BF16)
        pltpu.sync_copy(row, fold)


def fold_dpre_kernel(flags, partner, outer2, w1, spread, row, kernels, tap, term, total):
    @pl.when(flags[1] != 0)
    def _():
        pltpu.sync_copy(outer2.at[1], row)
        pltpu.sync_copy(w1, kernels)
        put_taps(tap, 0, row[...], True)
        kernel = jnp.concatenate([kernels[6 + b] for b in range(3)], axis=0)
        term[...] = jnp.dot(tap[...], kernel, preferred_element_type=F32)

        def step(i, carry):
            for k in range(16):
                j = i * 16 + k
                total[pl.ds(partner[j], 1), :] = term[pl.ds(j, 1), :]
            return carry

        lax.fori_loop(0, term.shape[0] // 16, step, 0)
        pltpu.sync_copy(total, spread)


def last_kernel(
    flags, halo, w2, w1, upd_o, mask_o, grad_o, upd_i, grad_i, fold, spread, updated, grad,
    taps, utaps, y, d, row, top_sems, out_u, out_g, sems
):
    parity, top = flags[0], flags[1]
    halo, w2 = halo.now(), w2.now()
    sent = []

    def send(src, dst):
        copy = pltpu.make_async_copy(src, dst, sems.at[len(sent)])
        copy.start()
        sent.append(copy)

    copies = top_copies(top, fold, row, spread, d, top_sems)
    forward_taps(taps, halo.at[0], row, copies[0], top)
    kernel = jnp.concatenate([w2[3 * row_tap(0, parity) + b] for b in range(3)], axis=1)
    y[...] = lax.dot_general(taps[...], kernel, CONTRACT_LAST, preferred_element_type=F32)
    w1, upd_o, mask_o = w1.now(), upd_o.now(), mask_o.now()

    def step(rows):
        out_u[rows, :] = (mask_o[rows, :].astype(F32) * (upd_o[rows, :] + y[rows, :])).astype(BF16)

    over_chunks(y.shape[0], step)
    send(out_u, updated.at[parity])
    send(upd_i.now(), updated.at[1 - parity])
    send(grad_i.now(), grad.at[1 - parity])

    @pl.when(top == 0)
    def _():
        put_taps(utaps, 0, halo[1], True)
        kernel = jnp.concatenate([w1[3 * row_tap(2, parity) + b] for b in range(3)], axis=0)
        d[...] = jnp.dot(utaps[...], kernel, preferred_element_type=F32)

    @pl.when(top != 0)
    def _():
        copies[1].wait()

    grad_o = grad_o.now()

    def step(rows):
        out_g[rows, :] = (grad_o[rows, :] + d[rows, :]).astype(BF16)

    over_chunks(y.shape[0], step)
    send(out_g, grad.at[parity])
    for copy in sent:
        copy.wait()


class Sent(tuple):
    def send(self, k):
        if k not in self.started:
            self.copies[k].start()
            self.started.append(k)


def call(kernel, scalars, operands, outs, scratch, limit, name, loose=(), loose_outs=()):
    n_in, n_out = len(operands), len(outs)
    shapes = [x[0].shape[1:] if isinstance(x, tuple) else x.shape for x in operands]
    arrays = [x[0] if isinstance(x, tuple) else x for x in operands]

    def run(*refs):
        refs = list(refs)

        def take(k):
            head = refs[:k]
            del refs[:k]
            return head

        small, given, free, results, free_out = (
            take(k) for k in (len(scalars), n_in, len(loose), n_out, len(loose_outs))
        )
        inside, made, sem_in, sem_out = take(n_in), take(n_out), *take(2)
        given = [g.at[x[1]] if isinstance(x, tuple) else g for g, x in zip(given, operands)]
        fetched = [Fetched(g, v, sem_in.at[k]) for k, (g, v) in enumerate(zip(given, inside))]
        sent = Sent(made)
        sent.started = []
        sent.copies = [pltpu.make_async_copy(v, r, sem_out.at[k]) for k, (v, r) in enumerate(zip(made, results))]
        kernel(*small, *fetched, *free, *([sent] if n_out else []), *free_out, *refs)
        for x in fetched:
            x.now()
        for k in range(n_out):
            sent.send(k)
        for copy in sent.copies:
            copy.wait()

    results = pl.pallas_call(
        run,
        in_specs=[SMEM] * len(scalars) + [HBM] * (n_in + len(loose)),
        out_specs=tuple(HBM for _ in range(n_out + len(loose_outs))),
        out_shape=tuple(outs) + tuple(loose_outs),
        scratch_shapes=[pltpu.VMEM(shape, x.dtype) for shape, x in zip(shapes, arrays)]
        + [pltpu.VMEM(x.shape, x.dtype) for x in outs]
        + [pltpu.SemaphoreType.DMA((max(1, n_in),)), pltpu.SemaphoreType.DMA((max(1, n_out),))]
        + list(scratch),
        compiler_params=pltpu.CompilerParams(vmem_limit_bytes=limit * MiB),
        cost_estimate=pl.CostEstimate(flops=1000, transcendentals=0, bytes_accessed=1000),
        name=name,
    )(*scalars, *arrays, *loose)
    return list(results)


def swap(x, n, inner):
    if inner:
        pairs = [(i, i ^ 1) for i in range(n)]
    else:
        pairs = [(i, i + 1) for i in range(1, n - 1, 2)]
        pairs = pairs + [(j, i) for i, j in pairs]
    return lax.ppermute(x, "lat", pairs)


def on_device(ocean_state, cotangent, land_mask, fold_partner, conv_first, conv_second):
    lat = lax.axis_size("lat")
    index = lax.axis_index("lat")
    n = ocean_state.shape[2]
    assert ocean_state.shape[1] == 2 and lat % 2 == 0
    bits = lat.bit_length() - 1
    parity = index & 1
    top = (index == lat - 1).astype(jnp.int32)
    order = list(range(2, bits)) + ([1] if bits > 1 else [])
    flags = jnp.stack([parity, top] + [(index >> bit) & 1 for bit in order]).astype(jnp.int32)
    row = jax.ShapeDtypeStruct((n, C), BF16)
    wide = jax.ShapeDtypeStruct((n, C), F32)
    pair = jax.ShapeDtypeStruct((2, n, C), BF16)
    taps1 = jax.ShapeDtypeStruct((n, ROW), BF16)
    per = 9 * C // lat
    part = jax.ShapeDtypeStruct((lat // 2, 2, per, C), F32)
    own = jax.ShapeDtypeStruct((per, C), F32)
    row_s, wide_s = pltpu.VMEM((n, C), BF16), pltpu.VMEM((n, C), F32)
    near_s = [pltpu.VMEM((n, 3 * ROW), BF16)] * 2 + [pltpu.VMEM((2 * C, 3 * ROW), BF16), pltpu.VMEM((3 * ROW, 2 * C), BF16)]
    near_s = near_s + [pltpu.VMEM((n, 2 * C), F32)] * 2
    dma = pltpu.SemaphoreType.DMA
    far_s = [pltpu.VMEM((n, ROW), BF16)] * 2 + [wide_s] * 2 + [row_s, dma((2,))]
    padded = pl.cdiv(n, C) * C

    outer, inner, mask_o, mask_i = call(
        start_kernel, (flags,), (), [pair, pair, row, row],
        [pltpu.VMEM((8, padded), F32), pltpu.VMEM((2, n), jnp.int32), pltpu.VMEM((2, n, C), BF16), dma((5,))],
        60, "start", loose=(ocean_state.transpose(1, 2, 0), cotangent.transpose(1, 2, 0), land_mask),
    )
    halo = swap(outer, lat, False)
    halo_in = swap(inner, lat, True)
    inner2, pre_o, dact_o, fold1, spread1 = call(
        first_kernel, (flags, fold_partner), (outer, inner, halo_in, mask_i, conv_first, conv_second), [pair],
        near_s + [wide_s, wide_s, pltpu.VMEM((n, ROW), F32), pltpu.VMEM((n, ROW), F32), row_s, dma((2,))], 60, "first",
        loose_outs=[wide, wide, row, taps1],
    )
    outer2 = call(
        far_kernel, (flags,), ((halo, 0), conv_first, pre_o, mask_o, (halo, 1), conv_second, dact_o), [pair],
        far_s, 60, "far", loose=(fold1, spread1),
    )[0]
    halo2 = swap(outer2, lat, False)
    halo_in2 = swap(inner2, lat, True)
    spread2, = call(
        fold_dpre_kernel, (flags, fold_partner), (), [],
        [row_s, pltpu.VMEM((9, C, C), BF16), pltpu.VMEM((n, ROW), BF16), wide_s, wide_s], 60, "fold_dpre",
        loose=(outer2, conv_first), loose_outs=[wide],
    )
    keep, give, own1, own2, *blank = call(
        weights_kernel, (flags,), (outer, inner, halo_in, (halo, 0), (halo, 1), outer2, inner2), [part, part],
        [pltpu.VMEM((9, C, C), F32)] * 2 + [pltpu.VMEM((n, 3 * ROW), BF16)] * 2
        + [pltpu.VMEM((n, ROW), BF16)] * 2 + [row_s, dma((2,))], 60, "wgrad", loose=(fold1, spread1, spread2),
        loose_outs=[own, own, row, wide, row, wide, row],
    )

    def body(carry):
        turn, given, _ = carry
        now = flags + 2 * turn
        arrived = swap(given, lat, True)
        g = (keep + arrived).reshape((2,) * (bits - 1) + (2, per, C))
        left = list(range(bits - 1, 0, -1))
        beside = []
        for stage, bit in enumerate(order):
            axis = left.index(bit)
            left.pop(axis)
            mine = ((index >> bit) + 2 * turn) & 1
            kept = lax.dynamic_index_in_dim(g, mine, axis, keepdims=False)
            go = lax.dynamic_index_in_dim(g, 1 - mine, axis, keepdims=False)
            if 1 <= stage <= 2:
                go, beside[stage - 1] = lax.optimization_barrier((go, beside[stage - 1]))
            pairs = [(i, i ^ (1 << bit)) for i in range(lat)]
            g = kept + lax.ppermute(go.astype(LINKS.get(stage, F32)), "lat", pairs).astype(F32)
            if stage == 0:
                beside.append(
                    call(
                        second_forward_kernel, (now,),
                        ((outer2, 0), (inner2, 0), (halo_in2, 0), conv_second, (outer, 0), (inner, 0), mask_i), [row, wide],
                        near_s[0:1] + near_s[2:3] + near_s[4:5], 28, "second",
                    )
                    + call(
                        fold_act_kernel, (now, fold_partner), (), [], [row_s, wide_s, wide_s], 16, "fold_act",
                        loose=(outer2,), loose_outs=[row],
                    )
                )
                beside.append(
                    call(
                        second_adjoint_kernel, (now,),
                        ((outer2, 1), (inner2, 1), (halo_in2, 1), conv_first, (outer, 1), (inner, 1)), [row, wide],
                        near_s[0:1] + near_s[3:4] + near_s[4:5], 28, "second_adjoint",
                    )
                )
        return turn + 1, arrived, ([g[0], g[1]], beside)

    stop = jnp.minimum(1, parity + 1)
    start = ([own1, own2], [[blank[0], blank[1], blank[4]], [blank[2], blank[3]]])
    _, _, ((g1, g2), (near, near_a)) = lax.while_loop(lambda c: c[0] < stop, body, (jnp.int32(0), give, start))
    fold2 = near[2], spread2
    (upd_i, upd_o), (grad_i, grad_o) = near[:2], near_a[:2]
    updated, grad = call(
        last_kernel, (flags,), (halo2, conv_second, conv_first, upd_o, mask_o, grad_o, upd_i, grad_i), [],
        far_s + [row_s, row_s, dma((4,))], 28, "last", loose=tuple(fold2), loose_outs=[pair, pair],
    )
    return (updated.transpose(2, 0, 1), grad.transpose(2, 0, 1), g1, g2)


def solution(mesh):
    placed = (
        P(None, ("rep", "lat"), None),
        P(None, ("rep", "lat"), None),
        P("lat", None),
        P(),
        P(),
        P(),
    )
    return jax.shard_map(
        on_device,
        mesh=mesh,
        in_specs=placed,
        out_specs=(
            P(None, ("rep", "lat"), None),
            P(None, ("rep", "lat"), None),
            P(("rep", "lat"), None),
            P(("rep", "lat"), None),
        ),
        check_vma=False,
    )
```

profile of v0, /device:TPU:0, one launch (start us, length us, event | category | flops | bytes accessed | tf_op | source)
XLA Modules:
  0.0 92.1 jit_solution(17466425992527409305)
XLA Ops:
  0.6 0.1 stack.27.refs_0_
  0.7 0.0 copy-start.10
  0.7 0.0 copy-start.12
  0.7 0.0 copy-start.14
  0.7 3.0 %start.1 = (bf16[2,2160,128]{2,1,0:T(8,128)(2,1)S(1)}, bf16[2,2160,128]{2,1,0:T(8,128)(2,1)S(1)}, bf16[2160,128]{1,0:T(8,128)(2,1)}, bf16[2160,128]{1,0:T(8,128)(2,1)S(1)}) custom-call(s32[5]{0:T(128)S(1)} %stack.27.refs_0_, bf16[2,2160,128]{2,1,0:T(8,128)(2,1)} %bitcast.44, bf16[2,2160,128]{2,1,0:T(8,128)(2,1)} %bitcast.45, s32[2,2160]{1,0:T(2,128)} %refs_3_.3), custom_call_target="tpu_custom_call" | custom-call | flops 1000 | bytes 1000 | tf_op jit(solution)/shard_map/start/pallas_call | solution.py:444
  3.8 0.0 copy-start.5
  3.8 0.0 copy-start.11
  3.8 0.0 copy-start.2
  3.8 0.5 collective-permute-start.5
  4.3 1.7 %collective-permute-start.4 = (bf16[2,2160,128]{2,1,0:T(8,128)(2,1)S(1)}, bf16[2,2160,128]{2,1,0:T(8,128)(2,1)}, u32[]{:S(2)}, u32[]{:S(2)}) collective-permute-start(bf16[2,2160,128]{2,1,0:T(8,128)(2,1)S(1)} %get-tuple-element.607.refs_2_.refs_1_), channel_id=1, source_target_pairs={{1,2},{3,4},{5,6},{7,8},{9,10},{11,12},{13,14},{2,1},{4,3},{6,5},{... | collective-permute-start | bytes 3317768 | tf_op jit(solution)/shard_map/ppermute | solution.py:466
  6.1 0.6 collective-permute-done.5.refs_4_.refs_3_
  6.7 0.0 copy-start.13
  6.7 1.0 %copy-done.13 = bf16[2,2160,128]{2,1,0:T(8,128)(2,1)} copy-done((bf16[2,2160,128]{2,1,0:T(8,128)(2,1)}, bf16[2,2160,128]{2,1,0:T(8,128)(2,1)S(1)}, u32[]{:S(2)}) %copy-start.13) | copy-done | bytes 1105944
  7.7 0.0 copy-done.10
  7.7 0.0 copy-done.12
  7.7 0.0 copy-done.14
  7.7 8.0 %first.1 = (bf16[2,2160,128]{2,1,0:T(8,128)(2,1)}, f32[2160,128]{1,0:T(8,128)}, f32[2160,128]{1,0:T(8,128)}, bf16[2160,128]{1,0:T(8,128)(2,1)}, bf16[2160,384]{1,0:T(8,128)(2,1)}) custom-call(s32[5]{0:T(128)S(1)} %stack.27.refs_0_, s32[2160]{0:T(1024)S(1)} %copy-done.14, bf16[2,2160,128]{2,1,0:T(8,128)(2,1)S(1)} %get-tuple-element.607.refs_2_.refs_1_, ...), custom_call_target="tpu_custom_call" | custom-call | flops 1000 | bytes 1000 | tf_op jit(solution)/shard_map/first/pallas_call | solution.py:444
  15.7 0.0 copy-done.5
  15.7 0.0 copy-done.11
  15.7 2.3 %collective-permute-start.7 = (bf16[2,2160,128]{2,1,0:T(8,128)(2,1)}, bf16[2,2160,128]{2,1,0:T(8,128)(2,1)}, u32[]{:S(2)}, u32[]{:S(2)}) collective-permute-start(bf16[2,2160,128]{2,1,0:T(8,128)(2,1)} %get-tuple-element.604.refs_7_), channel_id=1, source_target_pairs={{0,1},{1,0},{2,3},{3,2},{4,5},{5,4},{6,7},{7,6},{8,9},{9,8},{10,11... | collective-permute-start | bytes 3317768 | tf_op jit(solution)/shard_map/ppermute | solution.py:466
  18.0 0.0 collective-permute-done.4.refs_1_.refs_5_.refs_4_
  18.0 7.0 %far.1.refs_2_.refs_6_ = bf16[2,2160,128]{2,1,0:T(8,128)(2,1)} custom-call(s32[5]{0:T(128)S(1)} %stack.27.refs_0_, bf16[2,2160,128]{2,1,0:T(8,128)(2,1)} %collective-permute-done.4.refs_1_.refs_5_.refs_4_, bf16[9,128,128]{2,1,0:T(8,128)(2,1)S(1)} %copy-done.10, f32[2160,128]{1,0:T(8,128)} %get-tuple-element.357.refs_3_, ...), custom_call_target="tpu_custom_call" | custom-call | flops 1000 | bytes 1000 | tf_op jit(solution)/shard_map/far/pallas_call | solution.py:444
  25.0 0.0 copy-start.6
  25.0 0.7 fold_dpre.1.refs_10_
  25.7 0.9 collective-permute-start.6
  26.6 0.0 copy-done.2
  26.6 0.0 copy-done.6
  26.6 9.0 %wgrad.1 = (f32[8,2,72,128]{3,2,1,0:T(8,128)}, f32[8,2,72,128]{3,2,1,0:T(8,128)}, f32[72,128]{1,0:T(8,128)}, f32[72,128]{1,0:T(8,128)}, bf16[2160,128]{1,0:T(8,1...) custom-call(s32[5]{0:T(128)S(1)} %stack.27.refs_0_, ...), custom_call_target="tpu_custom_call" | custom-call | flops 1000 | bytes 1000 | tf_op jit(solution)/shard_map/wgrad/pallas_call | solution.py:444
  35.6 0.0 collective-permute-done.7
  35.6 0.0 copy-start
  35.6 0.0 copy-start.1
  35.6 51.5 %while.27 = (s32[]{:T(128)}, f32[8,2,72,128]{3,2,1,0:T(8,128)}, f32[72,128]{1,0:T(8,128)}, f32[72,128]{1,0:T(8,128)}, bf16[2160,128]{1,0:T(8,128)(2,1)}, /*index...) while((s32[]{:T(128)}, f32[8,2,72,128]{3,2,1,0:T(8,128)}, ...), condition=%wide.region_1.2_spmd, body=%wide.region_0.1_spmd.sunk | while | flops 279515 | bytes 26914656 | solution.py:563
  35.6 18.9 %collective-permute-start = (f32[8,2,72,128]{3,2,1,0:T(8,128)}, f32[8,2,72,128]{3,2,1,0:T(8,128)S(1)}, u32[]{:S(2)}, u32[]{:S(2)}) collective-permute-start(f32[8,2,72,128]{3,2,1,0:T(8,128)} %get-tuple-element.618), channel_id=1, source_target_pairs={{0,1},{1,0},{2,3},{3,2},{4,5},{5,4},{6,7},{7,6},{8,9},{9,8},{10,11... | collective-permute-start | bytes 1769480 | tf_op jit(solution)/shard_map/while/body/ppermute | solution.py:466
  54.6 1.8 %collective-permute-done = f32[8,2,72,128]{3,2,1,0:T(8,128)S(1)} collective-permute-done((f32[8,2,72,128]{3,2,1,0:T(8,128)}, f32[8,2,72,128]{3,2,1,0:T(8,128)S(1)}, u32[]{:S(2)}, u32[]{:S(2)}) %collective-permute-start) | collective-permute-done | bytes 589856 | tf_op jit(solution)/shard_map/while/body/ppermute | solution.py:466
  56.4 1.2 %add.139 = f32[8,2,72,128]{3,2,1,0:T(8,128)S(1)} add(f32[8,2,72,128]{3,2,1,0:T(8,128)} %get-tuple-element.655, f32[8,2,72,128]{3,2,1,0:T(8,128)S(1)} %collective-permute-done) | non-fusion elementwise | flops 147456 | bytes 1769472 | tf_op jit(solution)/shard_map/while/body/add | solution.py:527
  57.6 0.0 copy-start.3
  57.6 0.0 copy-start.7
  57.6 0.7 dynamic-slice_bitcast_fusion.6
  58.4 1.6 %collective-permute-start.1 = (f32[2,2,2,72,128]{4,3,2,1,0:T(8,128)}, f32[2,2,2,72,128]{4,3,2,1,0:T(8,128)}, u32[]{:S(2)}, u32[]{:S(2)}) collective-permute-start(f32[2,2,2,72,128]{4,3,2,1,0:T(8,128)} %dynamic-slice_bitcast_fusion.6), channel_id=1, source_target_pairs={{0,4},{1,5},{2,6},{3,7},{4,0},{5,1},{6,2},{7,3},{8,12},{9,13},{10,... | collective-permute-start | bytes 884744 | tf_op jit(solution)/shard_map/while/body/ppermute | solution.py:539
  59.9 0.0 copy-done.8
  60.0 0.7 fold_act.5
  60.7 0.0 copy-done.3
  60.7 0.0 copy-done.7
  60.7 5.5 %second.5 = (bf16[2160,128]{1,0:T(8,128)(2,1)}, f32[2160,128]{1,0:T(8,128)}) custom-call(s32[5]{0:T(128)S(1)} %broadcast_add_fusion.2.refs_0_, bf16[2,2160,128]{2,1,0:T(8,128)(2,1)} %get-tuple-element.659.refs_1_.refs_2_, bf16[2,2160,128]{2,1,0:T(8,128)(2,1)} %get-tuple-element.660.refs_2_, bf16[2,2160,128]{2,1,0:T(8,128)(2,1)} %get-tuple-element.661.refs_3_, ...), custom_call_target="tpu_custom_call" | custom-call | flops 1000 | bytes 1000 | tf_op jit(solution)/shard_map/while/body/second/pallas_call | solution.py:444
  66.2 0.0 copy-start.4
  66.2 1.7 %collective-permute-done.1 = f32[2,2,2,72,128]{4,3,2,1,0:T(8,128)} collective-permute-done((f32[2,2,2,72,128]{4,3,2,1,0:T(8,128)}, f32[2,2,2,72,128]{4,3,2,1,0:T(8,128)}, u32[]{:S(2)}, u32[]{:S(2)}) %collective-permute-start.1) | collective-permute-done | bytes 294944 | tf_op jit(solution)/shard_map/while/body/ppermute | solution.py:539
  68.0 1.1 %bitcast_add_fusion.6 = f32[2,2,2,72,128]{4,3,2,1,0:T(8,128)S(1)} fusion(f32[2,2,2,72,128]{4,3,2,1,0:T(8,128)} %collective-permute-done.1, f32[2,2,2,2,72,128]{5,4,3,2,1,0:T(8,128)} %bitcast.43, s32[]{:T(128)S(6)} %select_n.52), kind=kLoop, calls=%fused_computation.clone.1 | loop fusion | flops 73728 | bytes 884740 | tf_op jit(solution)/shard_map/while/body/add | solution.py:539
  69.0 0.0 copy-start.9
  69.1 0.7 copy-done.9
  69.8 2.7 %collective-permute-start.2 = (f32[2,2,72,128]{3,2,1,0:T(8,128)S(1)}, f32[2,2,72,128]{3,2,1,0:T(8,128)}, u32[]{:S(2)}, u32[]{:S(2)}) collective-permute-start(f32[2,2,72,128]{3,2,1,0:T(8,128)S(1)} %dynamic-slice_bitcast_fusion.7), channel_id=1, source_target_pairs={{0,8},{1,9},{2,10},{3,11},{4,12},{5,13},{6,14},{7,15},{8,0},{9,1},... | collective-permute-start | bytes 442376 | tf_op jit(solution)/shard_map/while/body/ppermute | solution.py:539
  72.4 0.0 copy-done.4
  72.4 5.4 %second_adjoint.5 = (bf16[2160,128]{1,0:T(8,128)(2,1)}, f32[2160,128]{1,0:T(8,128)}) custom-call(s32[5]{0:T(128)S(1)} %broadcast_add_fusion.2.refs_0_, bf16[2,2160,128]{2,1,0:T(8,128)(2,1)} %get-tuple-element.659.refs_1_.refs_2_, bf16[2,2160,128]{2,1,0:T(8,128)(2,1)} %get-tuple-element.660.refs_2_, bf16[2,2160,128]{2,1,0:T(8,128)(2,1)} %get-tuple-element.661.refs_3_, ...), custom_call_target="tpu_custom_call" | custom-call | flops 1000 | bytes 1000 | tf_op jit(solution)/shard_map/while/body/second_adjoint/pallas_call | solution.py:444
  77.8 1.5 %collective-permute-done.2 = f32[2,2,72,128]{3,2,1,0:T(8,128)} collective-permute-done((f32[2,2,72,128]{3,2,1,0:T(8,128)S(1)}, f32[2,2,72,128]{3,2,1,0:T(8,128)}, u32[]{:S(2)}, u32[]{:S(2)}) %collective-permute-start.2) | collective-permute-done | bytes 147488 | tf_op jit(solution)/shard_map/while/body/ppermute | solution.py:539
  79.3 1.0 %bitcast_add_fusion.7 = f32[2,2,72,128]{3,2,1,0:T(8,128)S(1)} fusion(f32[2,2,72,128]{3,2,1,0:T(8,128)} %collective-permute-done.2, f32[2,2,2,72,128]{4,3,2,1,0:T(8,128)} %copy-done.9, s32[]{:T(128)S(6)} %select_n.54), kind=kLoop, calls=%fused_computation.2.clone.1 | loop fusion | flops 36864 | bytes 442372 | tf_op jit(solution)/shard_map/while/body/add | solution.py:539
  80.3 0.6 dynamic-slice_bitcast_fusion.8
  81.0 0.5 collective-permute-start.3
  81.4 0.8 copy.29
  82.3 3.4 %collective-permute-done.3 = f32[2,72,128]{2,1,0:T(8,128)} collective-permute-done((f32[2,72,128]{2,1,0:T(8,128)}, f32[2,72,128]{2,1,0:T(8,128)}, u32[]{:S(2)}, u32[]{:S(2)}) %collective-permute-start.3) | collective-permute-done | bytes 73760 | tf_op jit(solution)/shard_map/while/body/ppermute | solution.py:539
  85.6 0.9 bitcast_add_fusion.8
  86.5 0.6 slice_bitcast_fusion.3
  87.2 0.0 collective-permute-done.6.refs_1_
  87.2 0.0 copy-done
  87.2 0.0 copy-done.1
  87.2 4.7 %last.1 = (bf16[2,2160,128]{2,1,0:T(8,128)(2,1)}, bf16[2,2160,128]{2,1,0:T(8,128)(2,1)}) custom-call(s32[5]{0:T(128)S(1)} %get-tuple-element.681, bf16[2,2160,128]{2,1,0:T(8,128)(2,1)S(1)} %collective-permute-done.6.refs_1_, bf16[9,128,128]{2,1,0:T(8,128)(2,1)} %get-tuple-element.678, bf16[9,128,128]{2,1,0:T(8,128)(2,1)} %get-tuple-element.677, ...), custom_call_target="tpu_custom_call" | custom-call | flops 1000 | bytes 1000 | tf_op jit(solution)/shard_map/last/pallas_call | solution.py:444
  (3 shorter events, 0.0 us)
Async XLA Ops:
  0.7 6.9 %copy-start.10 = (bf16[9,128,128]{2,1,0:T(8,128)(2,1)S(1)}, bf16[9,128,128]{2,1,0:T(8,128)(2,1)}, u32[]{:S(2)}) copy-start(bf16[9,128,128]{2,1,0:T(8,128)(2,1)} %refs_3_.5) | copy-start | bytes 884740
  0.7 6.9 %copy-start.12 = (bf16[9,128,128]{2,1,0:T(8,128)(2,1)S(1)}, bf16[9,128,128]{2,1,0:T(8,128)(2,1)}, u32[]{:S(2)}) copy-start(bf16[9,128,128]{2,1,0:T(8,128)(2,1)} %refs_2_.3) | copy-start | bytes 884740
  0.7 6.9 %copy-start.14 = (s32[2160]{0:T(1024)S(1)}, s32[2160]{0:T(1024)}, u32[]{:S(2)}) copy-start(s32[2160]{0:T(1024)} %refs_1_.3) | copy-start | bytes 25924
  3.8 11.9 %copy-start.5 = (bf16[2,2160,128]{2,1,0:T(8,128)(2,1)}, bf16[2,2160,128]{2,1,0:T(8,128)(2,1)S(1)}, u32[]{:S(2)}) copy-start(bf16[2,2160,128]{2,1,0:T(8,128)(2,1)S(1)} %get-tuple-element.608.refs_3_.refs_2_) | copy-start | bytes 3317764
  3.8 11.9 %copy-start.11 = (bf16[2160,128]{1,0:T(8,128)(2,1)}, bf16[2160,128]{1,0:T(8,128)(2,1)S(1)}, u32[]{:S(2)}) copy-start(bf16[2160,128]{1,0:T(8,128)(2,1)S(1)} %get-tuple-element.609.refs_5_) | copy-start | bytes 1658884
  3.8 22.8 %copy-start.2 = (bf16[2,2160,128]{2,1,0:T(8,128)(2,1)}, bf16[2,2160,128]{2,1,0:T(8,128)(2,1)S(1)}, u32[]{:S(2)}) copy-start(bf16[2,2160,128]{2,1,0:T(8,128)(2,1)S(1)} %get-tuple-element.607.refs_2_.refs_1_) | copy-start | bytes 3317764
  3.8 2.9 %collective-permute-start.5 = (bf16[2,2160,128]{2,1,0:T(8,128)(2,1)S(1)}, bf16[2,2160,128]{2,1,0:T(8,128)(2,1)S(1)}, u32[]{:S(2)}, u32[]{:S(2)}) collective-permute-start(bf16[2,2160,128]{2,1,0:T(8,128)(2,1)S(1)} %get-tuple-element.608.refs_3_.refs_2_), channel_id=1, source_target_pairs={{0,1},{1,0},{2,3},{3,2},{4,5},{5,4},{6,7},{7,6},{8,9},{9,8},{10,11... | collective-permute-start | bytes 3317768 | tf_op jit(solution)/shard_map/ppermute | solution.py:466
  4.3 13.7 %collective-permute-start.4 = (bf16[2,2160,128]{2,1,0:T(8,128)(2,1)S(1)}, bf16[2,2160,128]{2,1,0:T(8,128)(2,1)}, u32[]{:S(2)}, u32[]{:S(2)}) collective-permute-start(bf16[2,2160,128]{2,1,0:T(8,128)(2,1)S(1)} %get-tuple-element.607.refs_2_.refs_1_), channel_id=1, source_target_pairs={{1,2},{3,4},{5,6},{7,8},{9,10},{11,12},{13,14},{2,1},{4,3},{6,5},{... | collective-permute-start | bytes 3317768 | tf_op jit(solution)/shard_map/ppermute | solution.py:466
  6.7 1.0 %copy-start.13 = (bf16[2,2160,128]{2,1,0:T(8,128)(2,1)}, bf16[2,2160,128]{2,1,0:T(8,128)(2,1)S(1)}, u32[]{:S(2)}) copy-start(bf16[2,2160,128]{2,1,0:T(8,128)(2,1)S(1)} %collective-permute-done.5.refs_4_.refs_3_) | copy-start | bytes 3317764
  15.7 19.9 %collective-permute-start.7 = (bf16[2,2160,128]{2,1,0:T(8,128)(2,1)}, bf16[2,2160,128]{2,1,0:T(8,128)(2,1)}, u32[]{:S(2)}, u32[]{:S(2)}) collective-permute-start(bf16[2,2160,128]{2,1,0:T(8,128)(2,1)} %get-tuple-element.604.refs_7_), channel_id=1, source_target_pairs={{0,1},{1,0},{2,3},{3,2},{4,5},{5,4},{6,7},{7,6},{8,9},{9,8},{10,11... | collective-permute-start | bytes 3317768 | tf_op jit(solution)/shard_map/ppermute | solution.py:466
  25.0 1.7 %copy-start.6 = (bf16[2,2160,128]{2,1,0:T(8,128)(2,1)S(1)}, bf16[2,2160,128]{2,1,0:T(8,128)(2,1)}, u32[]{:S(2)}) copy-start(bf16[2,2160,128]{2,1,0:T(8,128)(2,1)} %copy-done.5) | copy-start | bytes 3317764
  25.7 61.5 %collective-permute-start.6 = (bf16[2,2160,128]{2,1,0:T(8,128)(2,1)}, bf16[2,2160,128]{2,1,0:T(8,128)(2,1)S(1)}, u32[]{:S(2)}, u32[]{:S(2)}) collective-permute-start(bf16[2,2160,128]{2,1,0:T(8,128)(2,1)} %far.1.refs_2_.refs_6_), channel_id=1, source_target_pairs={{1,2},{3,4},{5,6},{7,8},{9,10},{11,12},{13,14},{2,1},{4,3},{6,5},{... | collective-permute-start | bytes 3317768 | tf_op jit(solution)/shard_map/ppermute | solution.py:466
  35.6 51.6 %copy-start = (f32[2160,128]{1,0:T(8,128)S(1)}, f32[2160,128]{1,0:T(8,128)}, u32[]{:S(2)}) copy-start(f32[2160,128]{1,0:T(8,128)} %fold_dpre.1.refs_10_) | copy-start | bytes 3317764
  35.6 51.5 %copy-start.1 = (bf16[2160,128]{1,0:T(8,128)(2,1)S(1)}, bf16[2160,128]{1,0:T(8,128)(2,1)}, u32[]{:S(2)}) copy-start(bf16[2160,128]{1,0:T(8,128)(2,1)} %get-tuple-element.358.refs_4_.refs_5_) | copy-start | bytes 1658884
  35.6 20.8 %collective-permute-start = (f32[8,2,72,128]{3,2,1,0:T(8,128)}, f32[8,2,72,128]{3,2,1,0:T(8,128)S(1)}, u32[]{:S(2)}, u32[]{:S(2)}) collective-permute-start(f32[8,2,72,128]{3,2,1,0:T(8,128)} %get-tuple-element.618), channel_id=1, source_target_pairs={{0,1},{1,0},{2,3},{3,2},{4,5},{5,4},{6,7},{7,6},{8,9},{9,8},{10,11... | collective-permute-start | bytes 1769480 | tf_op jit(solution)/shard_map/while/body/ppermute | solution.py:466
  57.6 2.4 %copy-start.8 = (f32[8,2,72,128]{3,2,1,0:T(8,128)}, f32[8,2,72,128]{3,2,1,0:T(8,128)S(1)}, u32[]{:S(2)}) copy-start(f32[8,2,72,128]{3,2,1,0:T(8,128)S(1)} %add.139) | copy-start | bytes 1769476 | tf_op jit(solution)/shard_map/while
  57.6 3.1 %copy-start.3 = (bf16[2,2160,128]{2,1,0:T(8,128)(2,1)S(1)}, bf16[2,2160,128]{2,1,0:T(8,128)(2,1)}, u32[]{:S(2)}) copy-start(bf16[2,2160,128]{2,1,0:T(8,128)(2,1)} %get-tuple-element.663.refs_5_) | copy-start | bytes 3317764 | tf_op jit(solution)/shard_map/while
  57.6 3.1 %copy-start.7 = (bf16[2,2160,128]{2,1,0:T(8,128)(2,1)S(1)}, bf16[2,2160,128]{2,1,0:T(8,128)(2,1)}, u32[]{:S(2)}) copy-start(bf16[2,2160,128]{2,1,0:T(8,128)(2,1)} %get-tuple-element.664.refs_6_) | copy-start | bytes 3317764 | tf_op jit(solution)/shard_map/while
  58.4 9.6 %collective-permute-start.1 = (f32[2,2,2,72,128]{4,3,2,1,0:T(8,128)}, f32[2,2,2,72,128]{4,3,2,1,0:T(8,128)}, u32[]{:S(2)}, u32[]{:S(2)}) collective-permute-start(f32[2,2,2,72,128]{4,3,2,1,0:T(8,128)} %dynamic-slice_bitcast_fusion.6), channel_id=1, source_target_pairs={{0,4},{1,5},{2,6},{3,7},{4,0},{5,1},{6,2},{7,3},{8,12},{9,13},{10,... | collective-permute-start | bytes 884744 | tf_op jit(solution)/shard_map/while/body/ppermute | solution.py:539
  66.2 6.2 %copy-start.4 = (bf16[2,2160,128]{2,1,0:T(8,128)(2,1)S(1)}, bf16[2,2160,128]{2,1,0:T(8,128)(2,1)}, u32[]{:S(2)}) copy-start(bf16[2,2160,128]{2,1,0:T(8,128)(2,1)} %get-tuple-element.663.refs_5_) | copy-start | bytes 3317764 | tf_op jit(solution)/shard_map/while
  69.0 0.7 copy-start.9
  69.8 9.5 %collective-permute-start.2 = (f32[2,2,72,128]{3,2,1,0:T(8,128)S(1)}, f32[2,2,72,128]{3,2,1,0:T(8,128)}, u32[]{:S(2)}, u32[]{:S(2)}) collective-permute-start(f32[2,2,72,128]{3,2,1,0:T(8,128)S(1)} %dynamic-slice_bitcast_fusion.7), channel_id=1, source_target_pairs={{0,8},{1,9},{2,10},{3,11},{4,12},{5,13},{6,14},{7,15},{8,0},{9,1},... | collective-permute-start | bytes 442376 | tf_op jit(solution)/shard_map/while/body/ppermute | solution.py:539
  81.0 4.7 %collective-permute-start.3 = (f32[2,72,128]{2,1,0:T(8,128)}, f32[2,72,128]{2,1,0:T(8,128)}, u32[]{:S(2)}, u32[]{:S(2)}) collective-permute-start(f32[2,72,128]{2,1,0:T(8,128)} %dynamic-slice_bitcast_fusion.8), channel_id=1, source_target_pairs={{0,2},{1,3},{2,0},{3,1},{4,6},{5,7},{6,4},{7,5},{8,10},{9,11},{10,... | collective-permute-start | bytes 221192 | tf_op jit(solution)/shard_map/while/body/ppermute | solution.py:539
where the time goes:
time: 92.5 us; the launch traced here: 92.1 us
  Pallas kernels  44 us (48%)
  starting transfers between devices  29.1 us (31%)
  waiting for transfers between devices  9.08 us (10%)
  local copies, waits for them, and re-layouts  4.69 us (5%)
  other arithmetic  4.15 us (4%)
  between operations  0.97 us (1%)
    pallas_call x9, Pallas kernels, call(): pl.pallas_call(run, in_specs=[SMEM] * len(scalars) + [HBM] * (n_in + len(...  44 us
    ppermute x5, starting transfers between devices, swap(): return lax.ppermute(x, 'lat', pairs)  24.4 us
    ppermute x3, waiting for transfers between devices, body(): lax.ppermute(go.astype(LINKS.get(stage, F32)), 'lat', pairs).astype(F32)  6.61 us
    ppermute x3, starting transfers between devices, body(): lax.ppermute(go.astype(LINKS.get(stage, F32)), 'lat', pairs).astype(F32)  4.73 us
    add x3, other arithmetic, body(): kept + lax.ppermute(go.astype(LINKS.get(stage, F32)), 'lat', pairs).astyp...  2.97 us
    ppermute x5, waiting for transfers between devices, swap(): return lax.ppermute(x, 'lat', pairs)  2.47 us
  transfers between devices with their start and end apart: 8, of which 5 were waited for; matrix products, arithmetic and copies ran while one was open for 8% of the time, Pallas kernels for 39%

commit v1 on v0

--- a/solution.py
+++ b/solution.py
@@ -12,6 +12,7 @@
 F32 = jnp.float32
 BF16 = jnp.bfloat16
 SMEM = pl.BlockSpec(memory_space=pltpu.SMEM)
+VMEM = pl.BlockSpec(memory_space=pltpu.VMEM)
 HBM = pl.BlockSpec(memory_space=pltpu.HBM)
 MiB = 1 << 20
 OUT, INN = 0, 1
@@ -24,7 +25,6 @@
 SCALE = np.float32(np.sqrt(2 / np.pi))
 CUBE = np.float32(0.044715)
 HALF = np.float32(0.5)
-LINKS = {}
 
 
 def chunk_of(n):
@@ -242,8 +242,9 @@
 
 
 def weights_kernel(
-    flags, outer, inner, halo_in, halo_s, halo_g, outer2, inner2, fold, spread, spread2, outs,
-    blank1, blank2, blank3, blank4, blank5, blank6, blank7, g1, g2, taps, utaps, htaps, hutaps, row, sems
+    flags, partner, outer, inner, halo_in, halo_s, halo_g, outer2, inner2, fold, spread, w1, outs,
+    spread2, blank1, blank2, blank3, blank4, blank5, blank6, blank7,
+    g1, g2, taps, utaps, htaps, hutaps, row, sems, term, total
 ):
     parity, top = flags[0], flags[1]
     keep, give = outs
@@ -291,6 +292,25 @@
                         rows = slice(at - owner * per, stop - owner * per)
                         dst[owner // 2, which, rows, :] = g[t, at - t * C : stop - t * C, :]
                         at = stop
+    outs.send(0)
+    outs.send(1)
+
+    @pl.when(top != 0)
+    def _():
+        put_taps(hutaps, 0, outer2[1], True)
+        pltpu.sync_copy(w1.at[6], htaps.at[pl.ds(0, C), pl.ds(0, C)])
+        pltpu.sync_copy(w1.at[7], htaps.at[pl.ds(C, C), pl.ds(0, C)])
+        pltpu.sync_copy(w1.at[8], htaps.at[pl.ds(2 * C, C), pl.ds(0, C)])
+        term[...] = jnp.dot(hutaps[...], htaps[: 3 * C, :C], preferred_element_type=F32)
+
+        def step(i, carry):
+            for k in range(16):
+                j = i * 16 + k
+                total[pl.ds(partner[j], 1), :] = term[pl.ds(j, 1), :]
+            return carry
+
+        lax.fori_loop(0, term.shape[0] // 16, step, 0)
+        pltpu.sync_copy(total, spread2)
 
 
 def second_forward_kernel(flags, outer2, inner2, halo, w2, outer, inner, mask_i, outs, taps, fw, y):
@@ -337,23 +357,16 @@
         pltpu.sync_copy(row, fold)
 
 
-def fold_dpre_kernel(flags, partner, outer2, w1, spread, row, kernels, tap, term, total):
-    @pl.when(flags[1] != 0)
-    def _():
-        pltpu.sync_copy(outer2.at[1], row)
-        pltpu.sync_copy(w1, kernels)
-        put_taps(tap, 0, row[...], True)
-        kernel = jnp.concatenate([kernels[6 + b] for b in range(3)], axis=0)
-        term[...] = jnp.dot(tap[...], kernel, preferred_element_type=F32)
-
-        def step(i, carry):
-            for k in range(16):
-                j = i * 16 + k
-                total[pl.ds(partner[j], 1), :] = term[pl.ds(j, 1), :]
-            return carry
-
-        lax.fori_loop(0, term.shape[0] // 16, step, 0)
-        pltpu.sync_copy(total, spread)
+def halve_kernel(which, flags, kept, taken, go, stay):
+    mine = flags[which]
+    for at in range(kept.shape[0]):
+        go[at] = kept[at, 1 - mine] + taken[at, 1 - mine]
+        stay[at] = kept[at, mine] + taken[at, mine]
+
+
+def total_kernel(kept, taken, first, second):
+    first[...] = kept[0] + taken[0]
+    second[...] = kept[1] + taken[1]
 
 
 def last_kernel(
@@ -508,35 +521,35 @@
     )[0]
     halo2 = swap(outer2, lat, False)
     halo_in2 = swap(inner2, lat, True)
-    spread2, = call(
-        fold_dpre_kernel, (flags, fold_partner), (), [],
-        [row_s, pltpu.VMEM((9, C, C), BF16), pltpu.VMEM((n, ROW), BF16), wide_s, wide_s], 60, "fold_dpre",
-        loose=(outer2, conv_first), loose_outs=[wide],
-    )
-    keep, give, own1, own2, *blank = call(
-        weights_kernel, (flags,), (outer, inner, halo_in, (halo, 0), (halo, 1), outer2, inner2), [part, part],
+    keep, give, spread2, own1, own2, *blank = call(
+        weights_kernel, (flags, fold_partner), (outer, inner, halo_in, (halo, 0), (halo, 1), outer2, inner2), [part, part],
         [pltpu.VMEM((9, C, C), F32)] * 2 + [pltpu.VMEM((n, 3 * ROW), BF16)] * 2
-        + [pltpu.VMEM((n, ROW), BF16)] * 2 + [row_s, dma((2,))], 60, "wgrad", loose=(fold1, spread1, spread2),
-        loose_outs=[own, own, row, wide, row, wide, row],
+        + [pltpu.VMEM((n, ROW), BF16)] * 2 + [row_s, dma((2,)), wide_s, wide_s], 60, "wgrad",
+        loose=(fold1, spread1, conv_first), loose_outs=[wide, own, own, row, wide, row, wide, row],
     )
 
     def body(carry):
         turn, given, _ = carry
         now = flags + 2 * turn
         arrived = swap(given, lat, True)
-        g = (keep + arrived).reshape((2,) * (bits - 1) + (2, per, C))
+        kept, taken = keep, arrived
+        params = pltpu.CompilerParams(vmem_limit_bytes=8 * MiB)
+        cost = pl.CostEstimate(flops=1000, transcendentals=0, bytes_accessed=1000)
         left = list(range(bits - 1, 0, -1))
         beside = []
         for stage, bit in enumerate(order):
             axis = left.index(bit)
+            split = (2**axis, 2, 2 ** (len(left) - axis - 1) * 2, per, C)
             left.pop(axis)
-            mine = ((index >> bit) + 2 * turn) & 1
-            kept = lax.dynamic_index_in_dim(g, mine, axis, keepdims=False)
-            go = lax.dynamic_index_in_dim(g, 1 - mine, axis, keepdims=False)
+            half = jax.ShapeDtypeStruct(split[:1] + split[2:], F32)
+            go, kept = pl.pallas_call(
+                functools.partial(halve_kernel, 2 + stage), in_specs=[SMEM, VMEM, VMEM], out_specs=(VMEM, VMEM),
+                out_shape=(half, half), compiler_params=params, cost_estimate=cost, name=f"halve{stage}",
+            )(now, kept.reshape(split), taken.reshape(split))
             if 1 <= stage <= 2:
                 go, beside[stage - 1] = lax.optimization_barrier((go, beside[stage - 1]))
             pairs = [(i, i ^ (1 << bit)) for i in range(lat)]
-            g = kept + lax.ppermute(go.astype(LINKS.get(stage, F32)), "lat", pairs).astype(F32)
+            taken = lax.ppermute(go, "lat", pairs)
             if stage == 0:
                 beside.append(
                     call(
@@ -556,7 +569,11 @@
                         near_s[0:1] + near_s[3:4] + near_s[4:5], 28, "second_adjoint",
                     )
                 )
-        return turn + 1, arrived, ([g[0], g[1]], beside)
+        total = pl.pallas_call(
+            total_kernel, in_specs=[VMEM, VMEM], out_specs=(VMEM, VMEM), out_shape=(own, own), compiler_params=params,
+            cost_estimate=cost, name="total",
+        )(kept.reshape(2, per, C), taken.reshape(2, per, C))
+        return turn + 1, arrived, (list(total), beside)
 
     stop = jnp.minimum(1, parity + 1)
     start = ([own1, own2], [[blank[0], blank[1], blank[4]], [blank[2], blank[3]]])

time: 92.5 us -> 88 us (0.951)
  other arithmetic: 4.15 us -> 0.01 us
  Pallas kernels: 44 us -> 47 us
  local copies, waits for them, and re-layouts: 4.69 us -> 1.94 us
    add x4 -> x0, other arithmetic: 4.15 us -> none  [the longest x3 2.97 us: body(): kept + lax.ppermute(go.astype(LINKS.get(stage, F32)), 'lat', pairs).astyp...]
    pallas_call x0 -> x4, Pallas kernels: none -> 3.55 us  [the longest x3 2.91 us: body(): pl.pallas_call(functools.partial(halve_kernel, 2 + stage), in_specs=[SMEM...]
    squeeze x4 -> x0, local copies, waits for them, and re-layouts: 2.03 us -> none  [the longest x3 1.4 us: body(): go = lax.dynamic_index_in_dim(g, 1 - mine, axis, keepdims=False)]
    pallas_call x9 -> x8, Pallas kernels: 44 us -> 43.4 us  [call(): pl.pallas_call(run, in_specs=[SMEM] * len(scalars) + [HBM] * (n_in + len(...]
  transfers between devices with their start and end apart: 8 -> 8, of which waited for: 5 -> 5; matrix products, arithmetic and copies ran while one was open for 8% -> 1% of each run, Pallas kernels for 39% -> 45%
where the time goes in v1:
time: 88 us; the launch traced here: 87.5 us
  Pallas kernels  47 us (53%)
  starting transfers between devices  29 us (33%)
  waiting for transfers between devices  8.6 us (10%)
  local copies, waits for them, and re-layouts  1.94 us (2%)
  between operations  0.92 us (1%)
    pallas_call x8, Pallas kernels, call(): pl.pallas_call(run, in_specs=[SMEM] * len(scalars) + [HBM] * (n_in + len(...  43.4 us
    ppermute x5, starting transfers between devices, swap(): return lax.ppermute(x, 'lat', pairs)  24.2 us
    ppermute x3, waiting for transfers between devices, body(): taken = lax.ppermute(go, 'lat', pairs)  6.13 us
    ppermute x3, starting transfers between devices, body(): taken = lax.ppermute(go, 'lat', pairs)  4.8 us
    pallas_call x3, Pallas kernels, body(): pl.pallas_call(functools.partial(halve_kernel, 2 + stage), in_specs=[SMEM...  2.91 us
    ppermute x5, waiting for transfers between devices, swap(): return lax.ppermute(x, 'lat', pairs)  2.47 us
  transfers between devices with their start and end apart: 8, of which 5 were waited for; matrix products, arithmetic and copies ran while one was open for 1% of the time, Pallas kernels for 45%

profile of v1, /device:TPU:0, one launch (start us, length us, event | category | flops | bytes accessed | tf_op | source)
XLA Modules:
  0.0 87.5 jit_solution(11210682510281970191)
XLA Ops:
  0.6 0.1 stack.27.refs_0_
  0.7 0.0 copy-start.6
  0.7 0.0 copy-start.9
  0.7 0.0 copy-start.11
  0.7 3.0 %start.1 = (bf16[2,2160,128]{2,1,0:T(8,128)(2,1)S(1)}, bf16[2,2160,128]{2,1,0:T(8,128)(2,1)S(1)}, bf16[2160,128]{1,0:T(8,128)(2,1)}, bf16[2160,128]{1,0:T(8,128)(2,1)S(1)}) custom-call(s32[5]{0:T(128)S(1)} %stack.27.refs_0_, bf16[2,2160,128]{2,1,0:T(8,128)(2,1)} %bitcast.41, bf16[2,2160,128]{2,1,0:T(8,128)(2,1)} %bitcast.42, s32[2,2160]{1,0:T(2,128)} %refs_3_.2), custom_call_target="tpu_custom_call" | custom-call | flops 1000 | bytes 1000 | tf_op jit(solution)/shard_map/start/pallas_call | solution.py:457
  3.8 0.0 copy-start.8
  3.8 0.0 copy-start.2
  3.8 0.0 copy-start.4
  3.8 0.5 collective-permute-start.5
  4.3 1.7 %collective-permute-start.4 = (bf16[2,2160,128]{2,1,0:T(8,128)(2,1)S(1)}, bf16[2,2160,128]{2,1,0:T(8,128)(2,1)}, u32[]{:S(2)}, u32[]{:S(2)}) collective-permute-start(bf16[2,2160,128]{2,1,0:T(8,128)(2,1)S(1)} %get-tuple-element.389.refs_2_), channel_id=1, source_target_pairs={{1,2},{3,4},{5,6},{7,8},{9,10},{11,12},{13,14},{2,1},{4,3},{6,5},{... | collective-permute-start | bytes 3317768 | tf_op jit(solution)/shard_map/ppermute | solution.py:479
  6.0 0.6 collective-permute-done.5.refs_4_
  6.7 0.0 copy-start.10
  6.7 1.0 %copy-done.10 = bf16[2,2160,128]{2,1,0:T(8,128)(2,1)} copy-done((bf16[2,2160,128]{2,1,0:T(8,128)(2,1)}, bf16[2,2160,128]{2,1,0:T(8,128)(2,1)S(1)}, u32[]{:S(2)}) %copy-start.10) | copy-done | bytes 1105944
  7.7 0.0 copy-done.6
  7.7 0.0 copy-done.9
  7.7 0.0 copy-done.11
  7.7 8.1 %first.1 = (bf16[2,2160,128]{2,1,0:T(8,128)(2,1)}, f32[2160,128]{1,0:T(8,128)}, f32[2160,128]{1,0:T(8,128)}, bf16[2160,128]{1,0:T(8,128)(2,1)}, bf16[2160,384]{1,0:T(8,128)(2,1)}) custom-call(s32[5]{0:T(128)S(1)} %stack.27.refs_0_, s32[2160]{0:T(1024)S(1)} %copy-done.11, bf16[2,2160,128]{2,1,0:T(8,128)(2,1)S(1)} %get-tuple-element.389.refs_2_, ...), custom_call_target="tpu_custom_call" | custom-call | flops 1000 | bytes 1000 | tf_op jit(solution)/shard_map/first/pallas_call | solution.py:457
  15.7 0.0 copy-done.8
  15.7 2.3 %collective-permute-start.7 = (bf16[2,2160,128]{2,1,0:T(8,128)(2,1)}, bf16[2,2160,128]{2,1,0:T(8,128)(2,1)}, u32[]{:S(2)}, u32[]{:S(2)}) collective-permute-start(bf16[2,2160,128]{2,1,0:T(8,128)(2,1)} %get-tuple-element.386.refs_8_), channel_id=1, source_target_pairs={{0,1},{1,0},{2,3},{3,2},{4,5},{5,4},{6,7},{7,6},{8,9},{9,8},{10,11... | collective-permute-start | bytes 3317768 | tf_op jit(solution)/shard_map/ppermute | solution.py:479
  18.0 0.0 collective-permute-done.4.refs_1_.refs_5_.refs_6_
  18.0 7.0 %far.1.refs_7_ = bf16[2,2160,128]{2,1,0:T(8,128)(2,1)} custom-call(s32[5]{0:T(128)S(1)} %stack.27.refs_0_, bf16[2,2160,128]{2,1,0:T(8,128)(2,1)} %collective-permute-done.4.refs_1_.refs_5_.refs_6_, bf16[9,128,128]{2,1,0:T(8,128)(2,1)S(1)} %copy-done.6, f32[2160,128]{1,0:T(8,128)} %get-tuple-element.154.refs_3_, ...), custom_call_target="tpu_custom_call" | custom-call | flops 1000 | bytes 1000 | tf_op jit(solution)/shard_map/far/pallas_call | solution.py:457
  25.1 0.7 collective-permute-start.6
  25.8 0.0 copy-done.2
  25.8 0.0 copy-done.4
  25.8 9.1 %wgrad.1 = (f32[8,2,72,128]{3,2,1,0:T(8,128)}, f32[8,2,72,128]{3,2,1,0:T(8,128)}, f32[2160,128]{1,0:T(8,128)}, f32[72,128]{1,0:T(8,128)}, f32[72,128]{1,0:T(8,12...) custom-call(s32[5]{0:T(128)S(1)} %stack.27.refs_0_, ...), custom_call_target="tpu_custom_call" | custom-call | flops 1000 | bytes 1000 | tf_op jit(solution)/shard_map/wgrad/pallas_call | solution.py:457
  34.9 0.0 collective-permute-done.7
  34.9 0.0 copy-start
  34.9 0.0 copy-start.1
  34.9 47.7 %while.24 = (s32[]{:T(128)}, f32[8,2,72,128]{3,2,1,0:T(8,128)}, f32[72,128]{1,0:T(8,128)}, f32[72,128]{1,0:T(8,128)}, bf16[2160,128]{1,0:T(8,128)(2,1)}, /*index...) while((s32[]{:T(128)}, f32[8,2,72,128]{3,2,1,0:T(8,128)}, ...), condition=%wide.region_1.0_spmd, body=%wide.region_0.0_spmd.sunk | while | flops 7008 | bytes 15637841 | solution.py:580
  34.9 18.9 %collective-permute-start = (f32[8,2,72,128]{3,2,1,0:T(8,128)}, f32[8,2,72,128]{3,2,1,0:T(8,128)S(1)}, u32[]{:S(2)}, u32[]{:S(2)}) collective-permute-start(f32[8,2,72,128]{3,2,1,0:T(8,128)} %get-tuple-element.397), channel_id=1, source_target_pairs={{0,1},{1,0},{2,3},{3,2},{4,5},{5,4},{6,7},{7,6},{8,9},{9,8},{10,11... | collective-permute-start | bytes 1769480 | tf_op jit(solution)/shard_map/while/body/ppermute | solution.py:479
  53.8 1.8 %collective-permute-done = f32[8,2,72,128]{3,2,1,0:T(8,128)S(1)} collective-permute-done((f32[8,2,72,128]{3,2,1,0:T(8,128)}, f32[8,2,72,128]{3,2,1,0:T(8,128)S(1)}, u32[]{:S(2)}, u32[]{:S(2)}) %collective-permute-start) | collective-permute-done | bytes 589856 | tf_op jit(solution)/shard_map/while/body/ppermute | solution.py:479
  55.7 1.1 %halve0.1 = (f32[2,4,72,128]{3,2,1,0:T(8,128)S(1)}, f32[2,4,72,128]{3,2,1,0:T(8,128)S(1)}) custom-call(s32[5]{0:T(128)S(1)} %broadcast_add_fusion.2.flags.refs_0_, f32[2,2,4,72,128]{4,3,2,1,0:T(8,128)} %bitcast.40, f32[2,2,4,72,128]{4,3,2,1,0:T(8,128)S(1)} %bitcast.33), custom_call_target="tpu_custom_call" | custom-call | flops 1000 | bytes 1000 | tf_op jit(solution)/shard_map/while/body/halve0/pallas_call | solution.py:545
  56.8 0.0 copy-start.3
  56.8 1.7 %collective-permute-start.1 = (f32[2,4,72,128]{3,2,1,0:T(8,128)S(1)}, f32[2,4,72,128]{3,2,1,0:T(8,128)S(1)}, u32[]{:S(2)}, u32[]{:S(2)}) collective-permute-start(f32[2,4,72,128]{3,2,1,0:T(8,128)S(1)} %get-tuple-element.355), channel_id=1, source_target_pairs={{0,4},{1,5},{2,6},{3,7},{4,0},{5,1},{6,2},{7,3},{8,12},{9,13},{10,... | collective-permute-start | bytes 884744 | tf_op jit(solution)/shard_map/while/body/ppermute | solution.py:552
  58.5 0.7 fold_act.1
  59.2 0.0 copy-done.3
  59.2 0.0 copy-start.5
  59.2 0.0 copy-start.7
  59.2 5.5 %second.1 = (bf16[2160,128]{1,0:T(8,128)(2,1)}, f32[2160,128]{1,0:T(8,128)}) custom-call(s32[5]{0:T(128)S(1)} %broadcast_add_fusion.2.flags.refs_0_, bf16[2,2160,128]{2,1,0:T(8,128)(2,1)} %get-tuple-element.431.refs_1_.refs_2_, bf16[2,2160,128]{2,1,0:T(8,128)(2,1)} %get-tuple-element.432.refs_2_, bf16[2,2160,128]{2,1,0:T(8,128)(2,1)} %get-tuple-element.433.refs_3_, ...), custom_call_target="tpu_custom_call" | custom-call | flops 1000 | bytes 1000 | tf_op jit(solution)/shard_map/while/body/second/pallas_call | solution.py:457
  64.7 1.4 %collective-permute-done.1 = f32[2,4,72,128]{3,2,1,0:T(8,128)S(1)} collective-permute-done((f32[2,4,72,128]{3,2,1,0:T(8,128)S(1)}, f32[2,4,72,128]{3,2,1,0:T(8,128)S(1)}, u32[]{:S(2)}, u32[]{:S(2)}) %collective-permute-start.1) | collective-permute-done | bytes 294944 | tf_op jit(solution)/shard_map/while/body/ppermute | solution.py:552
  66.2 0.6 halve1.1
  66.8 2.7 %collective-permute-start.2 = (f32[1,4,72,128]{3,2,1,0:T(8,128)S(1)}, f32[1,4,72,128]{3,2,1,0:T(8,128)S(1)}, u32[]{:S(2)}, u32[]{:S(2)}) collective-permute-start(f32[1,4,72,128]{3,2,1,0:T(8,128)S(1)} %get-tuple-element.360), channel_id=1, source_target_pairs={{0,8},{1,9},{2,10},{3,11},{4,12},{5,13},{6,14},{7,15},{8,0},{9,1},... | collective-permute-start | bytes 442376 | tf_op jit(solution)/shard_map/while/body/ppermute | solution.py:552
  69.4 0.0 copy-done.5
  69.4 0.0 copy-done.7
  69.4 5.3 %second_adjoint.1 = (bf16[2160,128]{1,0:T(8,128)(2,1)}, f32[2160,128]{1,0:T(8,128)}) custom-call(s32[5]{0:T(128)S(1)} %broadcast_add_fusion.2.flags.refs_0_, bf16[2,2160,128]{2,1,0:T(8,128)(2,1)} %get-tuple-element.431.refs_1_.refs_2_, bf16[2,2160,128]{2,1,0:T(8,128)(2,1)} %get-tuple-element.432.refs_2_, bf16[2,2160,128]{2,1,0:T(8,128)(2,1)} %get-tuple-element.433.refs_3_, ...), custom_call_target="tpu_custom_call" | custom-call | flops 1000 | bytes 1000 | tf_op jit(solution)/shard_map/while/body/second_adjoint/pallas_call | solution.py:457
  74.7 1.4 %collective-permute-done.2 = f32[1,4,72,128]{3,2,1,0:T(8,128)S(1)} collective-permute-done((f32[1,4,72,128]{3,2,1,0:T(8,128)S(1)}, f32[1,4,72,128]{3,2,1,0:T(8,128)S(1)}, u32[]{:S(2)}, u32[]{:S(2)}) %collective-permute-start.2) | collective-permute-done | bytes 147488 | tf_op jit(solution)/shard_map/while/body/ppermute | solution.py:552
  76.2 1.2 %halve2.1 = (f32[1,2,72,128]{3,2,1,0:T(8,128)}, f32[1,2,72,128]{3,2,1,0:T(8,128)S(1)}) custom-call(s32[5]{0:T(128)S(1)} %broadcast_add_fusion.2.flags.refs_0_, f32[1,2,2,72,128]{4,3,2,1,0:T(8,128)S(1)} %bitcast.36, f32[1,2,2,72,128]{4,3,2,1,0:T(8,128)S(1)} %bitcast.37), custom_call_target="tpu_custom_call" | custom-call | flops 1000 | bytes 1000 | tf_op jit(solution)/shard_map/while/body/halve2/pallas_call | solution.py:545
  77.4 0.5 collective-permute-start.3
  77.9 0.8 copy.29
  78.7 3.3 %collective-permute-done.3 = f32[1,2,72,128]{3,2,1,0:T(8,128)S(1)} collective-permute-done((f32[1,2,72,128]{3,2,1,0:T(8,128)}, f32[1,2,72,128]{3,2,1,0:T(8,128)S(1)}, u32[]{:S(2)}, u32[]{:S(2)}) %collective-permute-start.3) | collective-permute-done | bytes 73760 | tf_op jit(solution)/shard_map/while/body/ppermute | solution.py:552
  81.9 0.6 total.1
  82.6 0.0 collective-permute-done.6.refs_1_
  82.6 0.0 copy-done
  82.6 0.0 copy-done.1
  82.6 4.7 %last.1 = (bf16[2,2160,128]{2,1,0:T(8,128)(2,1)}, bf16[2,2160,128]{2,1,0:T(8,128)(2,1)}) custom-call(s32[5]{0:T(128)S(1)} %get-tuple-element.454, bf16[2,2160,128]{2,1,0:T(8,128)(2,1)S(1)} %collective-permute-done.6.refs_1_, bf16[9,128,128]{2,1,0:T(8,128)(2,1)} %get-tuple-element.452, bf16[9,128,128]{2,1,0:T(8,128)(2,1)} %get-tuple-element.451, ...), custom_call_target="tpu_custom_call" | custom-call | flops 1000 | bytes 1000 | tf_op jit(solution)/shard_map/last/pallas_call | solution.py:457
  (1 shorter events, 0.0 us)
Async XLA Ops:
  0.7 6.9 %copy-start.6 = (bf16[9,128,128]{2,1,0:T(8,128)(2,1)S(1)}, bf16[9,128,128]{2,1,0:T(8,128)(2,1)}, u32[]{:S(2)}) copy-start(bf16[9,128,128]{2,1,0:T(8,128)(2,1)} %refs_3_.3) | copy-start | bytes 884740
  0.7 6.9 %copy-start.9 = (bf16[9,128,128]{2,1,0:T(8,128)(2,1)S(1)}, bf16[9,128,128]{2,1,0:T(8,128)(2,1)}, u32[]{:S(2)}) copy-start(bf16[9,128,128]{2,1,0:T(8,128)(2,1)} %refs_2_.3) | copy-start | bytes 884740
  0.7 6.9 %copy-start.11 = (s32[2160]{0:T(1024)S(1)}, s32[2160]{0:T(1024)}, u32[]{:S(2)}) copy-start(s32[2160]{0:T(1024)} %refs_1_.3) | copy-start | bytes 25924
  3.8 12.0 %copy-start.8 = (bf16[2160,128]{1,0:T(8,128)(2,1)}, bf16[2160,128]{1,0:T(8,128)(2,1)S(1)}, u32[]{:S(2)}) copy-start(bf16[2160,128]{1,0:T(8,128)(2,1)S(1)} %get-tuple-element.391.refs_5_) | copy-start | bytes 1658884
  3.8 22.0 %copy-start.2 = (bf16[2,2160,128]{2,1,0:T(8,128)(2,1)}, bf16[2,2160,128]{2,1,0:T(8,128)(2,1)S(1)}, u32[]{:S(2)}) copy-start(bf16[2,2160,128]{2,1,0:T(8,128)(2,1)S(1)} %get-tuple-element.389.refs_2_) | copy-start | bytes 3317764
  3.8 22.0 %copy-start.4 = (bf16[2,2160,128]{2,1,0:T(8,128)(2,1)}, bf16[2,2160,128]{2,1,0:T(8,128)(2,1)S(1)}, u32[]{:S(2)}) copy-start(bf16[2,2160,128]{2,1,0:T(8,128)(2,1)S(1)} %get-tuple-element.390.refs_3_) | copy-start | bytes 3317764
  3.8 2.9 %collective-permute-start.5 = (bf16[2,2160,128]{2,1,0:T(8,128)(2,1)S(1)}, bf16[2,2160,128]{2,1,0:T(8,128)(2,1)S(1)}, u32[]{:S(2)}, u32[]{:S(2)}) collective-permute-start(bf16[2,2160,128]{2,1,0:T(8,128)(2,1)S(1)} %get-tuple-element.390.refs_3_), channel_id=1, source_target_pairs={{0,1},{1,0},{2,3},{3,2},{4,5},{5,4},{6,7},{7,6},{8,9},{9,8},{10,11... | collective-permute-start | bytes 3317768 | tf_op jit(solution)/shard_map/ppermute | solution.py:479
  4.3 13.7 %collective-permute-start.4 = (bf16[2,2160,128]{2,1,0:T(8,128)(2,1)S(1)}, bf16[2,2160,128]{2,1,0:T(8,128)(2,1)}, u32[]{:S(2)}, u32[]{:S(2)}) collective-permute-start(bf16[2,2160,128]{2,1,0:T(8,128)(2,1)S(1)} %get-tuple-element.389.refs_2_), channel_id=1, source_target_pairs={{1,2},{3,4},{5,6},{7,8},{9,10},{11,12},{13,14},{2,1},{4,3},{6,5},{... | collective-permute-start | bytes 3317768 | tf_op jit(solution)/shard_map/ppermute | solution.py:479
  6.7 1.0 %copy-start.10 = (bf16[2,2160,128]{2,1,0:T(8,128)(2,1)}, bf16[2,2160,128]{2,1,0:T(8,128)(2,1)S(1)}, u32[]{:S(2)}) copy-start(bf16[2,2160,128]{2,1,0:T(8,128)(2,1)S(1)} %collective-permute-done.5.refs_4_) | copy-start | bytes 3317764
  15.7 19.1 %collective-permute-start.7 = (bf16[2,2160,128]{2,1,0:T(8,128)(2,1)}, bf16[2,2160,128]{2,1,0:T(8,128)(2,1)}, u32[]{:S(2)}, u32[]{:S(2)}) collective-permute-start(bf16[2,2160,128]{2,1,0:T(8,128)(2,1)} %get-tuple-element.386.refs_8_), channel_id=1, source_target_pairs={{0,1},{1,0},{2,3},{3,2},{4,5},{5,4},{6,7},{7,6},{8,9},{9,8},{10,11... | collective-permute-start | bytes 3317768 | tf_op jit(solution)/shard_map/ppermute | solution.py:479
  25.1 57.5 %collective-permute-start.6 = (bf16[2,2160,128]{2,1,0:T(8,128)(2,1)}, bf16[2,2160,128]{2,1,0:T(8,128)(2,1)S(1)}, u32[]{:S(2)}, u32[]{:S(2)}) collective-permute-start(bf16[2,2160,128]{2,1,0:T(8,128)(2,1)} %far.1.refs_7_), channel_id=1, source_target_pairs={{1,2},{3,4},{5,6},{7,8},{9,10},{11,12},{13,14},{2,1},{4,3},{6,5},{... | collective-permute-start | bytes 3317768 | tf_op jit(solution)/shard_map/ppermute | solution.py:479
  34.9 47.7 %copy-start = (bf16[2160,128]{1,0:T(8,128)(2,1)S(1)}, bf16[2160,128]{1,0:T(8,128)(2,1)}, u32[]{:S(2)}) copy-start(bf16[2160,128]{1,0:T(8,128)(2,1)} %get-tuple-element.155.refs_4_.refs_5_) | copy-start | bytes 1658884
  34.9 47.7 %copy-start.1 = (f32[2160,128]{1,0:T(8,128)S(1)}, f32[2160,128]{1,0:T(8,128)}, u32[]{:S(2)}) copy-start(f32[2160,128]{1,0:T(8,128)} %get-tuple-element.174.refs_10_) | copy-start | bytes 3317764
  34.9 20.7 %collective-permute-start = (f32[8,2,72,128]{3,2,1,0:T(8,128)}, f32[8,2,72,128]{3,2,1,0:T(8,128)S(1)}, u32[]{:S(2)}, u32[]{:S(2)}) collective-permute-start(f32[8,2,72,128]{3,2,1,0:T(8,128)} %get-tuple-element.397), channel_id=1, source_target_pairs={{0,1},{1,0},{2,3},{3,2},{4,5},{5,4},{6,7},{7,6},{8,9},{9,8},{10,11... | collective-permute-start | bytes 1769480 | tf_op jit(solution)/shard_map/while/body/ppermute | solution.py:479
  56.8 2.4 %copy-start.3 = (bf16[2,2160,128]{2,1,0:T(8,128)(2,1)S(1)}, bf16[2,2160,128]{2,1,0:T(8,128)(2,1)}, u32[]{:S(2)}) copy-start(bf16[2,2160,128]{2,1,0:T(8,128)(2,1)} %get-tuple-element.435.refs_5_) | copy-start | bytes 3317764 | tf_op jit(solution)/shard_map/while
  56.8 9.4 %collective-permute-start.1 = (f32[2,4,72,128]{3,2,1,0:T(8,128)S(1)}, f32[2,4,72,128]{3,2,1,0:T(8,128)S(1)}, u32[]{:S(2)}, u32[]{:S(2)}) collective-permute-start(f32[2,4,72,128]{3,2,1,0:T(8,128)S(1)} %get-tuple-element.355), channel_id=1, source_target_pairs={{0,4},{1,5},{2,6},{3,7},{4,0},{5,1},{6,2},{7,3},{8,12},{9,13},{10,... | collective-permute-start | bytes 884744 | tf_op jit(solution)/shard_map/while/body/ppermute | solution.py:552
  59.2 10.2 %copy-start.5 = (bf16[2,2160,128]{2,1,0:T(8,128)(2,1)S(1)}, bf16[2,2160,128]{2,1,0:T(8,128)(2,1)}, u32[]{:S(2)}) copy-start(bf16[2,2160,128]{2,1,0:T(8,128)(2,1)} %get-tuple-element.436.refs_6_) | copy-start | bytes 3317764 | tf_op jit(solution)/shard_map/while
  59.2 10.2 %copy-start.7 = (bf16[9,128,128]{2,1,0:T(8,128)(2,1)S(1)}, bf16[9,128,128]{2,1,0:T(8,128)(2,1)}, u32[]{:S(2)}) copy-start(bf16[9,128,128]{2,1,0:T(8,128)(2,1)} %get-tuple-element.439.refs_4_) | copy-start | bytes 884740 | tf_op jit(solution)/shard_map/while
  66.8 9.4 %collective-permute-start.2 = (f32[1,4,72,128]{3,2,1,0:T(8,128)S(1)}, f32[1,4,72,128]{3,2,1,0:T(8,128)S(1)}, u32[]{:S(2)}, u32[]{:S(2)}) collective-permute-start(f32[1,4,72,128]{3,2,1,0:T(8,128)S(1)} %get-tuple-element.360), channel_id=1, source_target_pairs={{0,8},{1,9},{2,10},{3,11},{4,12},{5,13},{6,14},{7,15},{8,0},{9,1},... | collective-permute-start | bytes 442376 | tf_op jit(solution)/shard_map/while/body/ppermute | solution.py:552
  77.4 4.6 %collective-permute-start.3 = (f32[1,2,72,128]{3,2,1,0:T(8,128)}, f32[1,2,72,128]{3,2,1,0:T(8,128)S(1)}, u32[]{:S(2)}, u32[]{:S(2)}) collective-permute-start(f32[1,2,72,128]{3,2,1,0:T(8,128)} %get-tuple-element.365), channel_id=1, source_target_pairs={{0,2},{1,3},{2,0},{3,1},{4,6},{5,7},{6,4},{7,5},{8,10},{9,11},{10,... | collective-permute-start | bytes 221192 | tf_op jit(solution)/shard_map/while/body/ppermute | solution.py:552

commit v2 on v1

--- a/solution.py
+++ b/solution.py
@@ -25,6 +25,7 @@
 SCALE = np.float32(np.sqrt(2 / np.pi))
 CUBE = np.float32(0.044715)
 HALF = np.float32(0.5)
+LINKS = {0: BF16, 1: BF16}
 
 
 def chunk_of(n):
@@ -313,7 +314,9 @@
         pltpu.sync_copy(total, spread2)
 
 
-def second_forward_kernel(flags, outer2, inner2, halo, w2, outer, inner, mask_i, outs, taps, fw, y):
+def second_forward_kernel(
+    flags, partner, outer2, inner2, halo, w2, outer, inner, mask_i, outs, fold, taps, fw, y, src, dst, row
+):
     upd_i, upd_o = outs
     outer2, inner2, halo, w2 = outer2.now(), inner2.now(), halo.now(), w2.now()
     near_forward(flags[0], (outer2[...], inner2[...], halo[...]), w2, taps, fw, y)
@@ -325,6 +328,22 @@
         upd_i[rows, :] = (keep * (inner[rows, :].astype(F32) + y[rows, C:])).astype(BF16)
 
     over_chunks(y.shape[0], finish)
+    outs.send(0)
+    outs.send(1)
+
+    @pl.when(flags[1] != 0)
+    def _():
+        src[...] = outer2[...].astype(F32)
+
+        def step(i, carry):
+            for k in range(16):
+                j = i * 16 + k
+                dst[pl.ds(j, 1), :] = src[pl.ds(partner[j], 1), :]
+            return carry
+
+        lax.fori_loop(0, src.shape[0] // 16, step, 0)
+        row[...] = dst[...].astype(BF16)
+        pltpu.sync_copy(row, fold)
 
 
 def second_adjoint_kernel(flags, outer2, inner2, halo, w1, outer, inner, outs, taps, ad, d):
@@ -340,33 +359,16 @@
     over_chunks(d.shape[0], finish)
 
 
-def fold_act_kernel(flags, partner, outer2, fold, row, src, dst):
-    @pl.when(flags[1] != 0)
-    def _():
-        pltpu.sync_copy(outer2.at[0], row)
-        src[...] = row[...].astype(F32)
-
-        def step(i, carry):
-            for k in range(16):
-                j = i * 16 + k
-                dst[pl.ds(j, 1), :] = src[pl.ds(partner[j], 1), :]
-            return carry
-
-        lax.fori_loop(0, src.shape[0] // 16, step, 0)
-        row[...] = dst[...].astype(BF16)
-        pltpu.sync_copy(row, fold)
-
-
 def halve_kernel(which, flags, kept, taken, go, stay):
     mine = flags[which]
     for at in range(kept.shape[0]):
-        go[at] = kept[at, 1 - mine] + taken[at, 1 - mine]
-        stay[at] = kept[at, mine] + taken[at, mine]
+        go[at] = (kept[at, 1 - mine] + taken[at, 1 - mine].astype(F32)).astype(go.dtype)
+        stay[at] = kept[at, mine] + taken[at, mine].astype(F32)
 
 
 def total_kernel(kept, taken, first, second):
-    first[...] = kept[0] + taken[0]
-    second[...] = kept[1] + taken[1]
+    first[...] = kept[0] + taken[0].astype(F32)
+    second[...] = kept[1] + taken[1].astype(F32)
 
 
 def last_kernel(
@@ -542,9 +544,10 @@
             split = (2**axis, 2, 2 ** (len(left) - axis - 1) * 2, per, C)
             left.pop(axis)
             half = jax.ShapeDtypeStruct(split[:1] + split[2:], F32)
+            sent = jax.ShapeDtypeStruct(half.shape, LINKS.get(stage, F32))
             go, kept = pl.pallas_call(
                 functools.partial(halve_kernel, 2 + stage), in_specs=[SMEM, VMEM, VMEM], out_specs=(VMEM, VMEM),
-                out_shape=(half, half), compiler_params=params, cost_estimate=cost, name=f"halve{stage}",
+                out_shape=(sent, half), compiler_params=params, cost_estimate=cost, name=f"halve{stage}",
             )(now, kept.reshape(split), taken.reshape(split))
             if 1 <= stage <= 2:
                 go, beside[stage - 1] = lax.optimization_barrier((go, beside[stage - 1]))
@@ -553,13 +556,9 @@
             if stage == 0:
                 beside.append(
                     call(
-                        second_forward_kernel, (now,),
+                        second_forward_kernel, (now, fold_partner),
                         ((outer2, 0), (inner2, 0), (halo_in2, 0), conv_second, (outer, 0), (inner, 0), mask_i), [row, wide],
-                        near_s[0:1] + near_s[2:3] + near_s[4:5], 28, "second",
-                    )
-                    + call(
-                        fold_act_kernel, (now, fold_partner), (), [], [row_s, wide_s, wide_s], 16, "fold_act",
-                        loose=(outer2,), loose_outs=[row],
+                        near_s[0:1] + near_s[2:3] + near_s[4:5] + [wide_s, wide_s, row_s], 30, "second", loose_outs=[row],
                     )
                 )
                 beside.append(

time: 88 us -> 83.6 us (0.950)
  waiting for transfers between devices: 8.6 us -> 4.26 us
    ppermute x3, waiting for transfers between devices: 6.13 us -> 1.8 us  [body(): taken = lax.ppermute(go, 'lat', pairs)]
    pallas_call x8 -> x7, Pallas kernels: 43.4 us -> 43.1 us  [call(): pl.pallas_call(run, in_specs=[SMEM] * len(scalars) + [HBM] * (n_in + len(...]
  transfers between devices with their start and end apart: 8 -> 8, of which waited for: 5 -> 3; matrix products, arithmetic and copies ran while one was open for 1% -> 1% of each run, Pallas kernels for 45% -> 47%
where the time goes in v2:
time: 83.6 us; the launch traced here: 83.1 us
  Pallas kernels  46.7 us (56%)
  starting transfers between devices  29.3 us (35%)
  waiting for transfers between devices  4.26 us (5%)
  local copies, waits for them, and re-layouts  1.95 us (2%)
  between operations  0.92 us (1%)
    pallas_call x7, Pallas kernels, call(): pl.pallas_call(run, in_specs=[SMEM] * len(scalars) + [HBM] * (n_in + len(...  43.1 us
    ppermute x5, starting transfers between devices, swap(): return lax.ppermute(x, 'lat', pairs)  24.2 us
    ppermute x3, starting transfers between devices, body(): taken = lax.ppermute(go, 'lat', pairs)  5.11 us
    pallas_call x3, Pallas kernels, body(): pl.pallas_call(functools.partial(halve_kernel, 2 + stage), in_specs=[SMEM...  2.91 us
    ppermute x5, waiting for transfers between devices, swap(): return lax.ppermute(x, 'lat', pairs)  2.45 us
    ppermute x3, waiting for transfers between devices, body(): taken = lax.ppermute(go, 'lat', pairs)  1.8 us
  transfers between devices with their start and end apart: 8, of which 3 were waited for; matrix products, arithmetic and copies ran while one was open for 1% of the time, Pallas kernels for 47%

profile of v2, /device:TPU:0, one launch (start us, length us, event | category | flops | bytes accessed | tf_op | source)
XLA Modules:
  0.0 83.1 jit_solution(1300192828668731138)
XLA Ops:
  0.6 0.1 stack.27.refs_0_
  0.7 0.0 copy-start.7
  0.7 0.0 copy-start.10
  0.7 0.0 copy-start.12
  0.7 3.0 %start.1 = (bf16[2,2160,128]{2,1,0:T(8,128)(2,1)S(1)}, bf16[2,2160,128]{2,1,0:T(8,128)(2,1)S(1)}, bf16[2160,128]{1,0:T(8,128)(2,1)}, bf16[2160,128]{1,0:T(8,128)(2,1)S(1)}) custom-call(s32[5]{0:T(128)S(1)} %stack.27.refs_0_, bf16[2,2160,128]{2,1,0:T(8,128)(2,1)} %bitcast.41, bf16[2,2160,128]{2,1,0:T(8,128)(2,1)} %bitcast.42, s32[2,2160]{1,0:T(2,128)} %refs_3_.2), custom_call_target="tpu_custom_call" | custom-call | flops 1000 | bytes 1000 | tf_op jit(solution)/shard_map/start/pallas_call | solution.py:459
  3.8 0.0 copy-start.9
  3.8 0.0 copy-start.2
  3.8 0.0 copy-start.4
  3.8 0.5 collective-permute-start.5
  4.3 1.8 %collective-permute-start.4 = (bf16[2,2160,128]{2,1,0:T(8,128)(2,1)S(1)}, bf16[2,2160,128]{2,1,0:T(8,128)(2,1)}, u32[]{:S(2)}, u32[]{:S(2)}) collective-permute-start(bf16[2,2160,128]{2,1,0:T(8,128)(2,1)S(1)} %get-tuple-element.393.refs_2_), channel_id=1, source_target_pairs={{1,2},{3,4},{5,6},{7,8},{9,10},{11,12},{13,14},{2,1},{4,3},{6,5},{... | collective-permute-start | bytes 3317768 | tf_op jit(solution)/shard_map/ppermute | solution.py:481
  6.1 0.6 collective-permute-done.5.refs_4_
  6.7 0.0 copy-start.11
  6.7 1.0 %copy-done.11 = bf16[2,2160,128]{2,1,0:T(8,128)(2,1)} copy-done((bf16[2,2160,128]{2,1,0:T(8,128)(2,1)}, bf16[2,2160,128]{2,1,0:T(8,128)(2,1)S(1)}, u32[]{:S(2)}) %copy-start.11) | copy-done | bytes 1105944
  7.7 0.0 copy-done.7
  7.7 0.0 copy-done.10
  7.7 0.0 copy-done.12
  7.7 8.1 %first.1 = (bf16[2,2160,128]{2,1,0:T(8,128)(2,1)}, f32[2160,128]{1,0:T(8,128)}, f32[2160,128]{1,0:T(8,128)}, bf16[2160,128]{1,0:T(8,128)(2,1)}, bf16[2160,384]{1,0:T(8,128)(2,1)}) custom-call(s32[5]{0:T(128)S(1)} %stack.27.refs_0_, s32[2160]{0:T(1024)S(1)} %copy-done.12, bf16[2,2160,128]{2,1,0:T(8,128)(2,1)S(1)} %get-tuple-element.393.refs_2_, ...), custom_call_target="tpu_custom_call" | custom-call | flops 1000 | bytes 1000 | tf_op jit(solution)/shard_map/first/pallas_call | solution.py:459
  15.7 0.0 copy-done.9
  15.8 2.3 %collective-permute-start.7 = (bf16[2,2160,128]{2,1,0:T(8,128)(2,1)}, bf16[2,2160,128]{2,1,0:T(8,128)(2,1)}, u32[]{:S(2)}, u32[]{:S(2)}) collective-permute-start(bf16[2,2160,128]{2,1,0:T(8,128)(2,1)} %get-tuple-element.390.refs_8_), channel_id=1, source_target_pairs={{0,1},{1,0},{2,3},{3,2},{4,5},{5,4},{6,7},{7,6},{8,9},{9,8},{10,11... | collective-permute-start | bytes 3317768 | tf_op jit(solution)/shard_map/ppermute | solution.py:481
  18.0 0.0 collective-permute-done.4.refs_1_.refs_5_.refs_6_
  18.0 7.0 %far.1.refs_7_ = bf16[2,2160,128]{2,1,0:T(8,128)(2,1)} custom-call(s32[5]{0:T(128)S(1)} %stack.27.refs_0_, bf16[2,2160,128]{2,1,0:T(8,128)(2,1)} %collective-permute-done.4.refs_1_.refs_5_.refs_6_, bf16[9,128,128]{2,1,0:T(8,128)(2,1)S(1)} %copy-done.7, f32[2160,128]{1,0:T(8,128)} %get-tuple-element.155.refs_3_, ...), custom_call_target="tpu_custom_call" | custom-call | flops 1000 | bytes 1000 | tf_op jit(solution)/shard_map/far/pallas_call | solution.py:459
  25.1 0.7 collective-permute-start.6
  25.8 0.0 copy-done.2
  25.8 0.0 copy-done.4
  25.8 9.1 %wgrad.1 = (f32[8,2,72,128]{3,2,1,0:T(8,128)}, f32[8,2,72,128]{3,2,1,0:T(8,128)}, f32[2160,128]{1,0:T(8,128)}, f32[72,128]{1,0:T(8,128)}, f32[72,128]{1,0:T(8,12...) custom-call(s32[5]{0:T(128)S(1)} %stack.27.refs_0_, ...), custom_call_target="tpu_custom_call" | custom-call | flops 1000 | bytes 1000 | tf_op jit(solution)/shard_map/wgrad/pallas_call | solution.py:459
  34.9 0.0 collective-permute-done.7
  34.9 0.0 copy-start
  34.9 0.0 copy-start.1
  34.9 43.3 %while.24 = (s32[]{:T(128)}, f32[8,2,72,128]{3,2,1,0:T(8,128)}, f32[72,128]{1,0:T(8,128)}, f32[72,128]{1,0:T(8,128)}, bf16[2160,128]{1,0:T(8,128)(2,1)}, /*index...) while((s32[]{:T(128)}, f32[8,2,72,128]{3,2,1,0:T(8,128)}, ...), condition=%wide.region_1.0_spmd, body=%wide.region_0.0_spmd.sunk | while | flops 6008 | bytes 19175812 | solution.py:579
  34.9 18.9 %collective-permute-start = (f32[8,2,72,128]{3,2,1,0:T(8,128)}, f32[8,2,72,128]{3,2,1,0:T(8,128)S(1)}, u32[]{:S(2)}, u32[]{:S(2)}) collective-permute-start(f32[8,2,72,128]{3,2,1,0:T(8,128)} %get-tuple-element.400), channel_id=1, source_target_pairs={{0,1},{1,0},{2,3},{3,2},{4,5},{5,4},{6,7},{7,6},{8,9},{9,8},{10,11... | collective-permute-start | bytes 1769480 | tf_op jit(solution)/shard_map/while/body/ppermute | solution.py:481
  53.8 1.8 %collective-permute-done = f32[8,2,72,128]{3,2,1,0:T(8,128)S(1)} collective-permute-done((f32[8,2,72,128]{3,2,1,0:T(8,128)}, f32[8,2,72,128]{3,2,1,0:T(8,128)S(1)}, u32[]{:S(2)}, u32[]{:S(2)}) %collective-permute-start) | collective-permute-done | bytes 589856 | tf_op jit(solution)/shard_map/while/body/ppermute | solution.py:481
  55.7 1.1 %halve0.1 = (bf16[2,4,72,128]{3,2,1,0:T(8,128)(2,1)S(1)}, f32[2,4,72,128]{3,2,1,0:T(8,128)S(1)}) custom-call(s32[5]{0:T(128)S(1)} %broadcast_add_fusion.2.flags.refs_0_, f32[2,2,4,72,128]{4,3,2,1,0:T(8,128)} %bitcast.40, f32[2,2,4,72,128]{4,3,2,1,0:T(8,128)S(1)} %bitcast.33), custom_call_target="tpu_custom_call" | custom-call | flops 1000 | bytes 1000 | tf_op jit(solution)/shard_map/while/body/halve0/pallas_call | solution.py:548
  56.8 1.7 %collective-permute-start.1 = (bf16[2,4,72,128]{3,2,1,0:T(8,128)(2,1)S(1)}, bf16[2,4,72,128]{3,2,1,0:T(8,128)(2,1)S(1)}, u32[]{:S(2)}, u32[]{:S(2)}) collective-permute-start(bf16[2,4,72,128]{3,2,1,0:T(8,128)(2,1)S(1)} %get-tuple-element.357), channel_id=1, source_target_pairs={{0,4},{1,5},{2,6},{3,7},{4,0},{5,1},{6,2},{7,3},{8,12},{9,13},{10,... | collective-permute-start | bytes 442376 | tf_op jit(solution)/shard_map/while/body/ppermute | solution.py:555
  58.5 0.0 copy-start.3
  58.5 0.0 copy-start.5
  58.5 0.0 copy-start.6
  58.5 0.0 copy-start.8
  58.5 6.0 %second.1 = (bf16[2160,128]{1,0:T(8,128)(2,1)}, f32[2160,128]{1,0:T(8,128)}, bf16[2160,128]{1,0:T(8,128)(2,1)}) custom-call(s32[5]{0:T(128)S(1)} %broadcast_add_fusion.2.flags.refs_0_, s32[2160]{0:T(1024)S(1)} %get-tuple-element.434.refs_1_, bf16[2,2160,128]{2,1,0:T(8,128)(2,1)} %get-tuple-element.435.refs_2_.refs_1_, ...), custom_call_target="tpu_custom_call" | custom-call | flops 1000 | bytes 1000 | tf_op jit(solution)/shard_map/while/body/second/pallas_call | solution.py:459
  64.5 0.0 collective-permute-done.1
  64.5 0.6 halve1.1
  65.1 1.5 %collective-permute-start.2 = (bf16[1,4,72,128]{3,2,1,0:T(8,128)(2,1)S(1)}, bf16[1,4,72,128]{3,2,1,0:T(8,128)(2,1)S(1)}, u32[]{:S(2)}, u32[]{:S(2)}) collective-permute-start(bf16[1,4,72,128]{3,2,1,0:T(8,128)(2,1)S(1)} %get-tuple-element.363), channel_id=1, source_target_pairs={{0,8},{1,9},{2,10},{3,11},{4,12},{5,13},{6,14},{7,15},{8,0},{9,1},... | collective-permute-start | bytes 221192 | tf_op jit(solution)/shard_map/while/body/ppermute | solution.py:555
  66.6 0.0 copy-done.3
  66.6 0.0 copy-done.5
  66.6 0.0 copy-done.6
  66.6 0.0 copy-done.8
  66.6 5.2 %second_adjoint.1 = (bf16[2160,128]{1,0:T(8,128)(2,1)}, f32[2160,128]{1,0:T(8,128)}) custom-call(s32[5]{0:T(128)S(1)} %broadcast_add_fusion.2.flags.refs_0_, bf16[2,2160,128]{2,1,0:T(8,128)(2,1)S(1)} %copy-done.6, bf16[2,2160,128]{2,1,0:T(8,128)(2,1)} %get-tuple-element.436.refs_3_.refs_2_, bf16[2,2160,128]{2,1,0:T(8,128)(2,1)} %get-tuple-element.437.refs_4_.refs_3_, ...), custom_call_target="tpu_custom_call" | custom-call | flops 1000 | bytes 1000 | tf_op jit(solution)/shard_map/while/body/second_adjoint/pallas_call | solution.py:459
  71.8 0.0 collective-permute-done.2
  71.8 1.2 %halve2.1 = (f32[1,2,72,128]{3,2,1,0:T(8,128)}, f32[1,2,72,128]{3,2,1,0:T(8,128)S(1)}) custom-call(s32[5]{0:T(128)S(1)} %broadcast_add_fusion.2.flags.refs_0_, f32[1,2,2,72,128]{4,3,2,1,0:T(8,128)S(1)} %bitcast.35, bf16[1,2,2,72,128]{4,3,2,1,0:T(8,128)(2,1)S(1)} %bitcast.37), custom_call_target="tpu_custom_call" | custom-call | flops 1000 | bytes 1000 | tf_op jit(solution)/shard_map/while/body/halve2/pallas_call | solution.py:548
  73.0 1.9 %collective-permute-start.3 = (f32[1,2,72,128]{3,2,1,0:T(8,128)}, f32[1,2,72,128]{3,2,1,0:T(8,128)S(1)}, u32[]{:S(2)}, u32[]{:S(2)}) collective-permute-start(f32[1,2,72,128]{3,2,1,0:T(8,128)} %get-tuple-element.368), channel_id=1, source_target_pairs={{0,2},{1,3},{2,0},{3,1},{4,6},{5,7},{6,4},{7,5},{8,10},{9,11},{10,... | collective-permute-start | bytes 221192 | tf_op jit(solution)/shard_map/while/body/ppermute | solution.py:555
  75.0 0.8 copy.29
  75.8 1.8 %collective-permute-done.3 = f32[1,2,72,128]{3,2,1,0:T(8,128)S(1)} collective-permute-done((f32[1,2,72,128]{3,2,1,0:T(8,128)}, f32[1,2,72,128]{3,2,1,0:T(8,128)S(1)}, u32[]{:S(2)}, u32[]{:S(2)}) %collective-permute-start.3) | collective-permute-done | bytes 73760 | tf_op jit(solution)/shard_map/while/body/ppermute | solution.py:555
  77.6 0.6 total.1
  78.2 0.0 collective-permute-done.6.refs_1_
  78.2 0.0 copy-done
  78.3 0.0 copy-done.1
  78.3 4.7 %last.1 = (bf16[2,2160,128]{2,1,0:T(8,128)(2,1)}, bf16[2,2160,128]{2,1,0:T(8,128)(2,1)}) custom-call(s32[5]{0:T(128)S(1)} %get-tuple-element.458, bf16[2,2160,128]{2,1,0:T(8,128)(2,1)S(1)} %collective-permute-done.6.refs_1_, bf16[9,128,128]{2,1,0:T(8,128)(2,1)} %get-tuple-element.456, bf16[9,128,128]{2,1,0:T(8,128)(2,1)} %get-tuple-element.455, ...), custom_call_target="tpu_custom_call" | custom-call | flops 1000 | bytes 1000 | tf_op jit(solution)/shard_map/last/pallas_call | solution.py:459
  (1 shorter events, 0.0 us)
Async XLA Ops:
  0.7 6.9 %copy-start.7 = (bf16[9,128,128]{2,1,0:T(8,128)(2,1)S(1)}, bf16[9,128,128]{2,1,0:T(8,128)(2,1)}, u32[]{:S(2)}) copy-start(bf16[9,128,128]{2,1,0:T(8,128)(2,1)} %refs_3_.3) | copy-start | bytes 884740
  0.7 7.0 %copy-start.10 = (bf16[9,128,128]{2,1,0:T(8,128)(2,1)S(1)}, bf16[9,128,128]{2,1,0:T(8,128)(2,1)}, u32[]{:S(2)}) copy-start(bf16[9,128,128]{2,1,0:T(8,128)(2,1)} %refs_2_.3) | copy-start | bytes 884740
  0.7 7.0 %copy-start.12 = (s32[2160]{0:T(1024)S(1)}, s32[2160]{0:T(1024)}, u32[]{:S(2)}) copy-start(s32[2160]{0:T(1024)} %refs_1_.3) | copy-start | bytes 25924
  3.8 12.0 %copy-start.9 = (bf16[2160,128]{1,0:T(8,128)(2,1)}, bf16[2160,128]{1,0:T(8,128)(2,1)S(1)}, u32[]{:S(2)}) copy-start(bf16[2160,128]{1,0:T(8,128)(2,1)S(1)} %get-tuple-element.395.refs_5_) | copy-start | bytes 1658884
  3.8 22.0 %copy-start.2 = (bf16[2,2160,128]{2,1,0:T(8,128)(2,1)}, bf16[2,2160,128]{2,1,0:T(8,128)(2,1)S(1)}, u32[]{:S(2)}) copy-start(bf16[2,2160,128]{2,1,0:T(8,128)(2,1)S(1)} %get-tuple-element.393.refs_2_) | copy-start | bytes 3317764
  3.8 22.0 %copy-start.4 = (bf16[2,2160,128]{2,1,0:T(8,128)(2,1)}, bf16[2,2160,128]{2,1,0:T(8,128)(2,1)S(1)}, u32[]{:S(2)}) copy-start(bf16[2,2160,128]{2,1,0:T(8,128)(2,1)S(1)} %get-tuple-element.394.refs_3_) | copy-start | bytes 3317764
  3.8 2.9 %collective-permute-start.5 = (bf16[2,2160,128]{2,1,0:T(8,128)(2,1)S(1)}, bf16[2,2160,128]{2,1,0:T(8,128)(2,1)S(1)}, u32[]{:S(2)}, u32[]{:S(2)}) collective-permute-start(bf16[2,2160,128]{2,1,0:T(8,128)(2,1)S(1)} %get-tuple-element.394.refs_3_), channel_id=1, source_target_pairs={{0,1},{1,0},{2,3},{3,2},{4,5},{5,4},{6,7},{7,6},{8,9},{9,8},{10,11... | collective-permute-start | bytes 3317768 | tf_op jit(solution)/shard_map/ppermute | solution.py:481
  4.3 13.7 %collective-permute-start.4 = (bf16[2,2160,128]{2,1,0:T(8,128)(2,1)S(1)}, bf16[2,2160,128]{2,1,0:T(8,128)(2,1)}, u32[]{:S(2)}, u32[]{:S(2)}) collective-permute-start(bf16[2,2160,128]{2,1,0:T(8,128)(2,1)S(1)} %get-tuple-element.393.refs_2_), channel_id=1, source_target_pairs={{1,2},{3,4},{5,6},{7,8},{9,10},{11,12},{13,14},{2,1},{4,3},{6,5},{... | collective-permute-start | bytes 3317768 | tf_op jit(solution)/shard_map/ppermute | solution.py:481
  6.7 1.0 %copy-start.11 = (bf16[2,2160,128]{2,1,0:T(8,128)(2,1)}, bf16[2,2160,128]{2,1,0:T(8,128)(2,1)S(1)}, u32[]{:S(2)}) copy-start(bf16[2,2160,128]{2,1,0:T(8,128)(2,1)S(1)} %collective-permute-done.5.refs_4_) | copy-start | bytes 3317764
  15.8 19.1 %collective-permute-start.7 = (bf16[2,2160,128]{2,1,0:T(8,128)(2,1)}, bf16[2,2160,128]{2,1,0:T(8,128)(2,1)}, u32[]{:S(2)}, u32[]{:S(2)}) collective-permute-start(bf16[2,2160,128]{2,1,0:T(8,128)(2,1)} %get-tuple-element.390.refs_8_), channel_id=1, source_target_pairs={{0,1},{1,0},{2,3},{3,2},{4,5},{5,4},{6,7},{7,6},{8,9},{9,8},{10,11... | collective-permute-start | bytes 3317768 | tf_op jit(solution)/shard_map/ppermute | solution.py:481
  25.1 53.2 %collective-permute-start.6 = (bf16[2,2160,128]{2,1,0:T(8,128)(2,1)}, bf16[2,2160,128]{2,1,0:T(8,128)(2,1)S(1)}, u32[]{:S(2)}, u32[]{:S(2)}) collective-permute-start(bf16[2,2160,128]{2,1,0:T(8,128)(2,1)} %far.1.refs_7_), channel_id=1, source_target_pairs={{1,2},{3,4},{5,6},{7,8},{9,10},{11,12},{13,14},{2,1},{4,3},{6,5},{... | collective-permute-start | bytes 3317768 | tf_op jit(solution)/shard_map/ppermute | solution.py:481
  34.9 43.3 %copy-start = (bf16[2160,128]{1,0:T(8,128)(2,1)S(1)}, bf16[2160,128]{1,0:T(8,128)(2,1)}, u32[]{:S(2)}) copy-start(bf16[2160,128]{1,0:T(8,128)(2,1)} %get-tuple-element.156.refs_4_.refs_5_) | copy-start | bytes 1658884
  34.9 43.3 %copy-start.1 = (f32[2160,128]{1,0:T(8,128)S(1)}, f32[2160,128]{1,0:T(8,128)}, u32[]{:S(2)}) copy-start(f32[2160,128]{1,0:T(8,128)} %get-tuple-element.175.refs_10_) | copy-start | bytes 3317764
  34.9 20.7 %collective-permute-start = (f32[8,2,72,128]{3,2,1,0:T(8,128)}, f32[8,2,72,128]{3,2,1,0:T(8,128)S(1)}, u32[]{:S(2)}, u32[]{:S(2)}) collective-permute-start(f32[8,2,72,128]{3,2,1,0:T(8,128)} %get-tuple-element.400), channel_id=1, source_target_pairs={{0,1},{1,0},{2,3},{3,2},{4,5},{5,4},{6,7},{7,6},{8,9},{9,8},{10,11... | collective-permute-start | bytes 1769480 | tf_op jit(solution)/shard_map/while/body/ppermute | solution.py:481
  56.8 7.7 %collective-permute-start.1 = (bf16[2,4,72,128]{3,2,1,0:T(8,128)(2,1)S(1)}, bf16[2,4,72,128]{3,2,1,0:T(8,128)(2,1)S(1)}, u32[]{:S(2)}, u32[]{:S(2)}) collective-permute-start(bf16[2,4,72,128]{3,2,1,0:T(8,128)(2,1)S(1)} %get-tuple-element.357), channel_id=1, source_target_pairs={{0,4},{1,5},{2,6},{3,7},{4,0},{5,1},{6,2},{7,3},{8,12},{9,13},{10,... | collective-permute-start | bytes 442376 | tf_op jit(solution)/shard_map/while/body/ppermute | solution.py:555
  58.5 8.1 %copy-start.3 = (bf16[2,2160,128]{2,1,0:T(8,128)(2,1)S(1)}, bf16[2,2160,128]{2,1,0:T(8,128)(2,1)}, u32[]{:S(2)}) copy-start(bf16[2,2160,128]{2,1,0:T(8,128)(2,1)} %get-tuple-element.439.refs_6_.refs_5_) | copy-start | bytes 3317764 | tf_op jit(solution)/shard_map/while
  58.5 8.1 %copy-start.5 = (bf16[2,2160,128]{2,1,0:T(8,128)(2,1)S(1)}, bf16[2,2160,128]{2,1,0:T(8,128)(2,1)}, u32[]{:S(2)}) copy-start(bf16[2,2160,128]{2,1,0:T(8,128)(2,1)} %get-tuple-element.440.refs_7_.refs_6_) | copy-start | bytes 3317764 | tf_op jit(solution)/shard_map/while
  58.5 8.1 %copy-start.6 = (bf16[2,2160,128]{2,1,0:T(8,128)(2,1)S(1)}, bf16[2,2160,128]{2,1,0:T(8,128)(2,1)}, u32[]{:S(2)}) copy-start(bf16[2,2160,128]{2,1,0:T(8,128)(2,1)} %get-tuple-element.435.refs_2_.refs_1_) | copy-start | bytes 3317764 | tf_op jit(solution)/shard_map/while
  58.5 8.1 %copy-start.8 = (bf16[9,128,128]{2,1,0:T(8,128)(2,1)S(1)}, bf16[9,128,128]{2,1,0:T(8,128)(2,1)}, u32[]{:S(2)}) copy-start(bf16[9,128,128]{2,1,0:T(8,128)(2,1)} %get-tuple-element.442.refs_4_) | copy-start | bytes 884740 | tf_op jit(solution)/shard_map/while
  65.1 6.8 %collective-permute-start.2 = (bf16[1,4,72,128]{3,2,1,0:T(8,128)(2,1)S(1)}, bf16[1,4,72,128]{3,2,1,0:T(8,128)(2,1)S(1)}, u32[]{:S(2)}, u32[]{:S(2)}) collective-permute-start(bf16[1,4,72,128]{3,2,1,0:T(8,128)(2,1)S(1)} %get-tuple-element.363), channel_id=1, source_target_pairs={{0,8},{1,9},{2,10},{3,11},{4,12},{5,13},{6,14},{7,15},{8,0},{9,1},... | collective-permute-start | bytes 221192 | tf_op jit(solution)/shard_map/while/body/ppermute | solution.py:555
  73.0 4.6 %collective-permute-start.3 = (f32[1,2,72,128]{3,2,1,0:T(8,128)}, f32[1,2,72,128]{3,2,1,0:T(8,128)S(1)}, u32[]{:S(2)}, u32[]{:S(2)}) collective-permute-start(f32[1,2,72,128]{3,2,1,0:T(8,128)} %get-tuple-element.368), channel_id=1, source_target_pairs={{0,2},{1,3},{2,0},{3,1},{4,6},{5,7},{6,4},{7,5},{8,10},{9,11},{10,... | collective-permute-start | bytes 221192 | tf_op jit(solution)/shard_map/while/body/ppermute | solution.py:555

commit v3 on v2

--- a/solution.py
+++ b/solution.py
@@ -206,38 +206,42 @@
         put_taps(taps, 0, row[...], False)
 
 
-def adjoint_taps(utaps, halo, copy, top):
+def adjoint_taps(utaps, at, halo, copy, top):
     @pl.when(top == 0)
     def _():
-        put_taps(utaps, 0, halo[...], True)
+        put_taps(utaps, at, halo[...], True)
 
     @pl.when(top != 0)
     def _():
         copy.wait()
 
 
+def build_far(dst, w_f, a_f, w_a, a_a):
+    dst[...] = jnp.zeros_like(dst)
+    for b in range(3):
+        dst[C * b : C * b + C, :C] = w_f[3 * a_f + b].astype(F32).T.astype(BF16)
+        dst[ROW + C * b : ROW + C * b + C, C:] = w_a[3 * a_a + b]
+
+
 def far_kernel(
-    flags, halo_s, w1, pre_o, mask_o, halo_g, w2, dact_o, fold, spread, outs, taps, utaps, y, d, row, sems
+    flags, halo_s, w1, pre_o, mask_o, halo_g, w2, dact_o, fold, spread, outs, taps, kernels, y, row, sems
 ):
     parity, top = flags[0], flags[1]
     act, dpre = outs[0].at[0], outs[0].at[1]
-    copies = top_copies(top, fold, row, spread, utaps, sems)
-    halo_s, w1 = halo_s.now(), w1.now()
+    copies = top_copies(top, fold, row, spread, taps.at[:, pl.ds(ROW, ROW)], sems)
+    w1, w2 = w1.now(), w2.now()
+    build_far(kernels, w1, row_tap(0, parity), w2, row_tap(2 - 2 * top, parity))
+    halo_s, halo_g = halo_s.now(), halo_g.now()
     forward_taps(taps, halo_s, row, copies[0], top)
-    kernel = jnp.concatenate([w1[3 * row_tap(0, parity) + b] for b in range(3)], axis=1)
-    y[...] = lax.dot_general(taps[...], kernel, CONTRACT_LAST, preferred_element_type=F32)
-    halo_g, w2 = halo_g.now(), w2.now()
-    adjoint_taps(utaps, halo_g, copies[1], top)
-    a = row_tap(2 - 2 * top, parity)
-    kernel = jnp.concatenate([w2[3 * a + b] for b in range(3)], axis=0)
-    d[...] = jnp.dot(utaps[...], kernel, preferred_element_type=F32)
+    adjoint_taps(taps, ROW, halo_g, copies[1], top)
+    y[...] = jnp.dot(taps[...], kernels[...], preferred_element_type=F32)
     pre_o, dact_o, mask_o = pre_o.now(), dact_o.now(), mask_o.now()
 
     def step(rows):
         keep = mask_o[rows, :].astype(F32)
-        value, slope = gelu_and_slope(pre_o[rows, :] + y[rows, :])
+        value, slope = gelu_and_slope(pre_o[rows, :] + y[rows, :C])
         act[rows, :] = (keep * value).astype(BF16)
-        dpre[rows, :] = (slope * (keep * (dact_o[rows, :] + d[rows, :]))).astype(BF16)
+        dpre[rows, :] = (slope * (keep * (dact_o[rows, :] + y[rows, C:]))).astype(BF16)
 
     over_chunks(y.shape[0], step)
 
@@ -255,7 +259,7 @@
         put_taps(taps, ROW * k, pair[0], False)
         put_taps(utaps, ROW * k, pair[1], True)
     forward_taps(htaps, halo_s.now(), row, copies[0], top)
-    adjoint_taps(hutaps, halo_g.now(), copies[1], top)
+    adjoint_taps(hutaps, 0, halo_g.now(), copies[1], top)
     outer2, inner2 = outer2.now(), inner2.now()
     act = jnp.concatenate([outer2[0], inner2[0]], axis=1)
     dpre = jnp.concatenate([outer2[1], inner2[1]], axis=1)
@@ -502,7 +506,7 @@
     near_s = [pltpu.VMEM((n, 3 * ROW), BF16)] * 2 + [pltpu.VMEM((2 * C, 3 * ROW), BF16), pltpu.VMEM((3 * ROW, 2 * C), BF16)]
     near_s = near_s + [pltpu.VMEM((n, 2 * C), F32)] * 2
     dma = pltpu.SemaphoreType.DMA
-    far_s = [pltpu.VMEM((n, ROW), BF16)] * 2 + [wide_s] * 2 + [row_s, dma((2,))]
+    far_s = [pltpu.VMEM((n, 2 * ROW), BF16), pltpu.VMEM((2 * ROW, 2 * C), BF16), pltpu.VMEM((n, 2 * C), F32), row_s, dma((2,))]
     padded = pl.cdiv(n, C) * C
 
     outer, inner, mask_o, mask_i = call(
@@ -581,7 +585,7 @@
     (upd_i, upd_o), (grad_i, grad_o) = near[:2], near_a[:2]
     updated, grad = call(
         last_kernel, (flags,), (halo2, conv_second, conv_first, upd_o, mask_o, grad_o, upd_i, grad_i), [],
-        far_s + [row_s, row_s, dma((4,))], 28, "last", loose=tuple(fold2), loose_outs=[pair, pair],
+        [pltpu.VMEM((n, ROW), BF16)] * 2 + [wide_s] * 2 + [row_s, dma((2,)), row_s, row_s, dma((4,))], 28, "last", loose=tuple(fold2), loose_outs=[pair, pair],
     )
     return (updated.transpose(2, 0, 1), grad.transpose(2, 0, 1), g1, g2)
 

time: 83.6 us -> 82.7 us (0.989)
  Pallas kernels: 46.7 us -> 45.8 us
    pallas_call x7, Pallas kernels: 43.1 us -> 42.2 us  [call(): pl.pallas_call(run, in_specs=[SMEM] * len(scalars) + [HBM] * (n_in + len(...]
  transfers between devices with their start and end apart: 8 -> 8, of which waited for: 3 -> 3; matrix products, arithmetic and copies ran while one was open for 1% -> 1% of each run, Pallas kernels for 47% -> 46%
where the time goes in v3:
time: 82.7 us; the launch traced here: 82.2 us
  Pallas kernels  45.8 us (55%)
  starting transfers between devices  29.3 us (35%)
  waiting for transfers between devices  4.25 us (5%)
  local copies, waits for them, and re-layouts  1.95 us (2%)
  between operations  0.92 us (1%)
    pallas_call x7, Pallas kernels, call(): pl.pallas_call(run, in_specs=[SMEM] * len(scalars) + [HBM] * (n_in + len(...  42.2 us
    ppermute x5, starting transfers between devices, swap(): return lax.ppermute(x, 'lat', pairs)  24.2 us
    ppermute x3, starting transfers between devices, body(): taken = lax.ppermute(go, 'lat', pairs)  5.11 us
    pallas_call x3, Pallas kernels, body(): pl.pallas_call(functools.partial(halve_kernel, 2 + stage), in_specs=[SMEM...  2.91 us
    ppermute x5, waiting for transfers between devices, swap(): return lax.ppermute(x, 'lat', pairs)  2.45 us
    ppermute x3, waiting for transfers between devices, body(): taken = lax.ppermute(go, 'lat', pairs)  1.8 us
  transfers between devices with their start and end apart: 8, of which 3 were waited for; matrix products, arithmetic and copies ran while one was open for 1% of the time, Pallas kernels for 46%

profile of v3, /device:TPU:0, one launch (start us, length us, event | category | flops | bytes accessed | tf_op | source)
XLA Modules:
  0.0 82.2 jit_solution(11035204237755204718)
XLA Ops:
  0.6 0.1 stack.27.refs_0_
  0.7 0.0 copy-start.7
  0.7 0.0 copy-start.10
  0.7 0.0 copy-start.12
  0.7 3.0 %start.1 = (bf16[2,2160,128]{2,1,0:T(8,128)(2,1)S(1)}, bf16[2,2160,128]{2,1,0:T(8,128)(2,1)S(1)}, bf16[2160,128]{1,0:T(8,128)(2,1)}, bf16[2160,128]{1,0:T(8,128)(2,1)S(1)}) custom-call(s32[5]{0:T(128)S(1)} %stack.27.refs_0_, bf16[2,2160,128]{2,1,0:T(8,128)(2,1)} %bitcast.41, bf16[2,2160,128]{2,1,0:T(8,128)(2,1)} %bitcast.42, s32[2,2160]{1,0:T(2,128)} %refs_3_.2), custom_call_target="tpu_custom_call" | custom-call | flops 1000 | bytes 1000 | tf_op jit(solution)/shard_map/start/pallas_call | solution.py:463
  3.8 0.0 copy-start.9
  3.8 0.0 copy-start.2
  3.8 0.0 copy-start.4
  3.8 0.5 collective-permute-start.5
  4.3 1.8 %collective-permute-start.4 = (bf16[2,2160,128]{2,1,0:T(8,128)(2,1)S(1)}, bf16[2,2160,128]{2,1,0:T(8,128)(2,1)}, u32[]{:S(2)}, u32[]{:S(2)}) collective-permute-start(bf16[2,2160,128]{2,1,0:T(8,128)(2,1)S(1)} %get-tuple-element.393.refs_2_), channel_id=1, source_target_pairs={{1,2},{3,4},{5,6},{7,8},{9,10},{11,12},{13,14},{2,1},{4,3},{6,5},{... | collective-permute-start | bytes 3317768 | tf_op jit(solution)/shard_map/ppermute | solution.py:485
  6.1 0.6 collective-permute-done.5.refs_4_
  6.7 0.0 copy-start.11
  6.7 1.0 %copy-done.11 = bf16[2,2160,128]{2,1,0:T(8,128)(2,1)} copy-done((bf16[2,2160,128]{2,1,0:T(8,128)(2,1)}, bf16[2,2160,128]{2,1,0:T(8,128)(2,1)S(1)}, u32[]{:S(2)}) %copy-start.11) | copy-done | bytes 1105944
  7.7 0.0 copy-done.7
  7.7 0.0 copy-done.10
  7.7 0.0 copy-done.12
  7.7 8.1 %first.1 = (bf16[2,2160,128]{2,1,0:T(8,128)(2,1)}, f32[2160,128]{1,0:T(8,128)}, f32[2160,128]{1,0:T(8,128)}, bf16[2160,128]{1,0:T(8,128)(2,1)}, bf16[2160,384]{1,0:T(8,128)(2,1)}) custom-call(s32[5]{0:T(128)S(1)} %stack.27.refs_0_, s32[2160]{0:T(1024)S(1)} %copy-done.12, bf16[2,2160,128]{2,1,0:T(8,128)(2,1)S(1)} %get-tuple-element.393.refs_2_, ...), custom_call_target="tpu_custom_call" | custom-call | flops 1000 | bytes 1000 | tf_op jit(solution)/shard_map/first/pallas_call | solution.py:463
  15.7 0.0 copy-done.9
  15.8 2.3 %collective-permute-start.7 = (bf16[2,2160,128]{2,1,0:T(8,128)(2,1)}, bf16[2,2160,128]{2,1,0:T(8,128)(2,1)}, u32[]{:S(2)}, u32[]{:S(2)}) collective-permute-start(bf16[2,2160,128]{2,1,0:T(8,128)(2,1)} %get-tuple-element.390.refs_8_), channel_id=1, source_target_pairs={{0,1},{1,0},{2,3},{3,2},{4,5},{5,4},{6,7},{7,6},{8,9},{9,8},{10,11... | collective-permute-start | bytes 3317768 | tf_op jit(solution)/shard_map/ppermute | solution.py:485
  18.0 0.0 collective-permute-done.4.refs_1_.refs_5_.refs_6_
  18.0 6.1 %far.1.refs_7_ = bf16[2,2160,128]{2,1,0:T(8,128)(2,1)} custom-call(s32[5]{0:T(128)S(1)} %stack.27.refs_0_, bf16[2,2160,128]{2,1,0:T(8,128)(2,1)} %collective-permute-done.4.refs_1_.refs_5_.refs_6_, bf16[9,128,128]{2,1,0:T(8,128)(2,1)S(1)} %copy-done.7, f32[2160,128]{1,0:T(8,128)} %get-tuple-element.155.refs_3_, ...), custom_call_target="tpu_custom_call" | custom-call | flops 1000 | bytes 1000 | tf_op jit(solution)/shard_map/far/pallas_call | solution.py:463
  24.2 0.7 collective-permute-start.6
  24.9 0.0 copy-done.2
  24.9 0.0 copy-done.4
  24.9 9.1 %wgrad.1 = (f32[8,2,72,128]{3,2,1,0:T(8,128)}, f32[8,2,72,128]{3,2,1,0:T(8,128)}, f32[2160,128]{1,0:T(8,128)}, f32[72,128]{1,0:T(8,128)}, f32[72,128]{1,0:T(8,12...) custom-call(s32[5]{0:T(128)S(1)} %stack.27.refs_0_, ...), custom_call_target="tpu_custom_call" | custom-call | flops 1000 | bytes 1000 | tf_op jit(solution)/shard_map/wgrad/pallas_call | solution.py:463
  34.0 0.0 collective-permute-done.7
  34.0 0.0 copy-start
  34.0 0.0 copy-start.1
  34.0 43.3 %while.24 = (s32[]{:T(128)}, f32[8,2,72,128]{3,2,1,0:T(8,128)}, f32[72,128]{1,0:T(8,128)}, f32[72,128]{1,0:T(8,128)}, bf16[2160,128]{1,0:T(8,128)(2,1)}, /*index...) while((s32[]{:T(128)}, f32[8,2,72,128]{3,2,1,0:T(8,128)}, ...), condition=%wide.region_1.0_spmd, body=%wide.region_0.0_spmd.sunk | while | flops 6008 | bytes 19175812 | solution.py:583
  34.0 18.9 %collective-permute-start = (f32[8,2,72,128]{3,2,1,0:T(8,128)}, f32[8,2,72,128]{3,2,1,0:T(8,128)S(1)}, u32[]{:S(2)}, u32[]{:S(2)}) collective-permute-start(f32[8,2,72,128]{3,2,1,0:T(8,128)} %get-tuple-element.400), channel_id=1, source_target_pairs={{0,1},{1,0},{2,3},{3,2},{4,5},{5,4},{6,7},{7,6},{8,9},{9,8},{10,11... | collective-permute-start | bytes 1769480 | tf_op jit(solution)/shard_map/while/body/ppermute | solution.py:485
  52.9 1.8 %collective-permute-done = f32[8,2,72,128]{3,2,1,0:T(8,128)S(1)} collective-permute-done((f32[8,2,72,128]{3,2,1,0:T(8,128)}, f32[8,2,72,128]{3,2,1,0:T(8,128)S(1)}, u32[]{:S(2)}, u32[]{:S(2)}) %collective-permute-start) | collective-permute-done | bytes 589856 | tf_op jit(solution)/shard_map/while/body/ppermute | solution.py:485
  54.8 1.1 %halve0.1 = (bf16[2,4,72,128]{3,2,1,0:T(8,128)(2,1)S(1)}, f32[2,4,72,128]{3,2,1,0:T(8,128)S(1)}) custom-call(s32[5]{0:T(128)S(1)} %broadcast_add_fusion.2.flags.refs_0_, f32[2,2,4,72,128]{4,3,2,1,0:T(8,128)} %bitcast.40, f32[2,2,4,72,128]{4,3,2,1,0:T(8,128)S(1)} %bitcast.33), custom_call_target="tpu_custom_call" | custom-call | flops 1000 | bytes 1000 | tf_op jit(solution)/shard_map/while/body/halve0/pallas_call | solution.py:552
  55.9 1.7 %collective-permute-start.1 = (bf16[2,4,72,128]{3,2,1,0:T(8,128)(2,1)S(1)}, bf16[2,4,72,128]{3,2,1,0:T(8,128)(2,1)S(1)}, u32[]{:S(2)}, u32[]{:S(2)}) collective-permute-start(bf16[2,4,72,128]{3,2,1,0:T(8,128)(2,1)S(1)} %get-tuple-element.357), channel_id=1, source_target_pairs={{0,4},{1,5},{2,6},{3,7},{4,0},{5,1},{6,2},{7,3},{8,12},{9,13},{10,... | collective-permute-start | bytes 442376 | tf_op jit(solution)/shard_map/while/body/ppermute | solution.py:559
  57.6 0.0 copy-start.3
  57.6 0.0 copy-start.5
  57.6 0.0 copy-start.6
  57.6 0.0 copy-start.8
  57.6 6.0 %second.1 = (bf16[2160,128]{1,0:T(8,128)(2,1)}, f32[2160,128]{1,0:T(8,128)}, bf16[2160,128]{1,0:T(8,128)(2,1)}) custom-call(s32[5]{0:T(128)S(1)} %broadcast_add_fusion.2.flags.refs_0_, s32[2160]{0:T(1024)S(1)} %get-tuple-element.434.refs_1_, bf16[2,2160,128]{2,1,0:T(8,128)(2,1)} %get-tuple-element.435.refs_2_.refs_1_, ...), custom_call_target="tpu_custom_call" | custom-call | flops 1000 | bytes 1000 | tf_op jit(solution)/shard_map/while/body/second/pallas_call | solution.py:463
  63.6 0.0 collective-permute-done.1
  63.6 0.6 halve1.1
  64.2 1.5 %collective-permute-start.2 = (bf16[1,4,72,128]{3,2,1,0:T(8,128)(2,1)S(1)}, bf16[1,4,72,128]{3,2,1,0:T(8,128)(2,1)S(1)}, u32[]{:S(2)}, u32[]{:S(2)}) collective-permute-start(bf16[1,4,72,128]{3,2,1,0:T(8,128)(2,1)S(1)} %get-tuple-element.363), channel_id=1, source_target_pairs={{0,8},{1,9},{2,10},{3,11},{4,12},{5,13},{6,14},{7,15},{8,0},{9,1},... | collective-permute-start | bytes 221192 | tf_op jit(solution)/shard_map/while/body/ppermute | solution.py:559
  65.7 0.0 copy-done.3
  65.7 0.0 copy-done.5
  65.7 0.0 copy-done.6
  65.7 0.0 copy-done.8
  65.7 5.2 %second_adjoint.1 = (bf16[2160,128]{1,0:T(8,128)(2,1)}, f32[2160,128]{1,0:T(8,128)}) custom-call(s32[5]{0:T(128)S(1)} %broadcast_add_fusion.2.flags.refs_0_, bf16[2,2160,128]{2,1,0:T(8,128)(2,1)S(1)} %copy-done.6, bf16[2,2160,128]{2,1,0:T(8,128)(2,1)} %get-tuple-element.436.refs_3_.refs_2_, bf16[2,2160,128]{2,1,0:T(8,128)(2,1)} %get-tuple-element.437.refs_4_.refs_3_, ...), custom_call_target="tpu_custom_call" | custom-call | flops 1000 | bytes 1000 | tf_op jit(solution)/shard_map/while/body/second_adjoint/pallas_call | solution.py:463
  70.9 0.0 collective-permute-done.2
  70.9 1.2 %halve2.1 = (f32[1,2,72,128]{3,2,1,0:T(8,128)}, f32[1,2,72,128]{3,2,1,0:T(8,128)S(1)}) custom-call(s32[5]{0:T(128)S(1)} %broadcast_add_fusion.2.flags.refs_0_, f32[1,2,2,72,128]{4,3,2,1,0:T(8,128)S(1)} %bitcast.35, bf16[1,2,2,72,128]{4,3,2,1,0:T(8,128)(2,1)S(1)} %bitcast.37), custom_call_target="tpu_custom_call" | custom-call | flops 1000 | bytes 1000 | tf_op jit(solution)/shard_map/while/body/halve2/pallas_call | solution.py:552
  72.1 1.9 %collective-permute-start.3 = (f32[1,2,72,128]{3,2,1,0:T(8,128)}, f32[1,2,72,128]{3,2,1,0:T(8,128)S(1)}, u32[]{:S(2)}, u32[]{:S(2)}) collective-permute-start(f32[1,2,72,128]{3,2,1,0:T(8,128)} %get-tuple-element.368), channel_id=1, source_target_pairs={{0,2},{1,3},{2,0},{3,1},{4,6},{5,7},{6,4},{7,5},{8,10},{9,11},{10,... | collective-permute-start | bytes 221192 | tf_op jit(solution)/shard_map/while/body/ppermute | solution.py:559
  74.1 0.8 %copy.29 = f32[8,2,72,128]{3,2,1,0:T(8,128)} copy(f32[8,2,72,128]{3,2,1,0:T(8,128)S(1)} %collective-permute-done) | data formatting | bytes 1179648 | tf_op jit(solution)/shard_map/while
  74.9 1.8 %collective-permute-done.3 = f32[1,2,72,128]{3,2,1,0:T(8,128)S(1)} collective-permute-done((f32[1,2,72,128]{3,2,1,0:T(8,128)}, f32[1,2,72,128]{3,2,1,0:T(8,128)S(1)}, u32[]{:S(2)}, u32[]{:S(2)}) %collective-permute-start.3) | collective-permute-done | bytes 73760 | tf_op jit(solution)/shard_map/while/body/ppermute | solution.py:559
  76.7 0.6 total.1
  77.3 0.0 collective-permute-done.6.refs_1_
  77.3 0.0 copy-done
  77.3 0.0 copy-done.1
  77.3 4.7 %last.1 = (bf16[2,2160,128]{2,1,0:T(8,128)(2,1)}, bf16[2,2160,128]{2,1,0:T(8,128)(2,1)}) custom-call(s32[5]{0:T(128)S(1)} %get-tuple-element.458, bf16[2,2160,128]{2,1,0:T(8,128)(2,1)S(1)} %collective-permute-done.6.refs_1_, bf16[9,128,128]{2,1,0:T(8,128)(2,1)} %get-tuple-element.456, bf16[9,128,128]{2,1,0:T(8,128)(2,1)} %get-tuple-element.455, ...), custom_call_target="tpu_custom_call" | custom-call | flops 1000 | bytes 1000 | tf_op jit(solution)/shard_map/last/pallas_call | solution.py:463
  (1 shorter events, 0.0 us)
Async XLA Ops:
  0.7 6.9 %copy-start.7 = (bf16[9,128,128]{2,1,0:T(8,128)(2,1)S(1)}, bf16[9,128,128]{2,1,0:T(8,128)(2,1)}, u32[]{:S(2)}) copy-start(bf16[9,128,128]{2,1,0:T(8,128)(2,1)} %refs_3_.3) | copy-start | bytes 884740
  0.7 7.0 %copy-start.10 = (bf16[9,128,128]{2,1,0:T(8,128)(2,1)S(1)}, bf16[9,128,128]{2,1,0:T(8,128)(2,1)}, u32[]{:S(2)}) copy-start(bf16[9,128,128]{2,1,0:T(8,128)(2,1)} %refs_2_.3) | copy-start | bytes 884740
  0.7 7.0 %copy-start.12 = (s32[2160]{0:T(1024)S(1)}, s32[2160]{0:T(1024)}, u32[]{:S(2)}) copy-start(s32[2160]{0:T(1024)} %refs_1_.3) | copy-start | bytes 25924
  3.8 12.0 %copy-start.9 = (bf16[2160,128]{1,0:T(8,128)(2,1)}, bf16[2160,128]{1,0:T(8,128)(2,1)S(1)}, u32[]{:S(2)}) copy-start(bf16[2160,128]{1,0:T(8,128)(2,1)S(1)} %get-tuple-element.395.refs_5_) | copy-start | bytes 1658884
  3.8 21.1 %copy-start.2 = (bf16[2,2160,128]{2,1,0:T(8,128)(2,1)}, bf16[2,2160,128]{2,1,0:T(8,128)(2,1)S(1)}, u32[]{:S(2)}) copy-start(bf16[2,2160,128]{2,1,0:T(8,128)(2,1)S(1)} %get-tuple-element.393.refs_2_) | copy-start | bytes 3317764
  3.8 21.1 %copy-start.4 = (bf16[2,2160,128]{2,1,0:T(8,128)(2,1)}, bf16[2,2160,128]{2,1,0:T(8,128)(2,1)S(1)}, u32[]{:S(2)}) copy-start(bf16[2,2160,128]{2,1,0:T(8,128)(2,1)S(1)} %get-tuple-element.394.refs_3_) | copy-start | bytes 3317764
  3.8 2.9 %collective-permute-start.5 = (bf16[2,2160,128]{2,1,0:T(8,128)(2,1)S(1)}, bf16[2,2160,128]{2,1,0:T(8,128)(2,1)S(1)}, u32[]{:S(2)}, u32[]{:S(2)}) collective-permute-start(bf16[2,2160,128]{2,1,0:T(8,128)(2,1)S(1)} %get-tuple-element.394.refs_3_), channel_id=1, source_target_pairs={{0,1},{1,0},{2,3},{3,2},{4,5},{5,4},{6,7},{7,6},{8,9},{9,8},{10,11... | collective-permute-start | bytes 3317768 | tf_op jit(solution)/shard_map/ppermute | solution.py:485
  4.3 13.7 %collective-permute-start.4 = (bf16[2,2160,128]{2,1,0:T(8,128)(2,1)S(1)}, bf16[2,2160,128]{2,1,0:T(8,128)(2,1)}, u32[]{:S(2)}, u32[]{:S(2)}) collective-permute-start(bf16[2,2160,128]{2,1,0:T(8,128)(2,1)S(1)} %get-tuple-element.393.refs_2_), channel_id=1, source_target_pairs={{1,2},{3,4},{5,6},{7,8},{9,10},{11,12},{13,14},{2,1},{4,3},{6,5},{... | collective-permute-start | bytes 3317768 | tf_op jit(solution)/shard_map/ppermute | solution.py:485
  6.7 1.0 %copy-start.11 = (bf16[2,2160,128]{2,1,0:T(8,128)(2,1)}, bf16[2,2160,128]{2,1,0:T(8,128)(2,1)S(1)}, u32[]{:S(2)}) copy-start(bf16[2,2160,128]{2,1,0:T(8,128)(2,1)S(1)} %collective-permute-done.5.refs_4_) | copy-start | bytes 3317764
  15.8 18.2 %collective-permute-start.7 = (bf16[2,2160,128]{2,1,0:T(8,128)(2,1)}, bf16[2,2160,128]{2,1,0:T(8,128)(2,1)}, u32[]{:S(2)}, u32[]{:S(2)}) collective-permute-start(bf16[2,2160,128]{2,1,0:T(8,128)(2,1)} %get-tuple-element.390.refs_8_), channel_id=1, source_target_pairs={{0,1},{1,0},{2,3},{3,2},{4,5},{5,4},{6,7},{7,6},{8,9},{9,8},{10,11... | collective-permute-start | bytes 3317768 | tf_op jit(solution)/shard_map/ppermute | solution.py:485
  24.2 53.2 %collective-permute-start.6 = (bf16[2,2160,128]{2,1,0:T(8,128)(2,1)}, bf16[2,2160,128]{2,1,0:T(8,128)(2,1)S(1)}, u32[]{:S(2)}, u32[]{:S(2)}) collective-permute-start(bf16[2,2160,128]{2,1,0:T(8,128)(2,1)} %far.1.refs_7_), channel_id=1, source_target_pairs={{1,2},{3,4},{5,6},{7,8},{9,10},{11,12},{13,14},{2,1},{4,3},{6,5},{... | collective-permute-start | bytes 3317768 | tf_op jit(solution)/shard_map/ppermute | solution.py:485
  34.0 43.3 %copy-start = (bf16[2160,128]{1,0:T(8,128)(2,1)S(1)}, bf16[2160,128]{1,0:T(8,128)(2,1)}, u32[]{:S(2)}) copy-start(bf16[2160,128]{1,0:T(8,128)(2,1)} %get-tuple-element.156.refs_4_.refs_5_) | copy-start | bytes 1658884
  34.0 43.3 %copy-start.1 = (f32[2160,128]{1,0:T(8,128)S(1)}, f32[2160,128]{1,0:T(8,128)}, u32[]{:S(2)}) copy-start(f32[2160,128]{1,0:T(8,128)} %get-tuple-element.175.refs_10_) | copy-start | bytes 3317764
  34.0 20.7 %collective-permute-start = (f32[8,2,72,128]{3,2,1,0:T(8,128)}, f32[8,2,72,128]{3,2,1,0:T(8,128)S(1)}, u32[]{:S(2)}, u32[]{:S(2)}) collective-permute-start(f32[8,2,72,128]{3,2,1,0:T(8,128)} %get-tuple-element.400), channel_id=1, source_target_pairs={{0,1},{1,0},{2,3},{3,2},{4,5},{5,4},{6,7},{7,6},{8,9},{9,8},{10,11... | collective-permute-start | bytes 1769480 | tf_op jit(solution)/shard_map/while/body/ppermute | solution.py:485
  55.9 7.7 %collective-permute-start.1 = (bf16[2,4,72,128]{3,2,1,0:T(8,128)(2,1)S(1)}, bf16[2,4,72,128]{3,2,1,0:T(8,128)(2,1)S(1)}, u32[]{:S(2)}, u32[]{:S(2)}) collective-permute-start(bf16[2,4,72,128]{3,2,1,0:T(8,128)(2,1)S(1)} %get-tuple-element.357), channel_id=1, source_target_pairs={{0,4},{1,5},{2,6},{3,7},{4,0},{5,1},{6,2},{7,3},{8,12},{9,13},{10,... | collective-permute-start | bytes 442376 | tf_op jit(solution)/shard_map/while/body/ppermute | solution.py:559
  57.6 8.1 %copy-start.3 = (bf16[2,2160,128]{2,1,0:T(8,128)(2,1)S(1)}, bf16[2,2160,128]{2,1,0:T(8,128)(2,1)}, u32[]{:S(2)}) copy-start(bf16[2,2160,128]{2,1,0:T(8,128)(2,1)} %get-tuple-element.439.refs_6_.refs_5_) | copy-start | bytes 3317764 | tf_op jit(solution)/shard_map/while
  57.6 8.1 %copy-start.5 = (bf16[2,2160,128]{2,1,0:T(8,128)(2,1)S(1)}, bf16[2,2160,128]{2,1,0:T(8,128)(2,1)}, u32[]{:S(2)}) copy-start(bf16[2,2160,128]{2,1,0:T(8,128)(2,1)} %get-tuple-element.440.refs_7_.refs_6_) | copy-start | bytes 3317764 | tf_op jit(solution)/shard_map/while
  57.6 8.1 %copy-start.6 = (bf16[2,2160,128]{2,1,0:T(8,128)(2,1)S(1)}, bf16[2,2160,128]{2,1,0:T(8,128)(2,1)}, u32[]{:S(2)}) copy-start(bf16[2,2160,128]{2,1,0:T(8,128)(2,1)} %get-tuple-element.435.refs_2_.refs_1_) | copy-start | bytes 3317764 | tf_op jit(solution)/shard_map/while
  57.6 8.1 %copy-start.8 = (bf16[9,128,128]{2,1,0:T(8,128)(2,1)S(1)}, bf16[9,128,128]{2,1,0:T(8,128)(2,1)}, u32[]{:S(2)}) copy-start(bf16[9,128,128]{2,1,0:T(8,128)(2,1)} %get-tuple-element.442.refs_4_) | copy-start | bytes 884740 | tf_op jit(solution)/shard_map/while
  64.2 6.8 %collective-permute-start.2 = (bf16[1,4,72,128]{3,2,1,0:T(8,128)(2,1)S(1)}, bf16[1,4,72,128]{3,2,1,0:T(8,128)(2,1)S(1)}, u32[]{:S(2)}, u32[]{:S(2)}) collective-permute-start(bf16[1,4,72,128]{3,2,1,0:T(8,128)(2,1)S(1)} %get-tuple-element.363), channel_id=1, source_target_pairs={{0,8},{1,9},{2,10},{3,11},{4,12},{5,13},{6,14},{7,15},{8,0},{9,1},... | collective-permute-start | bytes 221192 | tf_op jit(solution)/shard_map/while/body/ppermute | solution.py:559
  72.1 4.6 %collective-permute-start.3 = (f32[1,2,72,128]{3,2,1,0:T(8,128)}, f32[1,2,72,128]{3,2,1,0:T(8,128)S(1)}, u32[]{:S(2)}, u32[]{:S(2)}) collective-permute-start(f32[1,2,72,128]{3,2,1,0:T(8,128)} %get-tuple-element.368), channel_id=1, source_target_pairs={{0,2},{1,3},{2,0},{3,1},{4,6},{5,7},{6,4},{7,5},{8,10},{9,11},{10,... | collective-permute-start | bytes 221192 | tf_op jit(solution)/shard_map/while/body/ppermute | solution.py:559

commit v4 on v3

--- a/solution.py
+++ b/solution.py
@@ -17,6 +17,7 @@
 MiB = 1 << 20
 OUT, INN = 0, 1
 FAR = 2
+BEYOND = 3
 ROW = 3 * C
 CONTRACT_LAST = (((1,), (1,)), ((), ()))
 CONTRACT_ROWS = (((0,), (0,)), ((), ()))
@@ -195,15 +196,15 @@
     return copies
 
 
-def forward_taps(taps, halo, row, copy, top):
+def forward_taps(taps, halo, row, copy, top, at=0):
     @pl.when(top == 0)
     def _():
-        put_taps(taps, 0, halo[...], False)
+        put_taps(taps, at, halo[...], False)
 
     @pl.when(top != 0)
     def _():
         copy.wait()
-        put_taps(taps, 0, row[...], False)
+        put_taps(taps, at, row[...], False)
 
 
 def adjoint_taps(utaps, at, halo, copy, top):
@@ -253,32 +254,30 @@
 ):
     parity, top = flags[0], flags[1]
     keep, give = outs
-    copies = top_copies(top, fold, row, spread, hutaps, sems)
+    copies = top_copies(top, fold, row, spread, utaps.at[:, pl.ds(BEYOND * ROW, ROW)], sems)
     for k, pair in enumerate((outer, inner, halo_in)):
         pair = pair.now()
         put_taps(taps, ROW * k, pair[0], False)
         put_taps(utaps, ROW * k, pair[1], True)
-    forward_taps(htaps, halo_s.now(), row, copies[0], top)
-    adjoint_taps(hutaps, 0, halo_g.now(), copies[1], top)
+    forward_taps(taps, halo_s.now(), row, copies[0], top, BEYOND * ROW)
+    adjoint_taps(utaps, BEYOND * ROW, halo_g.now(), copies[1], top)
     outer2, inner2 = outer2.now(), inner2.now()
     act = jnp.concatenate([outer2[0], inner2[0]], axis=1)
     dpre = jnp.concatenate([outer2[1], inner2[1]], axis=1)
     p = lax.dot_general(dpre, taps[...], CONTRACT_ROWS, preferred_element_type=F32)
-    q = lax.dot_general(outer2[1], htaps[...], CONTRACT_ROWS, preferred_element_type=F32)
     first, last = row_tap(0, parity), row_tap(2, parity)
 
     def block(x, r, k, b):
         return x[r * C : r * C + C, ROW * k + C * b : ROW * k + C * b + C]
 
     for b in range(3):
-        g1[3 * first + b] = block(p, INN, OUT, b) + block(q, 0, 0, b)
+        g1[3 * first + b] = block(p, INN, OUT, b) + block(p, OUT, BEYOND, b)
         g1[3 + b] = block(p, OUT, OUT, b) + block(p, INN, INN, b)
         g1[3 * last + b] = block(p, OUT, INN, b) + block(p, INN, FAR, b)
     p = lax.dot_general(act, utaps[...], CONTRACT_ROWS, preferred_element_type=F32)
-    q = lax.dot_general(outer2[0], hutaps[...], CONTRACT_ROWS, preferred_element_type=F32)
     is_top = jnp.full((C, C), top, jnp.int32) != 0
     for b in range(3):
-        edge = block(q, 0, 0, b)
+        edge = block(p, OUT, BEYOND, b)
         g2[3 * first + b] = (block(p, OUT, INN, b) + block(p, INN, FAR, b) + jnp.where(is_top, edge, 0.0)).T
         g2[3 + b] = (block(p, OUT, OUT, b) + block(p, INN, INN, b)).T
         g2[3 * last + b] = (block(p, INN, OUT, b) + jnp.where(is_top, 0.0, edge)).T
@@ -529,7 +528,7 @@
     halo_in2 = swap(inner2, lat, True)
     keep, give, spread2, own1, own2, *blank = call(
         weights_kernel, (flags, fold_partner), (outer, inner, halo_in, (halo, 0), (halo, 1), outer2, inner2), [part, part],
-        [pltpu.VMEM((9, C, C), F32)] * 2 + [pltpu.VMEM((n, 3 * ROW), BF16)] * 2
+        [pltpu.VMEM((9, C, C), F32)] * 2 + [pltpu.VMEM((n, 4 * ROW), BF16)] * 2
         + [pltpu.VMEM((n, ROW), BF16)] * 2 + [row_s, dma((2,)), wide_s, wide_s], 60, "wgrad",
         loose=(fold1, spread1, conv_first), loose_outs=[wide, own, own, row, wide, row, wide, row],
     )

time: 82.7 us -> 82.7 us (level)
  no operation moved by 1% of the time
where the time goes in v4:
time: 82.7 us; the launch traced here: 82.2 us
  Pallas kernels  45.8 us (55%)
  starting transfers between devices  29.3 us (35%)
  waiting for transfers between devices  4.26 us (5%)
  local copies, waits for them, and re-layouts  1.95 us (2%)
  between operations  0.92 us (1%)
    pallas_call x7, Pallas kernels, call(): pl.pallas_call(run, in_specs=[SMEM] * len(scalars) + [HBM] * (n_in + len(...  42.2 us
    ppermute x5, starting transfers between devices, swap(): return lax.ppermute(x, 'lat', pairs)  24.2 us
    ppermute x3, starting transfers between devices, body(): taken = lax.ppermute(go, 'lat', pairs)  5.11 us
    pallas_call x3, Pallas kernels, body(): pl.pallas_call(functools.partial(halve_kernel, 2 + stage), in_specs=[SMEM...  2.91 us
    ppermute x5, waiting for transfers between devices, swap(): return lax.ppermute(x, 'lat', pairs)  2.45 us
    ppermute x3, waiting for transfers between devices, body(): taken = lax.ppermute(go, 'lat', pairs)  1.8 us
  transfers between devices with their start and end apart: 8, of which 3 were waited for; matrix products, arithmetic and copies ran while one was open for 1% of the time, Pallas kernels for 46%

profile of v4, /device:TPU:0, one launch (start us, length us, event | category | flops | bytes accessed | tf_op | source)
XLA Modules:
  0.0 82.2 jit_solution(7356167769640152252)
XLA Ops:
  0.6 0.1 stack.27.refs_0_
  0.7 0.0 copy-start.7
  0.7 0.0 copy-start.10
  0.7 0.0 copy-start.12
  0.7 3.0 %start.1 = (bf16[2,2160,128]{2,1,0:T(8,128)(2,1)S(1)}, bf16[2,2160,128]{2,1,0:T(8,128)(2,1)S(1)}, bf16[2160,128]{1,0:T(8,128)(2,1)}, bf16[2160,128]{1,0:T(8,128)(2,1)S(1)}) custom-call(s32[5]{0:T(128)S(1)} %stack.27.refs_0_, bf16[2,2160,128]{2,1,0:T(8,128)(2,1)} %bitcast.41, bf16[2,2160,128]{2,1,0:T(8,128)(2,1)} %bitcast.42, s32[2,2160]{1,0:T(2,128)} %refs_3_.2), custom_call_target="tpu_custom_call" | custom-call | flops 1000 | bytes 1000 | tf_op jit(solution)/shard_map/start/pallas_call | solution.py:462
  3.8 0.0 copy-start.9
  3.8 0.0 copy-start.2
  3.8 0.0 copy-start.4
  3.8 0.5 collective-permute-start.5
  4.3 1.8 %collective-permute-start.4 = (bf16[2,2160,128]{2,1,0:T(8,128)(2,1)S(1)}, bf16[2,2160,128]{2,1,0:T(8,128)(2,1)}, u32[]{:S(2)}, u32[]{:S(2)}) collective-permute-start(bf16[2,2160,128]{2,1,0:T(8,128)(2,1)S(1)} %get-tuple-element.393.refs_2_), channel_id=1, source_target_pairs={{1,2},{3,4},{5,6},{7,8},{9,10},{11,12},{13,14},{2,1},{4,3},{6,5},{... | collective-permute-start | bytes 3317768 | tf_op jit(solution)/shard_map/ppermute | solution.py:484
  6.1 0.6 collective-permute-done.5.refs_4_
  6.7 0.0 copy-start.11
  6.7 1.0 %copy-done.11 = bf16[2,2160,128]{2,1,0:T(8,128)(2,1)} copy-done((bf16[2,2160,128]{2,1,0:T(8,128)(2,1)}, bf16[2,2160,128]{2,1,0:T(8,128)(2,1)S(1)}, u32[]{:S(2)}) %copy-start.11) | copy-done | bytes 1105944
  7.7 0.0 copy-done.7
  7.7 0.0 copy-done.10
  7.7 0.0 copy-done.12
  7.7 8.1 %first.1 = (bf16[2,2160,128]{2,1,0:T(8,128)(2,1)}, f32[2160,128]{1,0:T(8,128)}, f32[2160,128]{1,0:T(8,128)}, bf16[2160,128]{1,0:T(8,128)(2,1)}, bf16[2160,384]{1,0:T(8,128)(2,1)}) custom-call(s32[5]{0:T(128)S(1)} %stack.27.refs_0_, s32[2160]{0:T(1024)S(1)} %copy-done.12, bf16[2,2160,128]{2,1,0:T(8,128)(2,1)S(1)} %get-tuple-element.393.refs_2_, ...), custom_call_target="tpu_custom_call" | custom-call | flops 1000 | bytes 1000 | tf_op jit(solution)/shard_map/first/pallas_call | solution.py:462
  15.7 0.0 copy-done.9
  15.8 2.3 %collective-permute-start.7 = (bf16[2,2160,128]{2,1,0:T(8,128)(2,1)}, bf16[2,2160,128]{2,1,0:T(8,128)(2,1)}, u32[]{:S(2)}, u32[]{:S(2)}) collective-permute-start(bf16[2,2160,128]{2,1,0:T(8,128)(2,1)} %get-tuple-element.390.refs_8_), channel_id=1, source_target_pairs={{0,1},{1,0},{2,3},{3,2},{4,5},{5,4},{6,7},{7,6},{8,9},{9,8},{10,11... | collective-permute-start | bytes 3317768 | tf_op jit(solution)/shard_map/ppermute | solution.py:484
  18.0 0.0 collective-permute-done.4.refs_1_.refs_5_.refs_6_
  18.0 6.1 %far.1.refs_7_ = bf16[2,2160,128]{2,1,0:T(8,128)(2,1)} custom-call(s32[5]{0:T(128)S(1)} %stack.27.refs_0_, bf16[2,2160,128]{2,1,0:T(8,128)(2,1)} %collective-permute-done.4.refs_1_.refs_5_.refs_6_, bf16[9,128,128]{2,1,0:T(8,128)(2,1)S(1)} %copy-done.7, f32[2160,128]{1,0:T(8,128)} %get-tuple-element.155.refs_3_, ...), custom_call_target="tpu_custom_call" | custom-call | flops 1000 | bytes 1000 | tf_op jit(solution)/shard_map/far/pallas_call | solution.py:462
  24.2 0.7 collective-permute-start.6
  24.9 0.0 copy-done.2
  24.9 0.0 copy-done.4
  24.9 9.1 %wgrad.1 = (f32[8,2,72,128]{3,2,1,0:T(8,128)}, f32[8,2,72,128]{3,2,1,0:T(8,128)}, f32[2160,128]{1,0:T(8,128)}, f32[72,128]{1,0:T(8,128)}, f32[72,128]{1,0:T(8,12...) custom-call(s32[5]{0:T(128)S(1)} %stack.27.refs_0_, ...), custom_call_target="tpu_custom_call" | custom-call | flops 1000 | bytes 1000 | tf_op jit(solution)/shard_map/wgrad/pallas_call | solution.py:462
  34.0 0.0 collective-permute-done.7
  34.0 0.0 copy-start
  34.0 0.0 copy-start.1
  34.0 43.3 %while.24 = (s32[]{:T(128)}, f32[8,2,72,128]{3,2,1,0:T(8,128)}, f32[72,128]{1,0:T(8,128)}, f32[72,128]{1,0:T(8,128)}, bf16[2160,128]{1,0:T(8,128)(2,1)}, /*index...) while((s32[]{:T(128)}, f32[8,2,72,128]{3,2,1,0:T(8,128)}, ...), condition=%wide.region_1.0_spmd, body=%wide.region_0.0_spmd.sunk | while | flops 6008 | bytes 19175812 | solution.py:582
  34.1 18.9 %collective-permute-start = (f32[8,2,72,128]{3,2,1,0:T(8,128)}, f32[8,2,72,128]{3,2,1,0:T(8,128)S(1)}, u32[]{:S(2)}, u32[]{:S(2)}) collective-permute-start(f32[8,2,72,128]{3,2,1,0:T(8,128)} %get-tuple-element.400), channel_id=1, source_target_pairs={{0,1},{1,0},{2,3},{3,2},{4,5},{5,4},{6,7},{7,6},{8,9},{9,8},{10,11... | collective-permute-start | bytes 1769480 | tf_op jit(solution)/shard_map/while/body/ppermute | solution.py:484
  52.9 1.8 %collective-permute-done = f32[8,2,72,128]{3,2,1,0:T(8,128)S(1)} collective-permute-done((f32[8,2,72,128]{3,2,1,0:T(8,128)}, f32[8,2,72,128]{3,2,1,0:T(8,128)S(1)}, u32[]{:S(2)}, u32[]{:S(2)}) %collective-permute-start) | collective-permute-done | bytes 589856 | tf_op jit(solution)/shard_map/while/body/ppermute | solution.py:484
  54.8 1.1 %halve0.1 = (bf16[2,4,72,128]{3,2,1,0:T(8,128)(2,1)S(1)}, f32[2,4,72,128]{3,2,1,0:T(8,128)S(1)}) custom-call(s32[5]{0:T(128)S(1)} %broadcast_add_fusion.2.flags.refs_0_, f32[2,2,4,72,128]{4,3,2,1,0:T(8,128)} %bitcast.40, f32[2,2,4,72,128]{4,3,2,1,0:T(8,128)S(1)} %bitcast.33), custom_call_target="tpu_custom_call" | custom-call | flops 1000 | bytes 1000 | tf_op jit(solution)/shard_map/while/body/halve0/pallas_call | solution.py:551
  55.9 1.7 %collective-permute-start.1 = (bf16[2,4,72,128]{3,2,1,0:T(8,128)(2,1)S(1)}, bf16[2,4,72,128]{3,2,1,0:T(8,128)(2,1)S(1)}, u32[]{:S(2)}, u32[]{:S(2)}) collective-permute-start(bf16[2,4,72,128]{3,2,1,0:T(8,128)(2,1)S(1)} %get-tuple-element.357), channel_id=1, source_target_pairs={{0,4},{1,5},{2,6},{3,7},{4,0},{5,1},{6,2},{7,3},{8,12},{9,13},{10,... | collective-permute-start | bytes 442376 | tf_op jit(solution)/shard_map/while/body/ppermute | solution.py:558
  57.6 0.0 copy-start.3
  57.6 0.0 copy-start.5
  57.6 0.0 copy-start.6
  57.6 0.0 copy-start.8
  57.6 6.0 %second.1 = (bf16[2160,128]{1,0:T(8,128)(2,1)}, f32[2160,128]{1,0:T(8,128)}, bf16[2160,128]{1,0:T(8,128)(2,1)}) custom-call(s32[5]{0:T(128)S(1)} %broadcast_add_fusion.2.flags.refs_0_, s32[2160]{0:T(1024)S(1)} %get-tuple-element.434.refs_1_, bf16[2,2160,128]{2,1,0:T(8,128)(2,1)} %get-tuple-element.435.refs_2_.refs_1_, ...), custom_call_target="tpu_custom_call" | custom-call | flops 1000 | bytes 1000 | tf_op jit(solution)/shard_map/while/body/second/pallas_call | solution.py:462
  63.6 0.0 collective-permute-done.1
  63.6 0.6 halve1.1
  64.2 1.5 %collective-permute-start.2 = (bf16[1,4,72,128]{3,2,1,0:T(8,128)(2,1)S(1)}, bf16[1,4,72,128]{3,2,1,0:T(8,128)(2,1)S(1)}, u32[]{:S(2)}, u32[]{:S(2)}) collective-permute-start(bf16[1,4,72,128]{3,2,1,0:T(8,128)(2,1)S(1)} %get-tuple-element.363), channel_id=1, source_target_pairs={{0,8},{1,9},{2,10},{3,11},{4,12},{5,13},{6,14},{7,15},{8,0},{9,1},... | collective-permute-start | bytes 221192 | tf_op jit(solution)/shard_map/while/body/ppermute | solution.py:558
  65.7 0.0 copy-done.3
  65.7 0.0 copy-done.5
  65.7 0.0 copy-done.6
  65.7 0.0 copy-done.8
  65.7 5.2 %second_adjoint.1 = (bf16[2160,128]{1,0:T(8,128)(2,1)}, f32[2160,128]{1,0:T(8,128)}) custom-call(s32[5]{0:T(128)S(1)} %broadcast_add_fusion.2.flags.refs_0_, bf16[2,2160,128]{2,1,0:T(8,128)(2,1)S(1)} %copy-done.6, bf16[2,2160,128]{2,1,0:T(8,128)(2,1)} %get-tuple-element.436.refs_3_.refs_2_, bf16[2,2160,128]{2,1,0:T(8,128)(2,1)} %get-tuple-element.437.refs_4_.refs_3_, ...), custom_call_target="tpu_custom_call" | custom-call | flops 1000 | bytes 1000 | tf_op jit(solution)/shard_map/while/body/second_adjoint/pallas_call | solution.py:462
  70.9 0.0 collective-permute-done.2
  71.0 1.2 %halve2.1 = (f32[1,2,72,128]{3,2,1,0:T(8,128)}, f32[1,2,72,128]{3,2,1,0:T(8,128)S(1)}) custom-call(s32[5]{0:T(128)S(1)} %broadcast_add_fusion.2.flags.refs_0_, f32[1,2,2,72,128]{4,3,2,1,0:T(8,128)S(1)} %bitcast.35, bf16[1,2,2,72,128]{4,3,2,1,0:T(8,128)(2,1)S(1)} %bitcast.37), custom_call_target="tpu_custom_call" | custom-call | flops 1000 | bytes 1000 | tf_op jit(solution)/shard_map/while/body/halve2/pallas_call | solution.py:551
  72.1 1.9 %collective-permute-start.3 = (f32[1,2,72,128]{3,2,1,0:T(8,128)}, f32[1,2,72,128]{3,2,1,0:T(8,128)S(1)}, u32[]{:S(2)}, u32[]{:S(2)}) collective-permute-start(f32[1,2,72,128]{3,2,1,0:T(8,128)} %get-tuple-element.368), channel_id=1, source_target_pairs={{0,2},{1,3},{2,0},{3,1},{4,6},{5,7},{6,4},{7,5},{8,10},{9,11},{10,... | collective-permute-start | bytes 221192 | tf_op jit(solution)/shard_map/while/body/ppermute | solution.py:558
  74.1 0.8 %copy.29 = f32[8,2,72,128]{3,2,1,0:T(8,128)} copy(f32[8,2,72,128]{3,2,1,0:T(8,128)S(1)} %collective-permute-done) | data formatting | bytes 1179648 | tf_op jit(solution)/shard_map/while
  74.9 1.8 %collective-permute-done.3 = f32[1,2,72,128]{3,2,1,0:T(8,128)S(1)} collective-permute-done((f32[1,2,72,128]{3,2,1,0:T(8,128)}, f32[1,2,72,128]{3,2,1,0:T(8,128)S(1)}, u32[]{:S(2)}, u32[]{:S(2)}) %collective-permute-start.3) | collective-permute-done | bytes 73760 | tf_op jit(solution)/shard_map/while/body/ppermute | solution.py:558
  76.7 0.6 total.1
  77.3 0.0 collective-permute-done.6.refs_1_
  77.4 0.0 copy-done
  77.4 0.0 copy-done.1
  77.4 4.7 %last.1 = (bf16[2,2160,128]{2,1,0:T(8,128)(2,1)}, bf16[2,2160,128]{2,1,0:T(8,128)(2,1)}) custom-call(s32[5]{0:T(128)S(1)} %get-tuple-element.458, bf16[2,2160,128]{2,1,0:T(8,128)(2,1)S(1)} %collective-permute-done.6.refs_1_, bf16[9,128,128]{2,1,0:T(8,128)(2,1)} %get-tuple-element.456, bf16[9,128,128]{2,1,0:T(8,128)(2,1)} %get-tuple-element.455, ...), custom_call_target="tpu_custom_call" | custom-call | flops 1000 | bytes 1000 | tf_op jit(solution)/shard_map/last/pallas_call | solution.py:462
  (1 shorter events, 0.0 us)
Async XLA Ops:
  0.7 6.9 %copy-start.7 = (bf16[9,128,128]{2,1,0:T(8,128)(2,1)S(1)}, bf16[9,128,128]{2,1,0:T(8,128)(2,1)}, u32[]{:S(2)}) copy-start(bf16[9,128,128]{2,1,0:T(8,128)(2,1)} %refs_3_.3) | copy-start | bytes 884740
  0.7 7.0 %copy-start.10 = (bf16[9,128,128]{2,1,0:T(8,128)(2,1)S(1)}, bf16[9,128,128]{2,1,0:T(8,128)(2,1)}, u32[]{:S(2)}) copy-start(bf16[9,128,128]{2,1,0:T(8,128)(2,1)} %refs_2_.3) | copy-start | bytes 884740
  0.7 7.0 %copy-start.12 = (s32[2160]{0:T(1024)S(1)}, s32[2160]{0:T(1024)}, u32[]{:S(2)}) copy-start(s32[2160]{0:T(1024)} %refs_1_.3) | copy-start | bytes 25924
  3.8 12.0 %copy-start.9 = (bf16[2160,128]{1,0:T(8,128)(2,1)}, bf16[2160,128]{1,0:T(8,128)(2,1)S(1)}, u32[]{:S(2)}) copy-start(bf16[2160,128]{1,0:T(8,128)(2,1)S(1)} %get-tuple-element.395.refs_5_) | copy-start | bytes 1658884
  3.8 21.1 %copy-start.2 = (bf16[2,2160,128]{2,1,0:T(8,128)(2,1)}, bf16[2,2160,128]{2,1,0:T(8,128)(2,1)S(1)}, u32[]{:S(2)}) copy-start(bf16[2,2160,128]{2,1,0:T(8,128)(2,1)S(1)} %get-tuple-element.393.refs_2_) | copy-start | bytes 3317764
  3.8 21.1 %copy-start.4 = (bf16[2,2160,128]{2,1,0:T(8,128)(2,1)}, bf16[2,2160,128]{2,1,0:T(8,128)(2,1)S(1)}, u32[]{:S(2)}) copy-start(bf16[2,2160,128]{2,1,0:T(8,128)(2,1)S(1)} %get-tuple-element.394.refs_3_) | copy-start | bytes 3317764
  3.8 2.9 %collective-permute-start.5 = (bf16[2,2160,128]{2,1,0:T(8,128)(2,1)S(1)}, bf16[2,2160,128]{2,1,0:T(8,128)(2,1)S(1)}, u32[]{:S(2)}, u32[]{:S(2)}) collective-permute-start(bf16[2,2160,128]{2,1,0:T(8,128)(2,1)S(1)} %get-tuple-element.394.refs_3_), channel_id=1, source_target_pairs={{0,1},{1,0},{2,3},{3,2},{4,5},{5,4},{6,7},{7,6},{8,9},{9,8},{10,11... | collective-permute-start | bytes 3317768 | tf_op jit(solution)/shard_map/ppermute | solution.py:484
  4.3 13.7 %collective-permute-start.4 = (bf16[2,2160,128]{2,1,0:T(8,128)(2,1)S(1)}, bf16[2,2160,128]{2,1,0:T(8,128)(2,1)}, u32[]{:S(2)}, u32[]{:S(2)}) collective-permute-start(bf16[2,2160,128]{2,1,0:T(8,128)(2,1)S(1)} %get-tuple-element.393.refs_2_), channel_id=1, source_target_pairs={{1,2},{3,4},{5,6},{7,8},{9,10},{11,12},{13,14},{2,1},{4,3},{6,5},{... | collective-permute-start | bytes 3317768 | tf_op jit(solution)/shard_map/ppermute | solution.py:484
  6.7 1.0 %copy-start.11 = (bf16[2,2160,128]{2,1,0:T(8,128)(2,1)}, bf16[2,2160,128]{2,1,0:T(8,128)(2,1)S(1)}, u32[]{:S(2)}) copy-start(bf16[2,2160,128]{2,1,0:T(8,128)(2,1)S(1)} %collective-permute-done.5.refs_4_) | copy-start | bytes 3317764
  15.8 18.3 %collective-permute-start.7 = (bf16[2,2160,128]{2,1,0:T(8,128)(2,1)}, bf16[2,2160,128]{2,1,0:T(8,128)(2,1)}, u32[]{:S(2)}, u32[]{:S(2)}) collective-permute-start(bf16[2,2160,128]{2,1,0:T(8,128)(2,1)} %get-tuple-element.390.refs_8_), channel_id=1, source_target_pairs={{0,1},{1,0},{2,3},{3,2},{4,5},{5,4},{6,7},{7,6},{8,9},{9,8},{10,11... | collective-permute-start | bytes 3317768 | tf_op jit(solution)/shard_map/ppermute | solution.py:484
  24.2 53.2 %collective-permute-start.6 = (bf16[2,2160,128]{2,1,0:T(8,128)(2,1)}, bf16[2,2160,128]{2,1,0:T(8,128)(2,1)S(1)}, u32[]{:S(2)}, u32[]{:S(2)}) collective-permute-start(bf16[2,2160,128]{2,1,0:T(8,128)(2,1)} %far.1.refs_7_), channel_id=1, source_target_pairs={{1,2},{3,4},{5,6},{7,8},{9,10},{11,12},{13,14},{2,1},{4,3},{6,5},{... | collective-permute-start | bytes 3317768 | tf_op jit(solution)/shard_map/ppermute | solution.py:484
  34.0 43.3 %copy-start = (bf16[2160,128]{1,0:T(8,128)(2,1)S(1)}, bf16[2160,128]{1,0:T(8,128)(2,1)}, u32[]{:S(2)}) copy-start(bf16[2160,128]{1,0:T(8,128)(2,1)} %get-tuple-element.156.refs_4_.refs_5_) | copy-start | bytes 1658884
  34.0 43.3 %copy-start.1 = (f32[2160,128]{1,0:T(8,128)S(1)}, f32[2160,128]{1,0:T(8,128)}, u32[]{:S(2)}) copy-start(f32[2160,128]{1,0:T(8,128)} %get-tuple-element.175.refs_10_) | copy-start | bytes 3317764
  34.1 20.7 %collective-permute-start = (f32[8,2,72,128]{3,2,1,0:T(8,128)}, f32[8,2,72,128]{3,2,1,0:T(8,128)S(1)}, u32[]{:S(2)}, u32[]{:S(2)}) collective-permute-start(f32[8,2,72,128]{3,2,1,0:T(8,128)} %get-tuple-element.400), channel_id=1, source_target_pairs={{0,1},{1,0},{2,3},{3,2},{4,5},{5,4},{6,7},{7,6},{8,9},{9,8},{10,11... | collective-permute-start | bytes 1769480 | tf_op jit(solution)/shard_map/while/body/ppermute | solution.py:484
  55.9 7.7 %collective-permute-start.1 = (bf16[2,4,72,128]{3,2,1,0:T(8,128)(2,1)S(1)}, bf16[2,4,72,128]{3,2,1,0:T(8,128)(2,1)S(1)}, u32[]{:S(2)}, u32[]{:S(2)}) collective-permute-start(bf16[2,4,72,128]{3,2,1,0:T(8,128)(2,1)S(1)} %get-tuple-element.357), channel_id=1, source_target_pairs={{0,4},{1,5},{2,6},{3,7},{4,0},{5,1},{6,2},{7,3},{8,12},{9,13},{10,... | collective-permute-start | bytes 442376 | tf_op jit(solution)/shard_map/while/body/ppermute | solution.py:558
  57.6 8.1 %copy-start.3 = (bf16[2,2160,128]{2,1,0:T(8,128)(2,1)S(1)}, bf16[2,2160,128]{2,1,0:T(8,128)(2,1)}, u32[]{:S(2)}) copy-start(bf16[2,2160,128]{2,1,0:T(8,128)(2,1)} %get-tuple-element.439.refs_6_.refs_5_) | copy-start | bytes 3317764 | tf_op jit(solution)/shard_map/while
  57.6 8.1 %copy-start.5 = (bf16[2,2160,128]{2,1,0:T(8,128)(2,1)S(1)}, bf16[2,2160,128]{2,1,0:T(8,128)(2,1)}, u32[]{:S(2)}) copy-start(bf16[2,2160,128]{2,1,0:T(8,128)(2,1)} %get-tuple-element.440.refs_7_.refs_6_) | copy-start | bytes 3317764 | tf_op jit(solution)/shard_map/while
  57.6 8.1 %copy-start.6 = (bf16[2,2160,128]{2,1,0:T(8,128)(2,1)S(1)}, bf16[2,2160,128]{2,1,0:T(8,128)(2,1)}, u32[]{:S(2)}) copy-start(bf16[2,2160,128]{2,1,0:T(8,128)(2,1)} %get-tuple-element.435.refs_2_.refs_1_) | copy-start | bytes 3317764 | tf_op jit(solution)/shard_map/while
  57.6 8.1 %copy-start.8 = (bf16[9,128,128]{2,1,0:T(8,128)(2,1)S(1)}, bf16[9,128,128]{2,1,0:T(8,128)(2,1)}, u32[]{:S(2)}) copy-start(bf16[9,128,128]{2,1,0:T(8,128)(2,1)} %get-tuple-element.442.refs_4_) | copy-start | bytes 884740 | tf_op jit(solution)/shard_map/while
  64.2 6.8 %collective-permute-start.2 = (bf16[1,4,72,128]{3,2,1,0:T(8,128)(2,1)S(1)}, bf16[1,4,72,128]{3,2,1,0:T(8,128)(2,1)S(1)}, u32[]{:S(2)}, u32[]{:S(2)}) collective-permute-start(bf16[1,4,72,128]{3,2,1,0:T(8,128)(2,1)S(1)} %get-tuple-element.363), channel_id=1, source_target_pairs={{0,8},{1,9},{2,10},{3,11},{4,12},{5,13},{6,14},{7,15},{8,0},{9,1},... | collective-permute-start | bytes 221192 | tf_op jit(solution)/shard_map/while/body/ppermute | solution.py:558
  72.1 4.6 %collective-permute-start.3 = (f32[1,2,72,128]{3,2,1,0:T(8,128)}, f32[1,2,72,128]{3,2,1,0:T(8,128)S(1)}, u32[]{:S(2)}, u32[]{:S(2)}) collective-permute-start(f32[1,2,72,128]{3,2,1,0:T(8,128)} %get-tuple-element.368), channel_id=1, source_target_pairs={{0,2},{1,3},{2,0},{3,1},{4,6},{5,7},{6,4},{7,5},{8,10},{9,11},{10,... | collective-permute-start | bytes 221192 | tf_op jit(solution)/shard_map/while/body/ppermute | solution.py:558

commit v5 on v3

--- a/solution.py
+++ b/solution.py
@@ -166,14 +166,14 @@
         wide[:, 2 * C :] = pltpu.roll(u, 1, 0)
 
         def step(i, carry):
-            for k in range(8):
-                j = i * 8 + k
+            for k in range(16):
+                j = i * 16 + k
                 at = partner[j]
                 dst[pl.ds(j, 1), :] = src[pl.ds(at, 1), :]
                 wide_dst[pl.ds(at, 1), :] = wide[pl.ds(j, 1), :]
             return carry
 
-        lax.fori_loop(0, n // 8, step, 0)
+        lax.fori_loop(0, n // 16, step, 0)
         row[...] = dst[...].astype(BF16)
         pltpu.sync_copy(row, fold)
         for b in range(3):
@@ -376,7 +376,7 @@
 
 
 def last_kernel(
-    flags, halo, w2, w1, upd_o, mask_o, grad_o, upd_i, grad_i, fold, spread, updated, grad,
+    flags, halo, w2, upd_o, mask_o, uhalo, w1, grad_o, upd_i, grad_i, fold, spread, updated, grad,
     taps, utaps, y, d, row, top_sems, out_u, out_g, sems
 ):
     parity, top = flags[0], flags[1]
@@ -389,10 +389,10 @@
         sent.append(copy)
 
     copies = top_copies(top, fold, row, spread, d, top_sems)
-    forward_taps(taps, halo.at[0], row, copies[0], top)
+    forward_taps(taps, halo, row, copies[0], top)
     kernel = jnp.concatenate([w2[3 * row_tap(0, parity) + b] for b in range(3)], axis=1)
     y[...] = lax.dot_general(taps[...], kernel, CONTRACT_LAST, preferred_element_type=F32)
-    w1, upd_o, mask_o = w1.now(), upd_o.now(), mask_o.now()
+    upd_o, mask_o = upd_o.now(), mask_o.now()
 
     def step(rows):
         out_u[rows, :] = (mask_o[rows, :].astype(F32) * (upd_o[rows, :] + y[rows, :])).astype(BF16)
@@ -401,10 +401,11 @@
     send(out_u, updated.at[parity])
     send(upd_i.now(), updated.at[1 - parity])
     send(grad_i.now(), grad.at[1 - parity])
+    uhalo, w1 = uhalo.now(), w1.now()
 
     @pl.when(top == 0)
     def _():
-        put_taps(utaps, 0, halo[1], True)
+        put_taps(utaps, 0, uhalo[...], True)
         kernel = jnp.concatenate([w1[3 * row_tap(2, parity) + b] for b in range(3)], axis=0)
         d[...] = jnp.dot(utaps[...], kernel, preferred_element_type=F32)
 
@@ -584,7 +585,7 @@
     fold2 = near[2], spread2
     (upd_i, upd_o), (grad_i, grad_o) = near[:2], near_a[:2]
     updated, grad = call(
-        last_kernel, (flags,), (halo2, conv_second, conv_first, upd_o, mask_o, grad_o, upd_i, grad_i), [],
+        last_kernel, (flags,), ((halo2, 0), conv_second, upd_o, mask_o, (halo2, 1), conv_first, grad_o, upd_i, grad_i), [],
         [pltpu.VMEM((n, ROW), BF16)] * 2 + [wide_s] * 2 + [row_s, dma((2,)), row_s, row_s, dma((4,))], 28, "last", loose=tuple(fold2), loose_outs=[pair, pair],
     )
     return (updated.transpose(2, 0, 1), grad.transpose(2, 0, 1), g1, g2)

time: 82.7 us -> 82.7 us (level)
  no operation moved by 1% of the time
where the time goes in v5:
time: 82.7 us; the launch traced here: 82.2 us
  Pallas kernels  45.7 us (55%)
  starting transfers between devices  29.3 us (35%)
  waiting for transfers between devices  4.25 us (5%)
  local copies, waits for them, and re-layouts  1.95 us (2%)
  between operations  0.92 us (1%)
    pallas_call x7, Pallas kernels, call(): pl.pallas_call(run, in_specs=[SMEM] * len(scalars) + [HBM] * (n_in + len(...  42.2 us
    ppermute x5, starting transfers between devices, swap(): return lax.ppermute(x, 'lat', pairs)  24.2 us
    ppermute x3, starting transfers between devices, body(): taken = lax.ppermute(go, 'lat', pairs)  5.11 us
    pallas_call x3, Pallas kernels, body(): pl.pallas_call(functools.partial(halve_kernel, 2 + stage), in_specs=[SMEM...  2.91 us
    ppermute x5, waiting for transfers between devices, swap(): return lax.ppermute(x, 'lat', pairs)  2.45 us
    ppermute x3, waiting for transfers between devices, body(): taken = lax.ppermute(go, 'lat', pairs)  1.8 us
  transfers between devices with their start and end apart: 8, of which 3 were waited for; matrix products, arithmetic and copies ran while one was open for 1% of the time, Pallas kernels for 46%

profile of v5, /device:TPU:0, one launch (start us, length us, event | category | flops | bytes accessed | tf_op | source)
XLA Modules:
  0.0 82.2 jit_solution(5088963901325730765)
XLA Ops:
  0.6 0.1 stack.27.refs_0_
  0.7 0.0 copy-start.7
  0.7 0.0 copy-start.10
  0.7 0.0 copy-start.12
  0.7 3.0 %start.1 = (bf16[2,2160,128]{2,1,0:T(8,128)(2,1)S(1)}, bf16[2,2160,128]{2,1,0:T(8,128)(2,1)S(1)}, bf16[2160,128]{1,0:T(8,128)(2,1)}, bf16[2160,128]{1,0:T(8,128)(2,1)S(1)}) custom-call(s32[5]{0:T(128)S(1)} %stack.27.refs_0_, bf16[2,2160,128]{2,1,0:T(8,128)(2,1)} %bitcast.41, bf16[2,2160,128]{2,1,0:T(8,128)(2,1)} %bitcast.42, s32[2,2160]{1,0:T(2,128)} %refs_3_.1), custom_call_target="tpu_custom_call" | custom-call | flops 1000 | bytes 1000 | tf_op jit(solution)/shard_map/start/pallas_call | solution.py:464
  3.8 0.0 copy-start.9
  3.8 0.0 copy-start.2
  3.8 0.0 copy-start.4
  3.8 0.5 collective-permute-start.5
  4.3 1.8 %collective-permute-start.4 = (bf16[2,2160,128]{2,1,0:T(8,128)(2,1)S(1)}, bf16[2,2160,128]{2,1,0:T(8,128)(2,1)}, u32[]{:S(2)}, u32[]{:S(2)}) collective-permute-start(bf16[2,2160,128]{2,1,0:T(8,128)(2,1)S(1)} %get-tuple-element.393.refs_2_), channel_id=1, source_target_pairs={{1,2},{3,4},{5,6},{7,8},{9,10},{11,12},{13,14},{2,1},{4,3},{6,5},{... | collective-permute-start | bytes 3317768 | tf_op jit(solution)/shard_map/ppermute | solution.py:486
  6.1 0.6 collective-permute-done.5.refs_4_
  6.7 0.0 copy-start.11
  6.7 1.0 %copy-done.11 = bf16[2,2160,128]{2,1,0:T(8,128)(2,1)} copy-done((bf16[2,2160,128]{2,1,0:T(8,128)(2,1)}, bf16[2,2160,128]{2,1,0:T(8,128)(2,1)S(1)}, u32[]{:S(2)}) %copy-start.11) | copy-done | bytes 1105944
  7.7 0.0 copy-done.7
  7.7 0.0 copy-done.10
  7.7 0.0 copy-done.12
  7.7 8.1 %first.1 = (bf16[2,2160,128]{2,1,0:T(8,128)(2,1)}, f32[2160,128]{1,0:T(8,128)}, f32[2160,128]{1,0:T(8,128)}, bf16[2160,128]{1,0:T(8,128)(2,1)}, bf16[2160,384]{1,0:T(8,128)(2,1)}) custom-call(s32[5]{0:T(128)S(1)} %stack.27.refs_0_, s32[2160]{0:T(1024)S(1)} %copy-done.12, bf16[2,2160,128]{2,1,0:T(8,128)(2,1)S(1)} %get-tuple-element.393.refs_2_, ...), custom_call_target="tpu_custom_call" | custom-call | flops 1000 | bytes 1000 | tf_op jit(solution)/shard_map/first/pallas_call | solution.py:464
  15.7 0.0 copy-done.9
  15.8 2.3 %collective-permute-start.7 = (bf16[2,2160,128]{2,1,0:T(8,128)(2,1)}, bf16[2,2160,128]{2,1,0:T(8,128)(2,1)}, u32[]{:S(2)}, u32[]{:S(2)}) collective-permute-start(bf16[2,2160,128]{2,1,0:T(8,128)(2,1)} %get-tuple-element.390.refs_8_), channel_id=1, source_target_pairs={{0,1},{1,0},{2,3},{3,2},{4,5},{5,4},{6,7},{7,6},{8,9},{9,8},{10,11... | collective-permute-start | bytes 3317768 | tf_op jit(solution)/shard_map/ppermute | solution.py:486
  18.0 0.0 collective-permute-done.4.refs_1_.refs_5_.refs_6_
  18.0 6.1 %far.1.refs_7_ = bf16[2,2160,128]{2,1,0:T(8,128)(2,1)} custom-call(s32[5]{0:T(128)S(1)} %stack.27.refs_0_, bf16[2,2160,128]{2,1,0:T(8,128)(2,1)} %collective-permute-done.4.refs_1_.refs_5_.refs_6_, bf16[9,128,128]{2,1,0:T(8,128)(2,1)S(1)} %copy-done.7, f32[2160,128]{1,0:T(8,128)} %get-tuple-element.155.refs_3_, ...), custom_call_target="tpu_custom_call" | custom-call | flops 1000 | bytes 1000 | tf_op jit(solution)/shard_map/far/pallas_call | solution.py:464
  24.2 0.7 collective-permute-start.6
  24.9 0.0 copy-done.2
  24.9 0.0 copy-done.4
  24.9 9.1 %wgrad.1 = (f32[8,2,72,128]{3,2,1,0:T(8,128)}, f32[8,2,72,128]{3,2,1,0:T(8,128)}, f32[2160,128]{1,0:T(8,128)}, f32[72,128]{1,0:T(8,128)}, f32[72,128]{1,0:T(8,12...) custom-call(s32[5]{0:T(128)S(1)} %stack.27.refs_0_, ...), custom_call_target="tpu_custom_call" | custom-call | flops 1000 | bytes 1000 | tf_op jit(solution)/shard_map/wgrad/pallas_call | solution.py:464
  34.0 0.0 collective-permute-done.7
  34.0 0.0 copy-start
  34.0 0.0 copy-start.1
  34.0 43.3 %while.24 = (s32[]{:T(128)}, f32[8,2,72,128]{3,2,1,0:T(8,128)}, f32[72,128]{1,0:T(8,128)}, f32[72,128]{1,0:T(8,128)}, bf16[2160,128]{1,0:T(8,128)(2,1)}, /*index...) while((s32[]{:T(128)}, f32[8,2,72,128]{3,2,1,0:T(8,128)}, ...), condition=%wide.region_1.0_spmd, body=%wide.region_0.0_spmd.sunk | while | flops 6008 | bytes 19175812 | solution.py:584
  34.0 18.9 %collective-permute-start = (f32[8,2,72,128]{3,2,1,0:T(8,128)}, f32[8,2,72,128]{3,2,1,0:T(8,128)S(1)}, u32[]{:S(2)}, u32[]{:S(2)}) collective-permute-start(f32[8,2,72,128]{3,2,1,0:T(8,128)} %get-tuple-element.400), channel_id=1, source_target_pairs={{0,1},{1,0},{2,3},{3,2},{4,5},{5,4},{6,7},{7,6},{8,9},{9,8},{10,11... | collective-permute-start | bytes 1769480 | tf_op jit(solution)/shard_map/while/body/ppermute | solution.py:486
  52.9 1.8 %collective-permute-done = f32[8,2,72,128]{3,2,1,0:T(8,128)S(1)} collective-permute-done((f32[8,2,72,128]{3,2,1,0:T(8,128)}, f32[8,2,72,128]{3,2,1,0:T(8,128)S(1)}, u32[]{:S(2)}, u32[]{:S(2)}) %collective-permute-start) | collective-permute-done | bytes 589856 | tf_op jit(solution)/shard_map/while/body/ppermute | solution.py:486
  54.8 1.1 %halve0.1 = (bf16[2,4,72,128]{3,2,1,0:T(8,128)(2,1)S(1)}, f32[2,4,72,128]{3,2,1,0:T(8,128)S(1)}) custom-call(s32[5]{0:T(128)S(1)} %broadcast_add_fusion.2.flags.refs_0_, f32[2,2,4,72,128]{4,3,2,1,0:T(8,128)} %bitcast.40, f32[2,2,4,72,128]{4,3,2,1,0:T(8,128)S(1)} %bitcast.33), custom_call_target="tpu_custom_call" | custom-call | flops 1000 | bytes 1000 | tf_op jit(solution)/shard_map/while/body/halve0/pallas_call | solution.py:553
  55.9 1.7 %collective-permute-start.1 = (bf16[2,4,72,128]{3,2,1,0:T(8,128)(2,1)S(1)}, bf16[2,4,72,128]{3,2,1,0:T(8,128)(2,1)S(1)}, u32[]{:S(2)}, u32[]{:S(2)}) collective-permute-start(bf16[2,4,72,128]{3,2,1,0:T(8,128)(2,1)S(1)} %get-tuple-element.357), channel_id=1, source_target_pairs={{0,4},{1,5},{2,6},{3,7},{4,0},{5,1},{6,2},{7,3},{8,12},{9,13},{10,... | collective-permute-start | bytes 442376 | tf_op jit(solution)/shard_map/while/body/ppermute | solution.py:560
  57.6 0.0 copy-start.3
  57.6 0.0 copy-start.5
  57.6 0.0 copy-start.6
  57.6 0.0 copy-start.8
  57.6 6.0 %second.1 = (bf16[2160,128]{1,0:T(8,128)(2,1)}, f32[2160,128]{1,0:T(8,128)}, bf16[2160,128]{1,0:T(8,128)(2,1)}) custom-call(s32[5]{0:T(128)S(1)} %broadcast_add_fusion.2.flags.refs_0_, s32[2160]{0:T(1024)S(1)} %get-tuple-element.434.refs_1_, bf16[2,2160,128]{2,1,0:T(8,128)(2,1)} %get-tuple-element.435.refs_2_.refs_1_, ...), custom_call_target="tpu_custom_call" | custom-call | flops 1000 | bytes 1000 | tf_op jit(solution)/shard_map/while/body/second/pallas_call | solution.py:464
  63.6 0.0 collective-permute-done.1
  63.6 0.6 halve1.1
  64.2 1.5 %collective-permute-start.2 = (bf16[1,4,72,128]{3,2,1,0:T(8,128)(2,1)S(1)}, bf16[1,4,72,128]{3,2,1,0:T(8,128)(2,1)S(1)}, u32[]{:S(2)}, u32[]{:S(2)}) collective-permute-start(bf16[1,4,72,128]{3,2,1,0:T(8,128)(2,1)S(1)} %get-tuple-element.363), channel_id=1, source_target_pairs={{0,8},{1,9},{2,10},{3,11},{4,12},{5,13},{6,14},{7,15},{8,0},{9,1},... | collective-permute-start | bytes 221192 | tf_op jit(solution)/shard_map/while/body/ppermute | solution.py:560
  65.7 0.0 copy-done.3
  65.7 0.0 copy-done.5
  65.7 0.0 copy-done.6
  65.7 0.0 copy-done.8
  65.7 5.2 %second_adjoint.1 = (bf16[2160,128]{1,0:T(8,128)(2,1)}, f32[2160,128]{1,0:T(8,128)}) custom-call(s32[5]{0:T(128)S(1)} %broadcast_add_fusion.2.flags.refs_0_, bf16[2,2160,128]{2,1,0:T(8,128)(2,1)S(1)} %copy-done.6, bf16[2,2160,128]{2,1,0:T(8,128)(2,1)} %get-tuple-element.436.refs_3_.refs_2_, bf16[2,2160,128]{2,1,0:T(8,128)(2,1)} %get-tuple-element.437.refs_4_.refs_3_, ...), custom_call_target="tpu_custom_call" | custom-call | flops 1000 | bytes 1000 | tf_op jit(solution)/shard_map/while/body/second_adjoint/pallas_call | solution.py:464
  70.9 0.0 collective-permute-done.2
  70.9 1.2 %halve2.1 = (f32[1,2,72,128]{3,2,1,0:T(8,128)}, f32[1,2,72,128]{3,2,1,0:T(8,128)S(1)}) custom-call(s32[5]{0:T(128)S(1)} %broadcast_add_fusion.2.flags.refs_0_, f32[1,2,2,72,128]{4,3,2,1,0:T(8,128)S(1)} %bitcast.35, bf16[1,2,2,72,128]{4,3,2,1,0:T(8,128)(2,1)S(1)} %bitcast.37), custom_call_target="tpu_custom_call" | custom-call | flops 1000 | bytes 1000 | tf_op jit(solution)/shard_map/while/body/halve2/pallas_call | solution.py:553
  72.1 1.9 %collective-permute-start.3 = (f32[1,2,72,128]{3,2,1,0:T(8,128)}, f32[1,2,72,128]{3,2,1,0:T(8,128)S(1)}, u32[]{:S(2)}, u32[]{:S(2)}) collective-permute-start(f32[1,2,72,128]{3,2,1,0:T(8,128)} %get-tuple-element.368), channel_id=1, source_target_pairs={{0,2},{1,3},{2,0},{3,1},{4,6},{5,7},{6,4},{7,5},{8,10},{9,11},{10,... | collective-permute-start | bytes 221192 | tf_op jit(solution)/shard_map/while/body/ppermute | solution.py:560
  74.1 0.8 %copy.29 = f32[8,2,72,128]{3,2,1,0:T(8,128)} copy(f32[8,2,72,128]{3,2,1,0:T(8,128)S(1)} %collective-permute-done) | data formatting | bytes 1179648 | tf_op jit(solution)/shard_map/while
  74.9 1.8 %collective-permute-done.3 = f32[1,2,72,128]{3,2,1,0:T(8,128)S(1)} collective-permute-done((f32[1,2,72,128]{3,2,1,0:T(8,128)}, f32[1,2,72,128]{3,2,1,0:T(8,128)S(1)}, u32[]{:S(2)}, u32[]{:S(2)}) %collective-permute-start.3) | collective-permute-done | bytes 73760 | tf_op jit(solution)/shard_map/while/body/ppermute | solution.py:560
  76.7 0.6 total.1
  77.3 0.0 collective-permute-done.6.refs_1_.refs_5_
  77.3 0.0 copy-done
  77.3 0.0 copy-done.1
  77.3 4.7 %last.1 = (bf16[2,2160,128]{2,1,0:T(8,128)(2,1)}, bf16[2,2160,128]{2,1,0:T(8,128)(2,1)}) custom-call(s32[5]{0:T(128)S(1)} %get-tuple-element.458, bf16[2,2160,128]{2,1,0:T(8,128)(2,1)S(1)} %collective-permute-done.6.refs_1_.refs_5_, bf16[9,128,128]{2,1,0:T(8,128)(2,1)} %get-tuple-element.456, f32[2160,128]{1,0:T(8,128)} %get-tuple-element.170.refs_3_, ...), custom_call_target="tpu_custom_call" | custom-call | flops 1000 | bytes 1000 | tf_op jit(solution)/shard_map/last/pallas_call | solution.py:464
  (1 shorter events, 0.0 us)
Async XLA Ops:
  0.7 6.9 %copy-start.7 = (bf16[9,128,128]{2,1,0:T(8,128)(2,1)S(1)}, bf16[9,128,128]{2,1,0:T(8,128)(2,1)}, u32[]{:S(2)}) copy-start(bf16[9,128,128]{2,1,0:T(8,128)(2,1)} %refs_6_.5) | copy-start | bytes 884740
  0.7 7.0 %copy-start.10 = (bf16[9,128,128]{2,1,0:T(8,128)(2,1)S(1)}, bf16[9,128,128]{2,1,0:T(8,128)(2,1)}, u32[]{:S(2)}) copy-start(bf16[9,128,128]{2,1,0:T(8,128)(2,1)} %refs_2_.3) | copy-start | bytes 884740
  0.7 7.0 %copy-start.12 = (s32[2160]{0:T(1024)S(1)}, s32[2160]{0:T(1024)}, u32[]{:S(2)}) copy-start(s32[2160]{0:T(1024)} %refs_1_.3) | copy-start | bytes 25924
  3.8 12.0 %copy-start.9 = (bf16[2160,128]{1,0:T(8,128)(2,1)}, bf16[2160,128]{1,0:T(8,128)(2,1)S(1)}, u32[]{:S(2)}) copy-start(bf16[2160,128]{1,0:T(8,128)(2,1)S(1)} %get-tuple-element.395.refs_5_) | copy-start | bytes 1658884
  3.8 21.1 %copy-start.2 = (bf16[2,2160,128]{2,1,0:T(8,128)(2,1)}, bf16[2,2160,128]{2,1,0:T(8,128)(2,1)S(1)}, u32[]{:S(2)}) copy-start(bf16[2,2160,128]{2,1,0:T(8,128)(2,1)S(1)} %get-tuple-element.393.refs_2_) | copy-start | bytes 3317764
  3.8 21.1 %copy-start.4 = (bf16[2,2160,128]{2,1,0:T(8,128)(2,1)}, bf16[2,2160,128]{2,1,0:T(8,128)(2,1)S(1)}, u32[]{:S(2)}) copy-start(bf16[2,2160,128]{2,1,0:T(8,128)(2,1)S(1)} %get-tuple-element.394.refs_3_) | copy-start | bytes 3317764
  3.8 2.9 %collective-permute-start.5 = (bf16[2,2160,128]{2,1,0:T(8,128)(2,1)S(1)}, bf16[2,2160,128]{2,1,0:T(8,128)(2,1)S(1)}, u32[]{:S(2)}, u32[]{:S(2)}) collective-permute-start(bf16[2,2160,128]{2,1,0:T(8,128)(2,1)S(1)} %get-tuple-element.394.refs_3_), channel_id=1, source_target_pairs={{0,1},{1,0},{2,3},{3,2},{4,5},{5,4},{6,7},{7,6},{8,9},{9,8},{10,11... | collective-permute-start | bytes 3317768 | tf_op jit(solution)/shard_map/ppermute | solution.py:486
  4.3 13.7 %collective-permute-start.4 = (bf16[2,2160,128]{2,1,0:T(8,128)(2,1)S(1)}, bf16[2,2160,128]{2,1,0:T(8,128)(2,1)}, u32[]{:S(2)}, u32[]{:S(2)}) collective-permute-start(bf16[2,2160,128]{2,1,0:T(8,128)(2,1)S(1)} %get-tuple-element.393.refs_2_), channel_id=1, source_target_pairs={{1,2},{3,4},{5,6},{7,8},{9,10},{11,12},{13,14},{2,1},{4,3},{6,5},{... | collective-permute-start | bytes 3317768 | tf_op jit(solution)/shard_map/ppermute | solution.py:486
  6.7 1.0 %copy-start.11 = (bf16[2,2160,128]{2,1,0:T(8,128)(2,1)}, bf16[2,2160,128]{2,1,0:T(8,128)(2,1)S(1)}, u32[]{:S(2)}) copy-start(bf16[2,2160,128]{2,1,0:T(8,128)(2,1)S(1)} %collective-permute-done.5.refs_4_) | copy-start | bytes 3317764
  15.8 18.2 %collective-permute-start.7 = (bf16[2,2160,128]{2,1,0:T(8,128)(2,1)}, bf16[2,2160,128]{2,1,0:T(8,128)(2,1)}, u32[]{:S(2)}, u32[]{:S(2)}) collective-permute-start(bf16[2,2160,128]{2,1,0:T(8,128)(2,1)} %get-tuple-element.390.refs_8_), channel_id=1, source_target_pairs={{0,1},{1,0},{2,3},{3,2},{4,5},{5,4},{6,7},{7,6},{8,9},{9,8},{10,11... | collective-permute-start | bytes 3317768 | tf_op jit(solution)/shard_map/ppermute | solution.py:486
  24.2 53.2 %collective-permute-start.6 = (bf16[2,2160,128]{2,1,0:T(8,128)(2,1)}, bf16[2,2160,128]{2,1,0:T(8,128)(2,1)S(1)}, u32[]{:S(2)}, u32[]{:S(2)}) collective-permute-start(bf16[2,2160,128]{2,1,0:T(8,128)(2,1)} %far.1.refs_7_), channel_id=1, source_target_pairs={{1,2},{3,4},{5,6},{7,8},{9,10},{11,12},{13,14},{2,1},{4,3},{6,5},{... | collective-permute-start | bytes 3317768 | tf_op jit(solution)/shard_map/ppermute | solution.py:486
  34.0 43.3 %copy-start = (bf16[2160,128]{1,0:T(8,128)(2,1)S(1)}, bf16[2160,128]{1,0:T(8,128)(2,1)}, u32[]{:S(2)}) copy-start(bf16[2160,128]{1,0:T(8,128)(2,1)} %get-tuple-element.156.refs_4_) | copy-start | bytes 1658884
  34.0 43.3 %copy-start.1 = (f32[2160,128]{1,0:T(8,128)S(1)}, f32[2160,128]{1,0:T(8,128)}, u32[]{:S(2)}) copy-start(f32[2160,128]{1,0:T(8,128)} %get-tuple-element.175.refs_11_) | copy-start | bytes 3317764
  34.0 20.7 %collective-permute-start = (f32[8,2,72,128]{3,2,1,0:T(8,128)}, f32[8,2,72,128]{3,2,1,0:T(8,128)S(1)}, u32[]{:S(2)}, u32[]{:S(2)}) collective-permute-start(f32[8,2,72,128]{3,2,1,0:T(8,128)} %get-tuple-element.400), channel_id=1, source_target_pairs={{0,1},{1,0},{2,3},{3,2},{4,5},{5,4},{6,7},{7,6},{8,9},{9,8},{10,11... | collective-permute-start | bytes 1769480 | tf_op jit(solution)/shard_map/while/body/ppermute | solution.py:486
  55.9 7.7 %collective-permute-start.1 = (bf16[2,4,72,128]{3,2,1,0:T(8,128)(2,1)S(1)}, bf16[2,4,72,128]{3,2,1,0:T(8,128)(2,1)S(1)}, u32[]{:S(2)}, u32[]{:S(2)}) collective-permute-start(bf16[2,4,72,128]{3,2,1,0:T(8,128)(2,1)S(1)} %get-tuple-element.357), channel_id=1, source_target_pairs={{0,4},{1,5},{2,6},{3,7},{4,0},{5,1},{6,2},{7,3},{8,12},{9,13},{10,... | collective-permute-start | bytes 442376 | tf_op jit(solution)/shard_map/while/body/ppermute | solution.py:560
  57.6 8.1 %copy-start.3 = (bf16[2,2160,128]{2,1,0:T(8,128)(2,1)S(1)}, bf16[2,2160,128]{2,1,0:T(8,128)(2,1)}, u32[]{:S(2)}) copy-start(bf16[2,2160,128]{2,1,0:T(8,128)(2,1)} %get-tuple-element.439.refs_6_.refs_5_) | copy-start | bytes 3317764 | tf_op jit(solution)/shard_map/while
  57.6 8.1 %copy-start.5 = (bf16[2,2160,128]{2,1,0:T(8,128)(2,1)S(1)}, bf16[2,2160,128]{2,1,0:T(8,128)(2,1)}, u32[]{:S(2)}) copy-start(bf16[2,2160,128]{2,1,0:T(8,128)(2,1)} %get-tuple-element.440.refs_7_.refs_6_) | copy-start | bytes 3317764 | tf_op jit(solution)/shard_map/while
  57.6 8.1 %copy-start.6 = (bf16[2,2160,128]{2,1,0:T(8,128)(2,1)S(1)}, bf16[2,2160,128]{2,1,0:T(8,128)(2,1)}, u32[]{:S(2)}) copy-start(bf16[2,2160,128]{2,1,0:T(8,128)(2,1)} %get-tuple-element.435.refs_2_.refs_1_) | copy-start | bytes 3317764 | tf_op jit(solution)/shard_map/while
  57.6 8.1 %copy-start.8 = (bf16[9,128,128]{2,1,0:T(8,128)(2,1)S(1)}, bf16[9,128,128]{2,1,0:T(8,128)(2,1)}, u32[]{:S(2)}) copy-start(bf16[9,128,128]{2,1,0:T(8,128)(2,1)} %get-tuple-element.442.refs_4_) | copy-start | bytes 884740 | tf_op jit(solution)/shard_map/while
  64.2 6.8 %collective-permute-start.2 = (bf16[1,4,72,128]{3,2,1,0:T(8,128)(2,1)S(1)}, bf16[1,4,72,128]{3,2,1,0:T(8,128)(2,1)S(1)}, u32[]{:S(2)}, u32[]{:S(2)}) collective-permute-start(bf16[1,4,72,128]{3,2,1,0:T(8,128)(2,1)S(1)} %get-tuple-element.363), channel_id=1, source_target_pairs={{0,8},{1,9},{2,10},{3,11},{4,12},{5,13},{6,14},{7,15},{8,0},{9,1},... | collective-permute-start | bytes 221192 | tf_op jit(solution)/shard_map/while/body/ppermute | solution.py:560
  72.1 4.6 %collective-permute-start.3 = (f32[1,2,72,128]{3,2,1,0:T(8,128)}, f32[1,2,72,128]{3,2,1,0:T(8,128)S(1)}, u32[]{:S(2)}, u32[]{:S(2)}) collective-permute-start(f32[1,2,72,128]{3,2,1,0:T(8,128)} %get-tuple-element.368), channel_id=1, source_target_pairs={{0,2},{1,3},{2,0},{3,1},{4,6},{5,7},{6,4},{7,5},{8,10},{9,11},{10,... | collective-permute-start | bytes 221192 | tf_op jit(solution)/shard_map/while/body/ppermute | solution.py:560
